TPU v7x, 32 devices: a whole 2x2x4 slice. The times are simulated.
32 devices in a mesh: seq: 32 (over z, y, x, core).
Axes of the slice: x: 2, y: 2, z: 4, core: 2. Of those that a mesh axis runs over, the one named last changes fastest.
Arguments:
- layer_input: float32 [4096, 1024], P('seq'), may hold values from -6 to 6
- out_grad: float32 [4096, 1024], P('seq'), may hold values from -6 to 6
- doc_ids: int32 [4096], replicated, may hold values from 0 to 23, never falling along the last dimension, each value on 1 to 2176 neighbouring positions
- norm1_gain: bfloat16 [1024], P('seq'), may hold values from 0.5 to 1.5
- in_weight: bfloat16 [1024, 3352], P('seq'), may hold values from -0.1875 to 0.1875
- conv_weight: float32 [4, 1792], replicated, may hold values from -3 to 3
- conv_bias: float32 [1792], replicated, may hold values from -3 to 3
- dt_bias: float32 [24], replicated, may hold values from -4.5 to -1.5
- decay_log: float32 [24], replicated, may hold values from -7 to -1
- skip_gain: float32 [24], replicated, may hold values from 0.5 to 1.5
- mixer_out: bfloat16 [1536, 1024], P(None, 'seq'), may hold values from -0.15625 to 0.15625
- query_weight: bfloat16 [1024, 512], P('seq'), may hold values from -0.1875 to 0.1875
- keyvalue_weight: bfloat16 [1024, 256], P('seq'), may hold values from -0.1875 to 0.1875
- attn_out: bfloat16 [512, 1024], P(None, 'seq'), may hold values from -2 to 2
- norm2_gain: bfloat16 [1024], P('seq'), may hold values from 0.5 to 1.5
- gate_up: bfloat16 [1024, 4096], P('seq'), may hold values from -0.1875 to 0.1875
- down_weight: bfloat16 [2048, 1024], P(None, 'seq'), may hold values from -0.125 to 0.125
Outputs:
- layer_output: float32 [4096, 1024], P('seq')
- input_grad: float32 [4096, 1024], P('seq')
- norm1_gain_grad: float32 [1024], P('seq')
- in_weight_grad: float32 [1024, 3352], P('seq')
- conv_weight_grad: float32 [4, 1792], replicated
- conv_bias_grad: float32 [1792], replicated
- dt_bias_grad: float32 [24], replicated
- decay_log_grad: float32 [24], replicated
- skip_gain_grad: float32 [24], replicated
- mixer_out_grad: float32 [1536, 1024], P(None, 'seq')
- query_weight_grad: float32 [1024, 512], P('seq')
- keyval_weight_grad: float32 [1024, 256], P('seq')
- attn_out_grad: float32 [512, 1024], P(None, 'seq')
- norm2_gain_grad: float32 [1024], P('seq')
- gate_up_grad: float32 [1024, 4096], P('seq')
- down_weight_grad: float32 [2048, 1024], P(None, 'seq')
Inputs may be any that keep to these rules, and one draw needn't show every extreme that they name: doc_ids never decreases along the sequence; each document is a run of 1 to 2176 positions, and one has exactly 2176.
All inputs are finite; a program needn't handle non-finite values.
Results may differ from a plain program's by a relative error of at most 0.013.
Values may be sent and summed in bfloat16 or wider, within the bound.
No kernel may reach another device: no remote copies, remote signals or barrier semaphores. Data moves between devices by JAX's collectives and lax.ppermute only.
A program may use at most 320 MiB of HBM per device.

v0:
```python
from functools import partial
import math

import jax
import jax.numpy as jnp
from jax import lax
from jax.sharding import PartitionSpec as P

FF = 2048
HM = 24
HP = 64
NS = 128
KC = 4
QUERY_HEADS = 8
KEYVALUE_HEADS = 2
HEAD_SIZE = 64
SPAN = 128
DSSM = 1536
CONV_CH = 1792


EPS = 1e-05
HIGH = lax.Precision.HIGHEST
NEG = -1e30


def passed_along(block, axis, distance):
    devices = range(lax.axis_size(axis))
    route = [(i - distance, i) for i in devices if i - distance in devices]
    return lax.ppermute(block, axis, route)


def prefix(shard, axis, combine, identity, reverse):
    size, here = (lax.axis_size(axis), lax.axis_index(axis))
    everything = jax.tree.map(
        lambda part, kind: lax.all_gather(part.astype(kind), axis),
        shard,
        (jnp.bfloat16, jnp.bfloat16),
    )
    start = jax.tree.map(
        lambda part, zero: jnp.broadcast_to(jnp.asarray(zero, part.dtype), part.shape),
        shard,
        identity,
    )

    def hop(k, before):
        at = size - 1 - k if reverse else k
        reached = at > here if reverse else at < here
        new = combine(
            before, jax.tree.map(lambda part, own: part[at].astype(own.dtype), everything, shard)
        )
        return jax.tree.map(lambda a, b: jnp.where(reached, a, b), new, before)

    return lax.fori_loop(0, size, hop, start)


def matmul(left, right):
    return jnp.dot(left, right, preferred_element_type=jnp.float32)


def matmul_tn(left, right):
    return lax.dot_general(
        left, right, (((0,), (0,)), ((), ())), preferred_element_type=jnp.float32
    )


def matmul_nt(left, right):
    return lax.dot_general(
        left, right, (((1,), (1,)), ((), ())), preferred_element_type=jnp.float32
    )


def rms_scale(values):
    return lax.rsqrt(jnp.mean(values * values, axis=-1, keepdims=True) + EPS)


def rms_back(values, inverse, gain_row, upstream):
    scaled = upstream * gain_row
    return inverse * (
        scaled - values * inverse * inverse * jnp.mean(scaled * values, axis=-1, keepdims=True)
    )


def silu_slope(values):
    logistic = jax.nn.sigmoid(values)
    return logistic * (1.0 + values * (1.0 - logistic))


def conv_apply(seg_window, conv_ext, conv_weight, conv_bias):
    out_rows = conv_ext.shape[0] - (KC - 1)
    summed = jnp.broadcast_to(conv_bias[None, :], (out_rows, conv_ext.shape[1]))
    for offset in range(KC):
        same_doc = seg_window[offset : offset + out_rows] == seg_window[KC - 1 :]
        summed = summed + conv_weight[offset][None, :] * jnp.where(
            same_doc[:, None], conv_ext[offset : offset + out_rows], 0.0
        )
    return jax.nn.silu(summed)


def ssm_core(seg_here, seg_before, conv_act, dt_raw, dt_bias, decay_log, skip_gain):
    row_count = conv_act.shape[0]
    blocks_count = row_count // SPAN
    ssm_x = conv_act[:, : HM * HP].reshape(blocks_count, SPAN, HM, HP)
    ssm_b = conv_act[:, HM * HP : HM * HP + NS].reshape(blocks_count, SPAN, NS)
    ssm_c = conv_act[:, HM * HP + NS :].reshape(blocks_count, SPAN, NS)
    step_size = jax.nn.softplus(dt_raw + dt_bias[None, :])
    log_decay = -jnp.exp(decay_log)[None, :] * step_size
    step_heads = step_size.reshape(blocks_count, SPAN, HM).transpose(0, 2, 1)
    cumulative = jnp.cumsum(log_decay.reshape(blocks_count, SPAN, HM).transpose(0, 2, 1), axis=2)
    seg_blocks = seg_here.reshape(blocks_count, SPAN)
    seg_prior = jnp.concatenate([jnp.reshape(seg_before, (1,)), seg_blocks[:-1, -1]])
    seg_last = seg_blocks[:, -1]
    lower = jnp.arange(SPAN)[:, None] >= jnp.arange(SPAN)[None, :]
    visible = (lower[None] & (seg_blocks[:, :, None] == seg_blocks[:, None, :]))[:, None]
    gaps = cumulative[:, :, :, None] - cumulative[:, :, None, :]
    mixing = jnp.where(visible, jnp.exp(jnp.where(visible, gaps, 0.0)), 0.0)
    inner = jnp.einsum("ktn,ksn->kts", ssm_c, ssm_b, precision=HIGH)
    weighted = mixing * inner[:, None] * step_heads[:, :, None, :]
    intra = jnp.einsum("khts,kshp->kthp", weighted, ssm_x, precision=HIGH)
    to_end = (
        jnp.where(
            (seg_blocks == seg_last[:, None])[:, None, :],
            jnp.exp(cumulative[:, :, -1:] - cumulative),
            0.0,
        )
        * step_heads
    )
    block_states = jnp.einsum("khs,kshp,ksn->khpn", to_end, ssm_x, ssm_b, precision=HIGH)
    from_start = jnp.where((seg_blocks == seg_prior[:, None])[:, None, :], jnp.exp(cumulative), 0.0)
    block_decay = from_start[:, :, -1]

    def advance(carried, inputs):
        state_now, product = carried
        decay_now, fresh = inputs
        return (
            (decay_now[:, None, None] * state_now + fresh, product * decay_now),
            (state_now, product),
        )

    initial_carry = (jnp.zeros((HM, HP, NS), jnp.float32), jnp.ones((HM,), jnp.float32))
    (final_state, unused), (entering, products) = lax.scan(
        advance, initial_carry, (block_decay, block_states)
    )
    carried_in = jnp.einsum("kht,ktn,khpn->kthp", from_start, ssm_c, entering, precision=HIGH)
    local_out = (intra + carried_in + skip_gain[None, None, :, None] * ssm_x).reshape(
        row_count, HM, HP
    )
    reach = (from_start * products[:, :, None]).transpose(1, 0, 2).reshape(HM, row_count)
    return (local_out, final_state, reach, ssm_c.reshape(row_count, NS))


def join_forward(earlier, later):
    decay_low, state_low = earlier
    decay_high, state_high = later
    return (decay_low * decay_high, decay_high[:, None, None] * state_low + state_high)


def join_backward(earlier, later):
    decay_high, grad_high = earlier
    decay_low, grad_lower = later
    return (decay_low * decay_high, grad_lower + decay_low[:, None, None] * grad_high)


def over_keys(update, initial_carry, key_rows_all, row_limit, query_rows, doc_span):
    count_all = key_rows_all.shape[0]
    block_size = math.gcd(count_all, 512)
    blocks = count_all // block_size
    visits = min(blocks, (doc_span + query_rows - 1) // block_size + 2)
    lowest = (row_limit - query_rows - doc_span + 1) // block_size
    begin = jnp.clip(lowest, 0, blocks - visits)

    def visit(number, current_block):
        offset = (begin + number) * block_size
        return update(
            current_block, lax.dynamic_slice_in_dim(key_rows_all, offset, block_size, 0), offset
        )

    return lax.fori_loop(0, visits, visit, initial_carry)


def block_scores(query_quadruple, positions, seg_rows, doc_ids, block_forward_pass, key_start):
    rows_per_block = block_forward_pass.shape[0]
    key_columns = KEYVALUE_HEADS * HEAD_SIZE
    key_row_block = block_forward_pass[:, :key_columns].reshape(
        rows_per_block, KEYVALUE_HEADS, HEAD_SIZE
    )
    value_row_block = block_forward_pass[:, key_columns:].reshape(
        rows_per_block, KEYVALUE_HEADS, HEAD_SIZE
    )
    key_pos = key_start + jnp.arange(rows_per_block, dtype=jnp.int32)
    key_seg = lax.dynamic_slice_in_dim(doc_ids, key_start, rows_per_block)
    visible = (key_pos[None, :] <= positions[:, None]) & (key_seg[None, :] == seg_rows[:, None])
    attention_scores = jnp.einsum(
        "uoiy,woy->oiuw", query_quadruple, key_row_block, preferred_element_type=jnp.float32
    ) * HEAD_SIZE ** (-0.5)
    return (key_row_block, value_row_block, visible[None, None], attention_scores)


def stats_step(
    query_quadruple, positions, seg_rows, doc_ids, denominator, block_forward_pass, key_start
):
    key_row_block, value_row_block, visible, attention_scores = block_scores(
        query_quadruple, positions, seg_rows, doc_ids, block_forward_pass, key_start
    )
    return denominator + jnp.sum(jnp.exp(jnp.where(visible, attention_scores, NEG)), axis=3)


def values_step(
    query_quadruple,
    positions,
    seg_rows,
    doc_ids,
    log_total,
    current_block,
    block_forward_pass,
    key_start,
):
    key_row_block, value_row_block, visible, attention_scores = block_scores(
        query_quadruple, positions, seg_rows, doc_ids, block_forward_pass, key_start
    )
    attention_weights_soft = jnp.exp(
        jnp.where(visible, attention_scores - log_total[..., None], NEG)
    ).astype(jnp.bfloat16)
    return current_block + jnp.einsum(
        "zilr,rzq->lziq",
        attention_weights_soft,
        value_row_block,
        preferred_element_type=jnp.float32,
    )


def back_step(
    query_quadruple,
    positions,
    seg_rows,
    doc_ids,
    log_total,
    gradient_quadruple,
    row_delta,
    current_block,
    block_forward_pass,
    key_start,
):
    query_accumulator, keyvalue_accumulator = current_block
    key_row_block, value_row_block, visible, attention_scores = block_scores(
        query_quadruple, positions, seg_rows, doc_ids, block_forward_pass, key_start
    )
    attention_weights_soft = jnp.exp(
        jnp.where(visible, attention_scores - log_total[..., None], NEG)
    )
    probability_gradient = jnp.einsum(
        "uoiy,woy->oiuw", gradient_quadruple, value_row_block, preferred_element_type=jnp.float32
    )
    score_gradient = (
        attention_weights_soft * (probability_gradient - row_delta[..., None])
    ).astype(jnp.bfloat16)
    query_accumulator = query_accumulator + jnp.einsum(
        "zilr,rzq->lziq", score_gradient, key_row_block, preferred_element_type=jnp.float32
    )
    key_portion = jnp.einsum(
        "luzn,zlup->nlp", score_gradient, query_quadruple, preferred_element_type=jnp.float32
    ) * HEAD_SIZE ** (-0.5)
    value_portion = jnp.einsum(
        "luzn,zlup->nlp",
        attention_weights_soft.astype(jnp.bfloat16),
        gradient_quadruple,
        preferred_element_type=jnp.float32,
    )
    rows_per_block = block_forward_pass.shape[0]
    block_gradient_out = jnp.concatenate(
        [
            key_portion.reshape(rows_per_block, KEYVALUE_HEADS * HEAD_SIZE),
            value_portion.reshape(rows_per_block, KEYVALUE_HEADS * HEAD_SIZE),
        ],
        axis=1,
    )
    old_rows = lax.dynamic_slice_in_dim(keyvalue_accumulator, key_start, rows_per_block, 0)
    keyvalue_accumulator = lax.dynamic_update_slice_in_dim(
        keyvalue_accumulator, old_rows + block_gradient_out, key_start, 0
    )
    return (query_accumulator, keyvalue_accumulator)


def local(
    layer_input,
    out_grad,
    doc_ids,
    norm1_gain,
    in_weight,
    conv_weight,
    conv_bias,
    dt_bias,
    decay_log,
    skip_gain,
    mixer_out,
    query_weight,
    keyvalue_weight,
    attn_out,
    norm2_gain,
    gate_up,
    down_weight,
):
    local_row_count = layer_input.shape[0]
    devices = lax.axis_size("seq")
    sequence_total = local_row_count * devices
    doc_span = sequence_total // 2 + local_row_count
    first_row = lax.axis_index("seq") * local_row_count
    query_group_width = QUERY_HEADS // KEYVALUE_HEADS
    gathered = (
        lax.all_gather(norm1_gain, "seq", axis=0, tiled=True),
        lax.all_gather(in_weight, "seq", axis=0, tiled=True),
        lax.all_gather(mixer_out, "seq", axis=1, tiled=True),
        lax.all_gather(query_weight, "seq", axis=0, tiled=True),
        lax.all_gather(keyvalue_weight, "seq", axis=0, tiled=True),
        lax.all_gather(attn_out, "seq", axis=1, tiled=True),
        lax.all_gather(norm2_gain, "seq", axis=0, tiled=True),
        lax.all_gather(gate_up, "seq", axis=0, tiled=True),
        lax.all_gather(down_weight, "seq", axis=1, tiled=True),
    )
    gain_first = gathered[0].astype(jnp.float32)
    inner_full = gathered[1]
    mixer_full = gathered[2]
    query_full = gathered[3]
    keyval_full = gathered[4]
    output_full = gathered[5]
    gain_second = gathered[6].astype(jnp.float32)
    gateup_full = gathered[7]
    downward_full = gathered[8]
    seg_here = lax.dynamic_slice_in_dim(doc_ids, first_row, local_row_count)
    seg_padded = jnp.concatenate([jnp.full((KC - 1,), -1, jnp.int32), doc_ids])
    seg_window = lax.dynamic_slice_in_dim(seg_padded, first_row, local_row_count + KC - 1)
    seg_before = seg_window[KC - 2]
    scale_one = rms_scale(layer_input)
    normed_one = (layer_input * scale_one * gain_first).astype(jnp.bfloat16)
    projected = matmul(normed_one, inner_full)
    gate_mix = projected[:, :DSSM]
    conv_in = projected[:, DSSM : DSSM + CONV_CH]
    dt_raw = projected[:, DSSM + CONV_CH :]
    edge_rows = passed_along(conv_in[local_row_count - (KC - 1) :], "seq", 1)
    conv_ext = jnp.concatenate([edge_rows, conv_in], axis=0)
    conv_act, conv_pull = jax.vjp(partial(conv_apply, seg_window), conv_ext, conv_weight, conv_bias)
    ssm_parts, ssm_pull = jax.vjp(
        partial(ssm_core, seg_here, seg_before), conv_act, dt_raw, dt_bias, decay_log, skip_gain
    )
    local_out, dev_state, reach, c_here = ssm_parts
    dev_decay = reach[:, -1]
    scanned = prefix(
        (dev_decay, dev_state),
        "seq",
        join_forward,
        (jnp.ones_like(dev_decay), jnp.zeros_like(dev_state)),
        False,
    )
    state_in = scanned[1]
    cross_base = jnp.einsum("tn,hpn->thp", c_here, state_in, precision=HIGH)
    ssm_out = (local_out + cross_base * reach.T[:, :, None]).reshape(local_row_count, DSSM)
    gated = (ssm_out * jax.nn.silu(gate_mix)).astype(jnp.bfloat16)
    mixer_part = matmul(gated, mixer_full)
    query_reduced = matmul(normed_one, query_full).astype(jnp.bfloat16)
    keyval_low = matmul(normed_one, keyval_full).astype(jnp.bfloat16)
    query_quadruple = query_reduced.reshape(
        local_row_count, KEYVALUE_HEADS, query_group_width, HEAD_SIZE
    )
    positions = first_row + jnp.arange(local_row_count, dtype=jnp.int32)
    row_limit = first_row + local_row_count
    statistics_initial = jnp.zeros(
        (KEYVALUE_HEADS, query_group_width, local_row_count), jnp.float32
    )
    middle_initial = jnp.zeros(
        (local_row_count, KEYVALUE_HEADS, query_group_width, HEAD_SIZE), jnp.float32
    )
    stats_update = partial(stats_step, query_quadruple, positions, seg_here, doc_ids)
    keyval_all = lax.all_gather(keyval_low, "seq", axis=0, tiled=True)
    denominator = over_keys(
        stats_update, statistics_initial, keyval_all, row_limit, local_row_count, doc_span
    )
    log_total = jnp.log(denominator)
    attention_middle = over_keys(
        partial(values_step, query_quadruple, positions, seg_here, doc_ids, log_total),
        middle_initial,
        keyval_all,
        row_limit,
        local_row_count,
        doc_span,
    )
    attn_low = attention_middle.reshape(local_row_count, QUERY_HEADS * HEAD_SIZE).astype(
        jnp.bfloat16
    )
    attn_part = matmul(attn_low, output_full)
    resid = layer_input + mixer_part + attn_part
    scale_two = rms_scale(resid)
    normed_two = (resid * scale_two * gain_second).astype(jnp.bfloat16)
    gateup = matmul(normed_two, gateup_full)
    gate_part = gateup[:, :FF]
    up_part = gateup[:, FF:]
    act_low = (jax.nn.silu(gate_part) * up_part).astype(jnp.bfloat16)
    layer_output = resid + matmul(act_low, downward_full)
    grad_low = out_grad.astype(jnp.bfloat16)
    down_grad = matmul_tn(act_low, grad_low)
    act_grad = matmul_nt(grad_low, downward_full)
    gateup_grad_low = jnp.concatenate(
        [act_grad * up_part * silu_slope(gate_part), act_grad * jax.nn.silu(gate_part)], axis=1
    ).astype(jnp.bfloat16)
    gateup_grad = matmul_tn(normed_two, gateup_grad_low)
    normed_two_grad = matmul_nt(gateup_grad_low, gateup_full)
    gain2_grad = jnp.sum(normed_two_grad * resid * scale_two, axis=0)
    resid_grad = out_grad + rms_back(resid, scale_two, gain_second, normed_two_grad)
    resid_low = resid_grad.astype(jnp.bfloat16)
    mixer_grad = matmul_tn(gated, resid_low)
    output_grad_w = matmul_tn(attn_low, resid_low)
    gated_grad = matmul_nt(resid_low, mixer_full)
    attention_gradient = matmul_nt(resid_low, output_full)
    gradient_quadruple = attention_gradient.astype(jnp.bfloat16).reshape(
        local_row_count, KEYVALUE_HEADS, query_group_width, HEAD_SIZE
    )
    row_delta = jnp.sum(
        attention_gradient.reshape(local_row_count, KEYVALUE_HEADS, query_group_width, HEAD_SIZE)
        * attention_middle,
        axis=3,
    ).transpose(1, 2, 0)
    back_init = (
        jnp.zeros((local_row_count, KEYVALUE_HEADS, query_group_width, HEAD_SIZE), jnp.float32),
        jnp.zeros((sequence_total, 2 * KEYVALUE_HEADS * HEAD_SIZE), jnp.float32),
    )
    back_update = partial(
        back_step,
        query_quadruple,
        positions,
        seg_here,
        doc_ids,
        log_total,
        gradient_quadruple,
        row_delta,
    )
    query_accumulator, keyvalue_accumulator = over_keys(
        back_update, back_init, keyval_all, row_limit, local_row_count, doc_span
    )
    keyval_here = lax.psum_scatter(keyvalue_accumulator, "seq", scatter_dimension=0, tiled=True)
    query_grad_low = (
        query_accumulator.reshape(local_row_count, QUERY_HEADS * HEAD_SIZE) * HEAD_SIZE ** (-0.5)
    ).astype(jnp.bfloat16)
    keyval_grad_low = keyval_here.astype(jnp.bfloat16)
    query_grad_w = matmul_tn(normed_one, query_grad_low)
    keyval_grad_w = matmul_tn(normed_one, keyval_grad_low)
    ssm_grad = gated_grad * jax.nn.silu(gate_mix)
    gate_mix_grad = gated_grad * ssm_out * silu_slope(gate_mix)
    ssm_grad_three = ssm_grad.reshape(local_row_count, HM, HP)
    weighted_grad = ssm_grad_three * reach.T[:, :, None]
    state_in_grad = jnp.einsum("thp,tn->hpn", weighted_grad, c_here, precision=HIGH)
    c_grad = jnp.einsum("thp,hpn->tn", weighted_grad, state_in, precision=HIGH)
    reach_grad = jnp.einsum("thp,thp->ht", ssm_grad_three, cross_base, precision=HIGH)
    back_scan = prefix(
        (dev_decay, state_in_grad),
        "seq",
        join_backward,
        (jnp.ones_like(dev_decay), jnp.zeros_like(dev_state)),
        True,
    )
    state_out_grad = back_scan[1]
    decay_grad = jnp.sum(state_out_grad * state_in, axis=(1, 2))
    reach_grad = jnp.concatenate(
        [reach_grad[:, :-1], reach_grad[:, -1:] + decay_grad[:, None]], axis=1
    )
    act_grad_ssm, dt_raw_grad, dt_bias_grad, decay_log_grad, skip_grad = ssm_pull(
        (ssm_grad_three, state_out_grad, reach_grad, c_grad)
    )
    ext_grad, conv_weight_grad, conv_bias_grad = conv_pull(act_grad_ssm)
    edge_back = passed_along(ext_grad[: KC - 1], "seq", -1)
    conv_in_grad = ext_grad[KC - 1 :] + jnp.concatenate(
        [jnp.zeros((local_row_count - (KC - 1), CONV_CH), jnp.float32), edge_back], axis=0
    )
    proj_grad_low = jnp.concatenate([gate_mix_grad, conv_in_grad, dt_raw_grad], axis=1).astype(
        jnp.bfloat16
    )
    inner_grad = matmul_tn(normed_one, proj_grad_low)
    normed_one_grad = (
        matmul_nt(proj_grad_low, inner_full)
        + matmul_nt(query_grad_low, query_full)
        + matmul_nt(keyval_grad_low, keyval_full)
    )
    gain1_grad = jnp.sum(normed_one_grad * layer_input * scale_one, axis=0)
    input_grad = resid_grad + rms_back(layer_input, scale_one, gain_first, normed_one_grad)
    shares = (
        lax.psum_scatter(gain1_grad, "seq", scatter_dimension=0, tiled=True),
        lax.psum_scatter(inner_grad, "seq", scatter_dimension=0, tiled=True),
        lax.psum_scatter(mixer_grad, "seq", scatter_dimension=1, tiled=True),
        lax.psum_scatter(query_grad_w, "seq", scatter_dimension=0, tiled=True),
        lax.psum_scatter(keyval_grad_w, "seq", scatter_dimension=0, tiled=True),
        lax.psum_scatter(output_grad_w, "seq", scatter_dimension=1, tiled=True),
        lax.psum_scatter(gain2_grad, "seq", scatter_dimension=0, tiled=True),
        lax.psum_scatter(gateup_grad, "seq", scatter_dimension=0, tiled=True),
        lax.psum_scatter(down_grad, "seq", scatter_dimension=1, tiled=True),
    )
    small = lax.psum(
        (conv_weight_grad, conv_bias_grad, dt_bias_grad, decay_log_grad, skip_grad), "seq"
    )
    return (
        layer_output,
        input_grad,
        shares[0],
        shares[1],
        small[0],
        small[1],
        small[2],
        small[3],
        small[4],
        shares[2],
        shares[3],
        shares[4],
        shares[5],
        shares[6],
        shares[7],
        shares[8],
    )


def solution(mesh):
    placed = (
        P("seq", None),
        P("seq", None),
        P(),
        P("seq"),
        P("seq", None),
        P(),
        P(),
        P(),
        P(),
        P(),
        P(None, "seq"),
        P("seq", None),
        P("seq", None),
        P(None, "seq"),
        P("seq"),
        P("seq", None),
        P(None, "seq"),
    )
    return jax.shard_map(
        local,
        mesh=mesh,
        in_specs=placed,
        out_specs=(
            P("seq", None),
            P("seq", None),
            P("seq"),
            P("seq", None),
            P(),
            P(),
            P(),
            P(),
            P(),
            P(None, "seq"),
            P("seq", None),
            P("seq", None),
            P(None, "seq"),
            P("seq"),
            P("seq", None),
            P(None, "seq"),
        ),
        check_vma=False,
    )
```

profile of v0, /device:TPU:0, one launch (start us, length us, event | category | flops | bytes accessed | tf_op | source)
XLA Modules:
  0.0 1909.4 jit_solution(7077545745463308693)
XLA Ops:
  9.6 42.5 %all-reduce.15 = bf16[1024]{0:T(1024)(128)(2,1)S(1)} all-reduce(bf16[1024]{0:T(1024)(128)(2,1)S(1)} %dynamic-update-slice), channel_id=1, replica_groups=mesh['seq'=32] {'seq'}, use_global_device_ids=true, to_apply=%add.15 | all-reduce | flops 1024 | bytes 4096
  54.5 43.8 %all_gather.51 = bf16[1024,256]{1,0:T(8,128)(2,1)S(1)} all-gather(bf16[32,256]{1,0:T(8,128)(2,1)} %param.39), channel_id=1, replica_groups=mesh['seq'=32] {'seq'}, dimensions={0}, use_global_device_ids=true | all-gather | bytes 540672 | tf_op jit(solution)/shard_map/all_gather | solution.py:314
  105.0 5.9 fusion.176
  113.8 2.2 collective-permute-start
  120.5 7.0 fusion.74
  135.3 8.6 all-gather.19.cloned.1.call-done
  143.9 2.2 convolution_convert_fusion.1
  147.1 55.4 %all-gather.17.cloned.1.call-done = bf16[4096,256]{1,0:T(8,128)(2,1)} async-done(((bf16[128,256]{1,0:T(8,128)(2,1)}), bf16[4096,256]{1,0:T(8,128)(2,1)}) %all-gather.17.cloned.1.call-update) | async-done | bytes 2097168 | tf_op jit(solution)/shard_map/all_gather | solution.py:373
  202.5 4.1 copy.126
  206.6 15.6 while.90
  222.9 21.5 %while.91 = (s32[]{:T(128)}, f32[128,2,4,64]{0,3,2,1:T(8,128)S(1)}, s32[]{:T(128)}, bf16[4096,256]{0,1:T(8,128)(2,1)}, s32[4096]{0:T(1024)}, /*index=5*/s32[128]...) while((s32[]{:T(128)}, f32[128,2,4,64]{0,3,2,1:T(8,128)S(1)}, ...), condition=%wide.region_8.9_spmd.clone, body=%wide.region_7.8_spmd.clone.sunk | while | flops 136643200 | bytes 1588977 | solution.py:178
  245.0 42.5 %all-reduce.21 = (bf16[768]{0:T(1024)(128)(2,1)S(1)}, bf16[1024]{0:T(1024)(128)(2,1)S(1)}) all-reduce(bf16[768]{0:T(1024)(128)(2,1)S(1)} %dynamic-update-slice.1, bf16[1024]{0:T(1024)(128)(2,1)S(1)} %copy-done.97), channel_id=2, replica_groups=mesh['seq'=32] {'seq'}, use_global_device_ids=true, to_apply=%add.16 | all-reduce | flops 1792 | bytes 7168
  287.6 2.5 convolution_bitcast_fusion.3
  291.2 8.9 all-gather.27.cloned.1.call-done
  300.2 39.8 %while.89 = (s32[]{:T(128)}, f32[24,64,128]{2,1,0:T(8,128)S(1)}, s32[]{:T(128)}, bf16[32,24]{1,0:T(8,128)(2,1)S(1)}, bf16[32,24,64,128]{3,2,1,0:T(8,128)(2,1)}, /*index=5*/s32[]{:T(128)}, s32[]{:T(128)}) while((s32[]{:T(128)}, f32[24,64,128]{2,1,0:T(8,128)S(1)}, s32[]{:T(128)}, bf16[32,24]{1,0:T(8,128)(2,1)S(1)}, ...), condition=%wide.region_3.4_spmd.clone, body=%wide.region_2.3_spmd.clone.sunk | while | flops 983068 | bytes 1966433 | solution.py:54
  341.8 5.2 fusion.56
  348.1 12.8 all-gather.15.cloned.1.call-done
  360.9 3.1 convolution_add_fusion.4
  364.0 52.0 %all-gather.21.cloned.1.call-done = bf16[512,1024]{0,1:T(8,128)(2,1)} async-done(((bf16[512,32]{0,1:T(8,128)(2,1)}), bf16[512,1024]{0,1:T(8,128)(2,1)}) %all-gather.21.cloned.1.call-update) | async-done | bytes 1048592 | tf_op jit(solution)/shard_map/all_gather | solution.py:315
  417.8 77.1 %all-gather.23.cloned.1.call-done = bf16[1024,4096]{1,0:T(8,128)(2,1)} async-done(((bf16[32,4096]{1,0:T(8,128)(2,1)}), bf16[1024,4096]{1,0:T(8,128)(2,1)}) %all-gather.23.cloned.1.call-update) | async-done | bytes 8388624 | tf_op jit(solution)/shard_map/all_gather | solution.py:317
  494.9 4.7 fusion.165
  499.7 58.5 %all-gather.25.cloned.1.call-done = bf16[2048,1024]{0,1:T(8,128)(2,1)} async-done(((bf16[2048,32]{0,1:T(8,128)(2,1)}), bf16[2048,1024]{0,1:T(8,128)(2,1)}) %all-gather.25.cloned.1.call-update) | async-done | bytes 4194320 | tf_op jit(solution)/shard_map/all_gather | solution.py:318
  558.2 4.3 multiply_convert_fusion.1
  563.0 3.5 multiply_reduce_fusion.12
  569.1 2.4 broadcast_in_dim.297
  571.6 61.9 %while.93 = (s32[]{:T(128)}, f32[128,2,4,64]{0,3,2,1:T(8,128)}, f32[4096,256]{0,1:T(8,128)}, s32[]{:T(128)}, bf16[4096,256]{0,1:T(8,128)(2,1)}, /*index=5*/s32[4...) while((s32[]{:T(128)}, f32[128,2,4,64]{0,3,2,1:T(8,128)}, ...), condition=%wide.region_23.24_spmd.clone, body=%wide.region_22.23_spmd.clone.sunk | while | flops 339870336 | bytes 13668137 | solution.py:178
  635.0 4.9 multiply_reduce_fusion.9
  645.3 3.6 fusion.177
  649.0 126.3 %reduce-scatter.9.cloned.1.call-done = f32[128,256]{0,1:T(8,128)} async-done(((f32[4096,256]{0,1:T(8,128)}), f32[128,256]{0,1:T(8,128)}) %reduce-scatter.9.cloned.1.call-update) | async-done | bytes 131088 | tf_op jit(solution)/shard_map/reduce_scatter | solution.py:438
  775.3 2.2 fusion.133
  777.6 4.6 fusion.110
  783.6 8.2 fusion.99
  793.0 4.3 fusion.76
  803.5 66.2 %all-gather.29.cloned.1.call-done = bf16[768,64,128]{2,1,0:T(8,128)(2,1)} async-done(((bf16[24,64,128]{2,1,0:T(8,128)(2,1)}), bf16[768,64,128]{2,1,0:T(8,128)(2,1)}) %all-gather.29.cloned.1.call-update) | async-done | bytes 12582928 | tf_op jit(solution)/shard_map/all_gather | solution.py:36
  869.7 60.5 %while.92 = (s32[]{:T(128)}, f32[24,64,128]{2,1,0:T(8,128)S(1)}, s32[]{:T(128)}, bf16[32,24,64,128]{3,2,1,0:T(8,128)(2,1)}, bf16[32,24]{1,0:T(8,128)(2,1)}, /*index=5*/s32[]{:T(128)}, s32[]{:T(128)}, s32[]{:T(128)}, s32[]{:T(128)}) while((s32[]{:T(128)}, f32[24,64,128]{2,1,0:T(8,128)S(1)}, s32[]{:T(128)}, ...), condition=%wide.region_13.14_spmd.clone, body=%wide.region_12.13_spmd.clone.sunk | while | flops 983072 | bytes 1966495 | solution.py:54
  930.6 2.9 multiply_reduce_fusion.8
  938.2 3.3 fusion.44
  941.6 2.8 multiply_reduce_fusion.4
  956.5 8.1 fusion.108
  965.6 4.6 convolution_add_fusion.3
  970.7 5.5 fusion.109
  977.0 42.8 %all-reduce.20 = (f32[1024]{0:T(1024)S(1)}, f32[4,1792]{1,0:T(4,128)}, f32[1792]{0:T(1024)}, f32[24]{0:T(128)}, f32[24]{0:T(128)}, /*index=5*/f32[24]{0:T(128)}, f32[1024]{0:T(1024)S(1)}) all-reduce(f32[1024]{0:T(1024)S(1)} %get-tuple-element.1064, f32[4,1792]{1,0:T(4,128)S(1)} %pad_add_fusion.1, ...), channel_id=6, replica_groups=mesh['seq'=32] {'seq'}, use_global_device_ids=true, to_apply=%region_27.28.clone | all-reduce | flops 11080 | bytes 88640
  1022.0 124.2 %reduce-scatter.19.cloned.1.call-done = f32[512,32]{0,1:T(8,128)} async-done(((f32[512,1024]{0,1:T(8,128)}), f32[512,32]{0,1:T(8,128)}) %reduce-scatter.19.cloned.1.call-update) | async-done | bytes 65552 | tf_op jit(solution)/shard_map/reduce_scatter | solution.py:489
  1146.1 117.1 %reduce-scatter.13.cloned.1.call-done = f32[1536,32]{0,1:T(8,128)} async-done(((f32[1536,1024]{0,1:T(8,128)}), f32[1536,32]{0,1:T(8,128)}) %reduce-scatter.13.cloned.1.call-update) | async-done | bytes 196624 | tf_op jit(solution)/shard_map/reduce_scatter | solution.py:486
  1263.2 138.3 %reduce-scatter.17.cloned.1.call-done = f32[32,256]{1,0:T(8,128)} async-done(((f32[1024,256]{1,0:T(8,128)}), f32[32,256]{1,0:T(8,128)}) %reduce-scatter.17.cloned.1.call-update) | async-done | bytes 32784 | tf_op jit(solution)/shard_map/reduce_scatter | solution.py:488
  1401.6 148.6 %reduce-scatter.23.cloned.1.call-done = f32[2048,32]{0,1:T(8,128)} async-done(((f32[2048,1024]{0,1:T(8,128)}), f32[2048,32]{0,1:T(8,128)}) %reduce-scatter.23.cloned.1.call-update) | async-done | bytes 262160 | tf_op jit(solution)/shard_map/reduce_scatter | solution.py:492
  1550.2 181.5 %reduce-scatter.21.cloned.1.call-done = f32[32,4096]{1,0:T(8,128)} async-done(((f32[1024,4096]{1,0:T(8,128)}), f32[32,4096]{1,0:T(8,128)}) %reduce-scatter.21.cloned.1.call-update) | async-done | bytes 524304 | tf_op jit(solution)/shard_map/reduce_scatter | solution.py:491
  1731.7 170.8 %reduce-scatter.11.cloned.1.call-done = f32[32,3352]{1,0:T(8,128)} async-done(((f32[1024,3352]{1,0:T(8,128)}), f32[32,3352]{1,0:T(8,128)}) %reduce-scatter.11.cloned.1.call-update) | async-done | bytes 429072 | tf_op jit(solution)/shard_map/reduce_scatter | solution.py:485
  (650 shorter events, 259.6 us)
Async XLA Ops:
  7.2 96.8 %copy-start.77 = (f32[4,1792]{1,0:T(4,128)S(1)}, f32[4,1792]{1,0:T(4,128)}, u32[]{:S(2)}) copy-start(f32[4,1792]{1,0:T(4,128)} %param.32) | copy-start | bytes 86020
  7.2 96.9 %copy-start.114 = (f32[24]{0:T(128)S(1)}, f32[24]{0:T(128)}, u32[]{:S(2)}) copy-start(f32[24]{0:T(128)} %param.35) | copy-start | bytes 292
  7.2 97.8 %all-gather.13.cloned.1.call-start = ((), (), s32[]{:S(2)}) async-start(), calls=%async_computation.8 | async-start | bytes 7299072 | tf_op jit(solution)/shard_map/all_gather | solution.py:311
  7.9 136.0 %all-gather.19.cloned.1.call-start = ((), (), s32[]{:S(2)}) async-start(), calls=%async_computation.11 | async-start | bytes 1081344 | tf_op jit(solution)/shard_map/all_gather | solution.py:313
  8.7 193.9 %all-gather.17.cloned.1.call-start = ((), (), s32[]{:S(2)}) async-start(), calls=%async_computation.10 | async-start | bytes 2162688 | tf_op jit(solution)/shard_map/all_gather | solution.py:373
  53.3 46.8 %copy-start.108 = (f32[128]{0:T(128)}, f32[128]{0:T(128)S(1)}, u32[]{:S(2)}) copy-start(f32[128]{0:T(128)S(1)} %add_rsqrt_fusion.1) | copy-start | bytes 1540
  54.5 89.4 %copy-start.9 = (bf16[128,1024]{1,0:T(8,128)(2,1)}, bf16[128,1024]{1,0:T(8,128)(2,1)S(1)}, u32[]{:S(2)}) copy-start(bf16[128,1024]{1,0:T(8,128)(2,1)S(1)} %multiply_convert_fusion.4) | copy-start | bytes 786436
  100.0 200.2 %all-gather.27.cloned.1.call-start = ((), (), s32[]{:S(2)}) async-start(), calls=%async_computation.23 | async-start | bytes 12976128 | tf_op jit(solution)/shard_map/all_gather | solution.py:36
  104.1 16.3 copy-start.64
  104.1 16.3 copy-start.66
  104.1 16.3 copy-start.68
  110.8 236.1 %copy-start.5 = (f32[128,3352]{0,1:T(8,128)}, f32[128,3352]{0,1:T(8,128)S(1)}, u32[]{:S(2)}) copy-start(f32[128,3352]{0,1:T(8,128)S(1)} %fusion.176) | copy-start | bytes 5148676
  113.8 5.4 collective-permute-start
  127.5 79.1 %copy-start.11 = (f32[128,1536]{0,1:T(8,128)}, f32[128,1536]{0,1:T(8,128)S(1)}, u32[]{:S(2)}) copy-start(f32[128,1536]{0,1:T(8,128)S(1)} %slice.168) | copy-start | bytes 2359300
  130.0 230.9 %all-gather.15.cloned.1.call-start = ((), (), s32[]{:S(2)}) async-start(), calls=%async_computation.9 | async-start | bytes 3244032 | tf_op jit(solution)/shard_map/all_gather | solution.py:312
  130.6 285.4 %all-gather.21.cloned.1.call-start = ((), (), s32[]{:S(2)}) async-start(), calls=%async_computation.12 | async-start | bytes 1081344 | tf_op jit(solution)/shard_map/all_gather | solution.py:315
  131.1 363.8 %all-gather.23.cloned.1.call-start = ((), (), s32[]{:S(2)}) async-start(), calls=%async_computation.13 | async-start | bytes 8650752 | tf_op jit(solution)/shard_map/all_gather | solution.py:317
  131.9 426.3 %all-gather.25.cloned.1.call-start = ((), (), s32[]{:S(2)}) async-start(), calls=%async_computation.14 | async-start | bytes 4325376 | tf_op jit(solution)/shard_map/all_gather | solution.py:318
  132.6 642.7 %reduce-scatter.9.cloned.1.call-start = ((), (), s32[]{:S(2)}) async-start(), calls=%async_computation.15 | async-start | bytes 4325376 | tf_op jit(solution)/shard_map/reduce_scatter | solution.py:438
  147.1 59.5 %copy-start.61 = (f32[2,4,128]{2,1,0:T(4,128)S(1)}, f32[2,4,128]{2,1,0:T(4,128)}, u32[]{:S(2)}) copy-start(f32[2,4,128]{2,1,0:T(4,128)} %custom-call.1) | copy-start | bytes 12292
  222.9 21.6 %copy-start.51 = (f32[1,24,128]{2,1,0:T(8,128)S(1)}, f32[1,24,128]{2,1,0:T(8,128)}, u32[]{:S(2)}) copy-start(f32[1,24,128]{2,1,0:T(8,128)} %copy-done.50) | copy-start | bytes 36868
  222.9 21.6 %copy-start.94 = (pred[128]{0:T(512)(128)(4,1)S(1)}, pred[128]{0:T(512)(128)(4,1)}, u32[]{:S(2)}) copy-start(pred[128]{0:T(512)(128)(4,1)} %copy-done.93) | copy-start | bytes 388
  222.9 22.1 %copy-start.97 = (bf16[1024]{0:T(1024)(128)(2,1)S(1)}, bf16[1024]{0:T(1024)(128)(2,1)}, u32[]{:S(2)}) copy-start(bf16[1024]{0:T(1024)(128)(2,1)} %dynamic-update-slice.2) | copy-start | bytes 6148
  244.4 43.2 %copy-start.58 = (s32[128]{0:T(128)}, s32[128]{0:T(128)S(1)}, u32[]{:S(2)}) copy-start(s32[128]{0:T(128)S(1)} %get-tuple-element.1685) | copy-start | bytes 1540
  244.4 55.8 %copy-start.24 = (bf16[128,2,4,64]{0,3,2,1:T(8,128)(2,1)}, bf16[128,2,4,64]{0,3,2,1:T(8,128)(2,1)S(1)}, u32[]{:S(2)}) copy-start(bf16[128,2,4,64]{0,3,2,1:T(8,128)(2,1)S(1)} %get-tuple-element.1663) | copy-start | bytes 393220
  244.4 55.8 %copy-start.46 = (f32[128,2,4,64]{0,3,2,1:T(8,128)}, f32[128,2,4,64]{0,3,2,1:T(8,128)S(1)}, u32[]{:S(2)}) copy-start(f32[128,2,4,64]{0,3,2,1:T(8,128)S(1)} %get-tuple-element.794) | copy-start | bytes 786436
  244.5 171.5 %copy-start.43 = (bf16[128,2,4,64]{0,3,2,1:T(8,128)(2,1)}, bf16[128,2,4,64]{0,3,2,1:T(8,128)(2,1)S(1)}, u32[]{:S(2)}) copy-start(bf16[128,2,4,64]{0,3,2,1:T(8,128)(2,1)S(1)} %convert_element_type.155) | copy-start | bytes 393220
  244.5 97.2 %copy-start.56 = (f32[128,24]{0,1:T(8,128)}, f32[128,24]{0,1:T(8,128)S(1)}, u32[]{:S(2)}) copy-start(f32[128,24]{0,1:T(8,128)S(1)} %fusion.236) | copy-start | bytes 36868
  291.2 50.5 %copy-start.74 = (f32[128,128]{1,0:T(8,128)}, f32[128,128]{1,0:T(8,128)S(1)}, u32[]{:S(2)}) copy-start(f32[128,128]{1,0:T(8,128)S(1)} %fusion.126) | copy-start | bytes 196612
  300.2 41.6 %copy-start.81 = (pred[128,128]{1,0:T(8,128)(4,1)S(1)}, pred[128,128]{1,0:T(8,128)(4,1)}, u32[]{:S(2)}) copy-start(pred[128,128]{1,0:T(8,128)(4,1)} %fusion.121) | copy-start | bytes 49156
  300.2 41.6 %copy-start.83 = (f32[24,128]{1,0:T(8,128)S(1)}, f32[24,128]{1,0:T(8,128)}, u32[]{:S(2)}) copy-start(f32[24,128]{1,0:T(8,128)} %get-tuple-element.1183) | copy-start | bytes 36868
  300.2 41.6 %copy-start.112 = (f32[24]{0:T(128)S(1)}, f32[24]{0:T(128)}, u32[]{:S(2)}) copy-start(f32[24]{0:T(128)} %param.36) | copy-start | bytes 292
  341.8 19.1 %copy-start.7 = (f32[128,1024]{1,0:T(8,128)S(1)}, f32[128,1024]{1,0:T(8,128)}, u32[]{:S(2)}) copy-start(f32[128,1024]{1,0:T(8,128)} %param.27) | copy-start | bytes 1572868
  417.8 148.7 %copy-start.3 = (f32[128,1024]{1,0:T(8,128)}, f32[128,1024]{1,0:T(8,128)S(1)}, u32[]{:S(2)}) copy-start(f32[128,1024]{1,0:T(8,128)S(1)} %get-tuple-element.1195) | copy-start | bytes 1572868
  417.8 148.7 %copy-start.78 = (f32[128]{0:T(128)}, f32[128]{0:T(128)S(1)}, u32[]{:S(2)}) copy-start(f32[128]{0:T(128)S(1)} %add_rsqrt_fusion) | copy-start | bytes 1540
  494.9 63.2 %copy-start.40 = (f32[128,1024]{1,0:T(8,128)S(1)}, f32[128,1024]{1,0:T(8,128)}, u32[]{:S(2)}) copy-start(f32[128,1024]{1,0:T(8,128)} %param.28) | copy-start | bytes 1572868
  633.6 236.1 %all-gather.29.cloned.1.call-start = ((), (), s32[]{:S(2)}) async-start(), calls=%async_computation.24 | async-start | bytes 12976128 | tf_op jit(solution)/shard_map/all_gather | solution.py:36
  641.4 380.5 %reduce-scatter.15.cloned.1.call-start = ((), (), s32[]{:S(2)}) async-start(), calls=%async_computation.18 | async-start | bytes 2162688 | tf_op jit(solution)/shard_map/reduce_scatter | solution.py:487
  643.4 502.7 %reduce-scatter.19.cloned.1.call-start = ((), (), s32[]{:S(2)}) async-start(), calls=%async_computation.20 | async-start | bytes 2162688 | tf_op jit(solution)/shard_map/reduce_scatter | solution.py:489
  645.3 618.0 %reduce-scatter.13.cloned.1.call-start = ((), (), s32[]{:S(2)}) async-start(), calls=%async_computation.17 | async-start | bytes 6488064 | tf_op jit(solution)/shard_map/reduce_scatter | solution.py:486
  648.9 128.6 %copy-start.34 = (bf16[128,2048]{1,0:T(8,128)(2,1)S(1)}, bf16[128,2048]{1,0:T(8,128)(2,1)}, u32[]{:S(2)}) copy-start(bf16[128,2048]{1,0:T(8,128)(2,1)} %get-tuple-element.1181) | copy-start | bytes 1572868
  649.0 128.6 %copy-start.41 = (f32[128,1024]{1,0:T(8,128)S(1)}, f32[128,1024]{1,0:T(8,128)}, u32[]{:S(2)}) copy-start(f32[128,1024]{1,0:T(8,128)} %param.28) | copy-start | bytes 1572868
  649.0 752.6 %reduce-scatter.17.cloned.1.call-start = ((), (), s32[]{:S(2)}) async-start(), calls=%async_computation.19 | async-start | bytes 1081344 | tf_op jit(solution)/shard_map/reduce_scatter | solution.py:488
  777.5 772.6 %reduce-scatter.23.cloned.1.call-start = ((), (), s32[]{:S(2)}) async-start(), calls=%async_computation.22 | async-start | bytes 8650752 | tf_op jit(solution)/shard_map/reduce_scatter | solution.py:492
  782.2 949.5 %reduce-scatter.21.cloned.1.call-start = ((), (), s32[]{:S(2)}) async-start(), calls=%async_computation.21 | async-start | bytes 17301504 | tf_op jit(solution)/shard_map/reduce_scatter | solution.py:491
  791.9 1110.5 %reduce-scatter.11.cloned.1.call-start = ((), (), s32[]{:S(2)}) async-start(), calls=%async_computation.16 | async-start | bytes 14598144 | tf_op jit(solution)/shard_map/reduce_scatter | solution.py:485
  951.0 3.1 collective-permute-start.1
  976.3 44.7 %copy-start.42 = (f32[128,1024]{1,0:T(8,128)S(1)}, f32[128,1024]{1,0:T(8,128)}, u32[]{:S(2)}) copy-start(f32[128,1024]{1,0:T(8,128)} %get-tuple-element.1169) | copy-start | bytes 1572868
  (92 other events, 426.3 us)
Sparse Core Ops, SparseCore 0:
  10.9 77.4 all-gather.12
  91.2 52.6 all-gather.18
  147.3 55.1 all-gather.16
  205.8 94.2 all-gather.26
  302.9 57.9 all-gather.14
  363.6 52.3 all-gather.20
  418.8 76.0 all-gather.22
  497.8 60.3 all-gather.24
  633.7 141.6 reduce-scatter.8
  778.6 91.0 all-gather.28
  872.5 136.7 reduce-scatter.14
  1012.0 134.0 reduce-scatter.18
  1152.3 110.8 reduce-scatter.12
  1265.9 135.6 reduce-scatter.16
  1404.3 145.8 reduce-scatter.22
  1552.9 178.7 reduce-scatter.20
  1738.1 164.2 reduce-scatter.10
where the time goes:
time: 1920 us; the launch traced here: 1910 us
  waiting for transfers between devices  1350 us (70%)
  blocking collectives  172 us (9%)
  matrix products  144 us (8%)
  other arithmetic  142 us (7%)
  local copies, waits for them, and re-layouts  65.8 us (3%)
    reduce_scatter x1, waiting for transfers between devices, local(): lax.psum_scatter(gateup_grad, 'seq', scatter_dimension=0, tiled=True)  182 us
    reduce_scatter x1, waiting for transfers between devices, local(): lax.psum_scatter(inner_grad, 'seq', scatter_dimension=0, tiled=True)  171 us
    reduce_scatter x1, waiting for transfers between devices, local(): lax.psum_scatter(down_grad, 'seq', scatter_dimension=1, tiled=True)  149 us
    reduce_scatter x1, waiting for transfers between devices, local(): lax.psum_scatter(keyval_grad_w, 'seq', scatter_dimension=0, tiled=True)  138 us
    unnamed x3, blocking collectives  128 us
    reduce_scatter x1, waiting for transfers between devices, local(): lax.psum_scatter(keyvalue_accumulator, 'seq', scatter_dimension=0, tiled=...  126 us
    reduce_scatter x1, waiting for transfers between devices, local(): lax.psum_scatter(output_grad_w, 'seq', scatter_dimension=1, tiled=True)  124 us
    reduce_scatter x1, waiting for transfers between devices, local(): lax.psum_scatter(mixer_grad, 'seq', scatter_dimension=1, tiled=True)  117 us
  transfers between devices with their start and end apart: 19, of which 16 were waited for; matrix products, arithmetic and copies ran while one was open for 15% of the time, Pallas kernels for 0%

commit v1 on v0

--- a/solution.py
+++ b/solution.py
@@ -4,6 +4,8 @@
 import jax
 import jax.numpy as jnp
 from jax import lax
+from jax.experimental import pallas as pl
+from jax.experimental.pallas import tpu as pltpu
 from jax.sharding import PartitionSpec as P
 
 FF = 2048
@@ -30,28 +32,104 @@
     return lax.ppermute(block, axis, route)
 
 
-def prefix(shard, axis, combine, identity, reverse):
-    size, here = (lax.axis_size(axis), lax.axis_index(axis))
-    everything = jax.tree.map(
-        lambda part, kind: lax.all_gather(part.astype(kind), axis),
-        shard,
-        (jnp.bfloat16, jnp.bfloat16),
-    )
-    start = jax.tree.map(
-        lambda part, zero: jnp.broadcast_to(jnp.asarray(zero, part.dtype), part.shape),
-        shard,
-        identity,
-    )
-
-    def hop(k, before):
-        at = size - 1 - k if reverse else k
-        reached = at > here if reverse else at < here
-        new = combine(
-            before, jax.tree.map(lambda part, own: part[at].astype(own.dtype), everything, shard)
+def ring_order(devices):
+    chips = devices // 2
+    depth = 4
+    side = math.isqrt(max(chips // depth, 1))
+    if devices % 2 or chips != depth * side * side or side % 2:
+        return list(range(devices))
+    plane = []
+    for a in range(side):
+        line = [(a, b) for b in range(1, side)]
+        plane += line if a % 2 == 0 else line[::-1]
+    plane += [(a, 0) for a in range(side - 1, -1, -1)]
+    order = []
+    for number, (a, b) in enumerate(plane):
+        levels = range(depth) if number % 2 == 0 else range(depth - 1, -1, -1)
+        for z in levels:
+            chip = (z * side + a) * side + b
+            order += [2 * chip, 2 * chip + 1]
+    return order
+
+
+def reordered(values, order):
+    width = values.shape[1] // len(order)
+    runs = []
+    for block in order:
+        if runs and runs[-1][1] == block:
+            runs[-1][1] = block + 1
+        else:
+            runs.append([block, block + 1])
+    return jnp.concatenate([values[:, a * width : b * width] for a, b in runs], axis=1)
+
+
+def inverse_of(order):
+    inverse = [0] * len(order)
+    for place, block in enumerate(order):
+        inverse[block] = place
+    return inverse
+
+
+def swapped(values, axis, bit):
+    size = lax.axis_size(axis)
+    return lax.ppermute(values, axis, [(i, i ^ bit) for i in range(size)])
+
+
+def gathered_by_doubling(rows, axis):
+    size, here = lax.axis_size(axis), lax.axis_index(axis)
+    levels = size.bit_length() - 1
+    if size != 1 << levels:
+        return lax.all_gather(rows, axis, axis=0, tiled=True)
+    block = rows.reshape((1,) * levels + rows.shape)
+    for place in range(levels):
+        bit = 1 << (levels - 1 - place)
+        other = swapped(block, axis, bit)
+        high = (here & bit) != 0
+        block = jnp.concatenate(
+            [jnp.where(high, other, block), jnp.where(high, block, other)], axis=place
         )
-        return jax.tree.map(lambda a, b: jnp.where(reached, a, b), new, before)
-
-    return lax.fori_loop(0, size, hop, start)
+    return block.reshape((size * rows.shape[0],) + rows.shape[1:])
+
+
+def scattered_by_halving(total, axis):
+    size, here = lax.axis_size(axis), lax.axis_index(axis)
+    levels = size.bit_length() - 1
+    if size != 1 << levels:
+        return lax.psum_scatter(total, axis, scatter_dimension=0, tiled=True)
+    rows = total.shape[0] // size
+    block = total.reshape((2,) * levels + (rows,) + total.shape[1:])
+    for place in range(levels - 1, -1, -1):
+        bit = 1 << (levels - 1 - place)
+        high = ((here & bit) != 0).astype(jnp.int32)
+        kept = lax.dynamic_index_in_dim(block, high, axis=place, keepdims=False)
+        sent = lax.dynamic_index_in_dim(block, 1 - high, axis=place, keepdims=False)
+        block = kept + swapped(sent.astype(jnp.bfloat16), axis, bit).astype(jnp.float32)
+    return block.reshape((rows,) + total.shape[1:])
+
+
+def carry_kernel(decay_ref, fresh_ref, out_ref, *, reverse):
+    count = fresh_ref.shape[0]
+
+    def hop(number, carried):
+        k = count - 1 - number if reverse else number
+        out_ref[k] = carried.astype(out_ref.dtype)
+        return decay_ref[k] * carried + fresh_ref[k].astype(jnp.float32)
+
+    lax.fori_loop(0, count, hop, jnp.zeros(fresh_ref.shape[1:], jnp.float32))
+
+
+def carried_states(decay_rows, states, axis, reverse):
+    size = lax.axis_size(axis)
+    share = states.shape[0] // size
+    sent = states.astype(jnp.bfloat16).reshape(size, share, states.shape[1])
+    fresh = lax.all_to_all(sent, axis, 0, 0, tiled=True)
+    folded = pl.pallas_call(
+        partial(carry_kernel, reverse=reverse),
+        out_shape=jax.ShapeDtypeStruct(fresh.shape, jnp.bfloat16),
+        name="carry",
+    )(decay_rows, fresh)
+    back = lax.all_to_all(folded, axis, 0, 0, tiled=True)
+    return back.reshape(states.shape).astype(jnp.float32)
 
 
 def matmul(left, right):
@@ -149,18 +227,6 @@
     return (local_out, final_state, reach, ssm_c.reshape(row_count, NS))
 
 
-def join_forward(earlier, later):
-    decay_low, state_low = earlier
-    decay_high, state_high = later
-    return (decay_low * decay_high, decay_high[:, None, None] * state_low + state_high)
-
-
-def join_backward(earlier, later):
-    decay_high, grad_high = earlier
-    decay_low, grad_lower = later
-    return (decay_low * decay_high, grad_lower + decay_low[:, None, None] * grad_high)
-
-
 def over_keys(update, initial_carry, key_rows_all, row_limit, query_rows, doc_span):
     count_all = key_rows_all.shape[0]
     block_size = math.gcd(count_all, 512)
@@ -282,6 +348,7 @@
 
 
 def local(
+    order,
     layer_input,
     out_grad,
     doc_ids,
@@ -302,41 +369,63 @@
 ):
     local_row_count = layer_input.shape[0]
     devices = lax.axis_size("seq")
+    here = lax.axis_index("seq")
     sequence_total = local_row_count * devices
     doc_span = sequence_total // 2 + local_row_count
-    first_row = lax.axis_index("seq") * local_row_count
+    first_row = here * local_row_count
     query_group_width = QUERY_HEADS // KEYVALUE_HEADS
-    gathered = (
-        lax.all_gather(norm1_gain, "seq", axis=0, tiled=True),
-        lax.all_gather(in_weight, "seq", axis=0, tiled=True),
-        lax.all_gather(mixer_out, "seq", axis=1, tiled=True),
-        lax.all_gather(query_weight, "seq", axis=0, tiled=True),
-        lax.all_gather(keyvalue_weight, "seq", axis=0, tiled=True),
-        lax.all_gather(attn_out, "seq", axis=1, tiled=True),
-        lax.all_gather(norm2_gain, "seq", axis=0, tiled=True),
-        lax.all_gather(gate_up, "seq", axis=0, tiled=True),
-        lax.all_gather(down_weight, "seq", axis=1, tiled=True),
-    )
-    gain_first = gathered[0].astype(jnp.float32)
-    inner_full = gathered[1]
-    mixer_full = gathered[2]
-    query_full = gathered[3]
-    keyval_full = gathered[4]
-    output_full = gathered[5]
-    gain_second = gathered[6].astype(jnp.float32)
-    gateup_full = gathered[7]
-    downward_full = gathered[8]
+    query_cols = QUERY_HEADS * HEAD_SIZE
+    keyval_cols = 2 * KEYVALUE_HEADS * HEAD_SIZE
+    feature_rows = in_weight.shape[0]
+    q_at = DSSM + CONV_CH
+    kv_at = q_at + query_cols
+    dt_at = kv_at + keyval_cols
+    gain_at = dt_at + HM
+    packed_cols = -(-(gain_at + 2) // 128) * 128
+    first_pack = jnp.concatenate(
+        [
+            in_weight[:, :q_at],
+            query_weight,
+            keyvalue_weight,
+            in_weight[:, q_at:],
+            norm1_gain[:, None],
+            norm2_gain[:, None],
+            jnp.zeros((feature_rows, packed_cols - gain_at - 2), jnp.bfloat16),
+        ],
+        axis=1,
+    )
+    second_pack = jnp.concatenate(
+        [gate_up, jnp.concatenate([mixer_out, attn_out, down_weight], axis=0).T], axis=1
+    )
+    first_full = lax.all_gather(
+        first_pack, "seq", axis=0, tiled=True, axis_index_groups=[order]
+    )
+    second_pack, first_full = lax.optimization_barrier((second_pack, first_full))
+    second_full = lax.all_gather(
+        second_pack, "seq", axis=0, tiled=True, axis_index_groups=[order]
+    )
+    gains = first_full[:, gain_at : gain_at + 2].astype(jnp.float32)
+    gain_first = gains[:, 0]
+    gain_second = gains[:, 1]
+    gateup_full = second_full[:, : 2 * FF]
+    outward_full = second_full[:, 2 * FF : 2 * FF + DSSM + query_cols]
+    downward_full = second_full[:, 2 * FF + DSSM + query_cols :]
+    layer_input = reordered(layer_input, order)
+    out_grad = reordered(out_grad, order)
     seg_here = lax.dynamic_slice_in_dim(doc_ids, first_row, local_row_count)
     seg_padded = jnp.concatenate([jnp.full((KC - 1,), -1, jnp.int32), doc_ids])
     seg_window = lax.dynamic_slice_in_dim(seg_padded, first_row, local_row_count + KC - 1)
     seg_before = seg_window[KC - 2]
     scale_one = rms_scale(layer_input)
     normed_one = (layer_input * scale_one * gain_first).astype(jnp.bfloat16)
-    projected = matmul(normed_one, inner_full)
+    projected = matmul(normed_one, first_full)
     gate_mix = projected[:, :DSSM]
-    conv_in = projected[:, DSSM : DSSM + CONV_CH]
-    dt_raw = projected[:, DSSM + CONV_CH :]
+    conv_in = projected[:, DSSM:q_at]
+    query_reduced = projected[:, q_at:kv_at].astype(jnp.bfloat16)
+    keyval_low = projected[:, kv_at:dt_at].astype(jnp.bfloat16)
+    dt_raw = projected[:, dt_at:gain_at]
     edge_rows = passed_along(conv_in[local_row_count - (KC - 1) :], "seq", 1)
+    keyval_all = gathered_by_doubling(keyval_low, "seq")
     conv_ext = jnp.concatenate([edge_rows, conv_in], axis=0)
     conv_act, conv_pull = jax.vjp(partial(conv_apply, seg_window), conv_ext, conv_weight, conv_bias)
     ssm_parts, ssm_pull = jax.vjp(
@@ -344,20 +433,17 @@
     )
     local_out, dev_state, reach, c_here = ssm_parts
     dev_decay = reach[:, -1]
-    scanned = prefix(
-        (dev_decay, dev_state),
-        "seq",
-        join_forward,
-        (jnp.ones_like(dev_decay), jnp.zeros_like(dev_state)),
-        False,
-    )
-    state_in = scanned[1]
+    share = HM * HP // devices
+    decay_all = gathered_by_doubling(dev_decay[None], "seq")
+    decay_rows = lax.dynamic_slice_in_dim(
+        jnp.repeat(decay_all, HP, axis=1), here * share, share, 1
+    )[:, :, None]
+    state_in = carried_states(decay_rows, dev_state.reshape(HM * HP, NS), "seq", False).reshape(
+        HM, HP, NS
+    )
     cross_base = jnp.einsum("tn,hpn->thp", c_here, state_in, precision=HIGH)
     ssm_out = (local_out + cross_base * reach.T[:, :, None]).reshape(local_row_count, DSSM)
     gated = (ssm_out * jax.nn.silu(gate_mix)).astype(jnp.bfloat16)
-    mixer_part = matmul(gated, mixer_full)
-    query_reduced = matmul(normed_one, query_full).astype(jnp.bfloat16)
-    keyval_low = matmul(normed_one, keyval_full).astype(jnp.bfloat16)
     query_quadruple = query_reduced.reshape(
         local_row_count, KEYVALUE_HEADS, query_group_width, HEAD_SIZE
     )
@@ -370,7 +456,6 @@
         (local_row_count, KEYVALUE_HEADS, query_group_width, HEAD_SIZE), jnp.float32
     )
     stats_update = partial(stats_step, query_quadruple, positions, seg_here, doc_ids)
-    keyval_all = lax.all_gather(keyval_low, "seq", axis=0, tiled=True)
     denominator = over_keys(
         stats_update, statistics_initial, keyval_all, row_limit, local_row_count, doc_span
     )
@@ -383,33 +468,41 @@
         local_row_count,
         doc_span,
     )
-    attn_low = attention_middle.reshape(local_row_count, QUERY_HEADS * HEAD_SIZE).astype(
-        jnp.bfloat16
-    )
-    attn_part = matmul(attn_low, output_full)
-    resid = layer_input + mixer_part + attn_part
+    attn_low = attention_middle.reshape(local_row_count, query_cols).astype(jnp.bfloat16)
+    mixed_low = jnp.concatenate([gated, attn_low], axis=1)
+    resid = layer_input + matmul_nt(mixed_low, outward_full)
     scale_two = rms_scale(resid)
     normed_two = (resid * scale_two * gain_second).astype(jnp.bfloat16)
     gateup = matmul(normed_two, gateup_full)
     gate_part = gateup[:, :FF]
     up_part = gateup[:, FF:]
     act_low = (jax.nn.silu(gate_part) * up_part).astype(jnp.bfloat16)
-    layer_output = resid + matmul(act_low, downward_full)
+    layer_output = reordered(
+        resid + matmul_nt(act_low, downward_full), inverse_of(order)
+    )
     grad_low = out_grad.astype(jnp.bfloat16)
-    down_grad = matmul_tn(act_low, grad_low)
-    act_grad = matmul_nt(grad_low, downward_full)
+    act_grad = matmul(grad_low, downward_full)
     gateup_grad_low = jnp.concatenate(
         [act_grad * up_part * silu_slope(gate_part), act_grad * jax.nn.silu(gate_part)], axis=1
     ).astype(jnp.bfloat16)
-    gateup_grad = matmul_tn(normed_two, gateup_grad_low)
     normed_two_grad = matmul_nt(gateup_grad_low, gateup_full)
     gain2_grad = jnp.sum(normed_two_grad * resid * scale_two, axis=0)
     resid_grad = out_grad + rms_back(resid, scale_two, gain_second, normed_two_grad)
     resid_low = resid_grad.astype(jnp.bfloat16)
-    mixer_grad = matmul_tn(gated, resid_low)
-    output_grad_w = matmul_tn(attn_low, resid_low)
-    gated_grad = matmul_nt(resid_low, mixer_full)
-    attention_gradient = matmul_nt(resid_low, output_full)
+    second_grad = jnp.concatenate(
+        [
+            matmul_tn(normed_two, gateup_grad_low).astype(jnp.bfloat16),
+            matmul_tn(resid_low, mixed_low).astype(jnp.bfloat16),
+            matmul_tn(grad_low, act_low).astype(jnp.bfloat16),
+        ],
+        axis=1,
+    )
+    second_share = lax.psum_scatter(
+        second_grad, "seq", scatter_dimension=0, tiled=True, axis_index_groups=[order]
+    ).astype(jnp.float32)
+    mixed_grad = matmul(resid_low, outward_full)
+    gated_grad = mixed_grad[:, :DSSM]
+    attention_gradient = mixed_grad[:, DSSM:]
     gradient_quadruple = attention_gradient.astype(jnp.bfloat16).reshape(
         local_row_count, KEYVALUE_HEADS, query_group_width, HEAD_SIZE
     )
@@ -420,7 +513,7 @@
     ).transpose(1, 2, 0)
     back_init = (
         jnp.zeros((local_row_count, KEYVALUE_HEADS, query_group_width, HEAD_SIZE), jnp.float32),
-        jnp.zeros((sequence_total, 2 * KEYVALUE_HEADS * HEAD_SIZE), jnp.float32),
+        jnp.zeros((sequence_total, keyval_cols), jnp.float32),
     )
     back_update = partial(
         back_step,
@@ -435,13 +528,11 @@
     query_accumulator, keyvalue_accumulator = over_keys(
         back_update, back_init, keyval_all, row_limit, local_row_count, doc_span
     )
-    keyval_here = lax.psum_scatter(keyvalue_accumulator, "seq", scatter_dimension=0, tiled=True)
+    keyval_here = scattered_by_halving(keyvalue_accumulator, "seq")
     query_grad_low = (
-        query_accumulator.reshape(local_row_count, QUERY_HEADS * HEAD_SIZE) * HEAD_SIZE ** (-0.5)
+        query_accumulator.reshape(local_row_count, query_cols) * HEAD_SIZE ** (-0.5)
     ).astype(jnp.bfloat16)
     keyval_grad_low = keyval_here.astype(jnp.bfloat16)
-    query_grad_w = matmul_tn(normed_one, query_grad_low)
-    keyval_grad_w = matmul_tn(normed_one, keyval_grad_low)
     ssm_grad = gated_grad * jax.nn.silu(gate_mix)
     gate_mix_grad = gated_grad * ssm_out * silu_slope(gate_mix)
     ssm_grad_three = ssm_grad.reshape(local_row_count, HM, HP)
@@ -449,14 +540,9 @@
     state_in_grad = jnp.einsum("thp,tn->hpn", weighted_grad, c_here, precision=HIGH)
     c_grad = jnp.einsum("thp,hpn->tn", weighted_grad, state_in, precision=HIGH)
     reach_grad = jnp.einsum("thp,thp->ht", ssm_grad_three, cross_base, precision=HIGH)
-    back_scan = prefix(
-        (dev_decay, state_in_grad),
-        "seq",
-        join_backward,
-        (jnp.ones_like(dev_decay), jnp.zeros_like(dev_state)),
-        True,
-    )
-    state_out_grad = back_scan[1]
+    state_out_grad = carried_states(
+        decay_rows, state_in_grad.reshape(HM * HP, NS), "seq", True
+    ).reshape(HM, HP, NS)
     decay_grad = jnp.sum(state_out_grad * state_in, axis=(1, 2))
     reach_grad = jnp.concatenate(
         [reach_grad[:, :-1], reach_grad[:, -1:] + decay_grad[:, None]], axis=1
@@ -469,48 +555,64 @@
     conv_in_grad = ext_grad[KC - 1 :] + jnp.concatenate(
         [jnp.zeros((local_row_count - (KC - 1), CONV_CH), jnp.float32), edge_back], axis=0
     )
-    proj_grad_low = jnp.concatenate([gate_mix_grad, conv_in_grad, dt_raw_grad], axis=1).astype(
-        jnp.bfloat16
-    )
-    inner_grad = matmul_tn(normed_one, proj_grad_low)
-    normed_one_grad = (
-        matmul_nt(proj_grad_low, inner_full)
-        + matmul_nt(query_grad_low, query_full)
-        + matmul_nt(keyval_grad_low, keyval_full)
-    )
+    first_grad_low = jnp.concatenate(
+        [
+            gate_mix_grad.astype(jnp.bfloat16),
+            conv_in_grad.astype(jnp.bfloat16),
+            query_grad_low,
+            keyval_grad_low,
+            dt_raw_grad.astype(jnp.bfloat16),
+            jnp.zeros((local_row_count, packed_cols - gain_at), jnp.bfloat16),
+        ],
+        axis=1,
+    )
+    first_share = lax.psum_scatter(
+        matmul_tn(normed_one, first_grad_low).astype(jnp.bfloat16),
+        "seq",
+        scatter_dimension=0,
+        tiled=True,
+        axis_index_groups=[order],
+    ).astype(jnp.float32)
+    normed_one_grad = matmul_nt(first_grad_low, first_full)
     gain1_grad = jnp.sum(normed_one_grad * layer_input * scale_one, axis=0)
-    input_grad = resid_grad + rms_back(layer_input, scale_one, gain_first, normed_one_grad)
-    shares = (
-        lax.psum_scatter(gain1_grad, "seq", scatter_dimension=0, tiled=True),
-        lax.psum_scatter(inner_grad, "seq", scatter_dimension=0, tiled=True),
-        lax.psum_scatter(mixer_grad, "seq", scatter_dimension=1, tiled=True),
-        lax.psum_scatter(query_grad_w, "seq", scatter_dimension=0, tiled=True),
-        lax.psum_scatter(keyval_grad_w, "seq", scatter_dimension=0, tiled=True),
-        lax.psum_scatter(output_grad_w, "seq", scatter_dimension=1, tiled=True),
-        lax.psum_scatter(gain2_grad, "seq", scatter_dimension=0, tiled=True),
-        lax.psum_scatter(gateup_grad, "seq", scatter_dimension=0, tiled=True),
-        lax.psum_scatter(down_grad, "seq", scatter_dimension=1, tiled=True),
-    )
-    small = lax.psum(
-        (conv_weight_grad, conv_bias_grad, dt_bias_grad, decay_log_grad, skip_grad), "seq"
-    )
+    input_grad = reordered(
+        resid_grad + rms_back(layer_input, scale_one, gain_first, normed_one_grad),
+        inverse_of(order),
+    )
+    small = (
+        conv_weight_grad,
+        conv_bias_grad,
+        dt_bias_grad,
+        decay_log_grad,
+        skip_grad,
+        gain1_grad,
+        gain2_grad,
+    )
+    flat = lax.psum(jnp.concatenate([part.reshape(-1) for part in small]), "seq")
+    sums, at = ([], 0)
+    for part in small:
+        sums.append(flat[at : at + part.size].reshape(part.shape))
+        at += part.size
+    place = jnp.asarray(inverse_of(order), jnp.int32)[here] * feature_rows
+    mixed_at = 2 * FF
+    down_at = mixed_at + DSSM + query_cols
     return (
         layer_output,
         input_grad,
-        shares[0],
-        shares[1],
-        small[0],
-        small[1],
-        small[2],
-        small[3],
-        small[4],
-        shares[2],
-        shares[3],
-        shares[4],
-        shares[5],
-        shares[6],
-        shares[7],
-        shares[8],
+        lax.dynamic_slice_in_dim(sums[5], place, feature_rows),
+        jnp.concatenate([first_share[:, :q_at], first_share[:, dt_at:gain_at]], axis=1),
+        sums[0],
+        sums[1],
+        sums[2],
+        sums[3],
+        sums[4],
+        second_share[:, mixed_at : mixed_at + DSSM].T,
+        first_share[:, q_at:kv_at],
+        first_share[:, kv_at:dt_at],
+        second_share[:, mixed_at + DSSM : down_at].T,
+        lax.dynamic_slice_in_dim(sums[6], place, feature_rows),
+        second_share[:, :mixed_at],
+        second_share[:, down_at:].T,
     )
 
 
@@ -535,7 +637,7 @@
         P(None, "seq"),
     )
     return jax.shard_map(
-        local,
+        partial(local, ring_order(mesh.shape["seq"])),
         mesh=mesh,
         in_specs=placed,
         out_specs=(

time: 1920 us -> 704 us (0.37)
  waiting for transfers between devices: 1350 us -> 232 us
  blocking collectives: 172 us -> 38.7 us
  local copies, waits for them, and re-layouts: 65.8 us -> 144 us
  other arithmetic: 142 us -> 82.1 us
  starting transfers between devices: 4.47 us -> 45.3 us
  matrix products: 144 us -> 124 us
    reduce_scatter x8 -> x2, waiting for transfers between devices: 1010 us -> 129 us  [the longest x1 107 us: local(): lax.psum_scatter(second_grad, 'seq', scatter_dimension=0, tiled=True, axi...]
    all_gather x9 -> x2, waiting for transfers between devices: 339 us -> 63.3 us  [the longest x1 63.3 us: local(): lax.all_gather(first_pack, 'seq', axis=0, tiled=True, axis_index_groups=[...]
    unnamed x3 -> x0, blocking collectives: 128 us -> none
    select_n x64 -> x10, other arithmetic: 76.2 us -> 7.04 us  [gathered_by_doubling(): jnp.where(high, other, block)]
    all_gather x1 -> x0, blocking collectives: 43.8 us -> none  [local(): lax.all_gather(keyvalue_weight, 'seq', axis=0, tiled=True)]
    psum x0 -> x1, blocking collectives: none -> 38.7 us  [local(): lax.psum(jnp.concatenate([part.reshape(-1) for part in small]), 'seq')]
    ppermute x0 -> x15, waiting for transfers between devices: none -> 34.5 us  [swapped(): return lax.ppermute(values, axis, [(i, i ^ bit) for i in range(size)])]
    dynamic_slice x0 -> x15, local copies, waits for them, and re-layouts: none -> 25.2 us  [the longest x12 23.5 us: back_step(): lax.dynamic_slice_in_dim(keyvalue_accumulator, key_start, rows_per_block, 0)]
  transfers between devices with their start and end apart: 19 -> 25, of which waited for: 16 -> 12; matrix products, arithmetic and copies ran while one was open for 15% -> 43% of each run, Pallas kernels for 0% -> 1%
where the time goes in v1:
time: 704 us; the launch traced here: 692 us
  waiting for transfers between devices  232 us (33%)
  local copies, waits for them, and re-layouts  144 us (20%)
  matrix products  124 us (18%)
  other arithmetic  82.1 us (12%)
  starting transfers between devices  45.3 us (6%)
  blocking collectives  38.7 us (5%)
  between operations  16.4 us (2%)
  Pallas kernels  8.67 us (1%)
    reduce_scatter x1, waiting for transfers between devices, local(): lax.psum_scatter(second_grad, 'seq', scatter_dimension=0, tiled=True, axi...  107 us
    all_gather x1, waiting for transfers between devices, local(): lax.all_gather(first_pack, 'seq', axis=0, tiled=True, axis_index_groups=[...  63.3 us
    psum x1, blocking collectives, local(): lax.psum(jnp.concatenate([part.reshape(-1) for part in small]), 'seq')  38.7 us
    ppermute x15, waiting for transfers between devices, swapped(): return lax.ppermute(values, axis, [(i, i ^ bit) for i in range(size)])  34.5 us
    dynamic_slice x12, local copies, waits for them, and re-layouts, back_step(): lax.dynamic_slice_in_dim(keyvalue_accumulator, key_start, rows_per_block, 0)  23.5 us
    ppermute x15, starting transfers between devices, swapped(): return lax.ppermute(values, axis, [(i, i ^ bit) for i in range(size)])  23.2 us
    reduce_scatter x1, waiting for transfers between devices, local(): lax.psum_scatter(matmul_tn(normed_one, first_grad_low).astype(jnp.bfloat1...  22.4 us
    dot_general x4, matrix products, matmul_nt(): lax.dot_general(left, right, (((1,), (1,)), ((), ())), preferred_element_...  18.1 us
  transfers between devices with their start and end apart: 25, of which 12 were waited for; matrix products, arithmetic and copies ran while one was open for 43% of the time, Pallas kernels for 1%

profile of v1, /device:TPU:0, one launch (start us, length us, event | category | flops | bytes accessed | tf_op | source)
XLA Modules:
  0.0 691.9 jit_solution(8067525324421084466)
XLA Ops:
  14.9 63.3 %all-gather.3.cloned.1.call-done = bf16[1024,4224]{1,0:T(8,128)(2,1)} async-done(((bf16[32,4224]{1,0:T(8,128)(2,1)}), bf16[1024,4224]{1,0:T(8,128)(2,1)}) %all-gather.3.cloned.1.call-update) | async-done | bytes 8650768 | tf_op jit(solution)/shard_map/all_gather | solution.py:400
  91.3 6.1 fusion.179
  99.8 3.0 collective-permute-done.1
  122.0 4.7 fusion.87
  136.2 3.4 all-to-all-start
  139.6 3.9 collective-permute-done.7
  151.2 3.5 collective-permute-done.8
  157.3 6.2 collective-permute-start.9
  165.6 4.3 carry.2
  169.9 4.0 all-to-all-start.1
  175.7 2.5 convolution_bitcast_fusion.2
  178.2 12.7 %collective-permute-done.9 = bf16[2,2,2,1,1,128,256]{6,5,4,3,2,1,0:T(8,128)(2,1)} collective-permute-done((bf16[2,2,2,1,1,128,256]{6,5,4,3,2,1,0:T(8,128)(2,1)}, bf16[2,2,2,1,1,128,256]{6,5,4,3,2,1,0:T(8,128)(2,1)}, u32[]{:S(2)}, u32[]{:S(2)}) %collective-permute-start.9) | collective-permute-done | bytes 524320 | tf_op jit(solution)/shard_map/ppermute | solution.py:75
  195.7 5.6 fusion.65
  207.0 4.1 copy.159
  211.1 24.9 %while.28 = (s32[]{:T(128)}, f32[2,4,128]{2,1,0:T(4,128)S(1)}, s32[]{:T(128)}, s32[4096]{0:T(1024)}, s32[128]{0:T(128)}, /*index=5*/bf16[4096,256]{0,1:T(8,128)(...) while((s32[]{:T(128)}, f32[2,4,128]{2,1,0:T(4,128)S(1)}, ...), condition=%wide.region_4.5_spmd.clone, body=%wide.region_2.4_spmd.clone.sunk | while | flops 68880008 | bytes 683729 | solution.py:244
  236.6 36.2 %while.29 = (s32[]{:T(128)}, f32[128,2,4,64]{0,3,2,1:T(8,128)}, s32[]{:T(128)}, bf16[4096,256]{0,1:T(8,128)(2,1)}, s32[4096]{0:T(1024)}, /*index=5*/s32[128]{0:T...) while((s32[]{:T(128)}, f32[128,2,4,64]{0,3,2,1:T(8,128)}, ...), condition=%wide.region_6.7_spmd.clone, body=%wide.region_5.6_spmd.clone.sunk | while | flops 136643200 | bytes 1588977 | solution.py:244
  239.9 2.6 fusion.242
  245.8 2.7 fusion.242
  251.8 2.7 fusion.242
  257.9 2.7 fusion.242
  263.9 2.7 fusion.242
  269.9 2.7 fusion.242
  276.1 4.1 multiply_reduce_fusion.14
  280.3 5.7 fusion.30
  288.1 3.5 multiply_reduce_fusion.10
  292.6 3.5 multiply_reduce_fusion.9
  301.8 5.9 all-to-all-start.2
  312.2 70.2 %while.30 = (s32[]{:T(128)}, f32[128,2,4,64]{0,3,2,1:T(8,128)}, f32[4096,256]{1,0:T(8,128)}, s32[]{:T(128)}, bf16[4096,256]{0,1:T(8,128)(2,1)}, /*index=5*/s32[4...) while((s32[]{:T(128)}, f32[128,2,4,64]{0,3,2,1:T(8,128)}, ...), condition=%wide.region_12.13_spmd.clone, body=%wide.region_11.12_spmd.clone.sunk | while | flops 339870336 | bytes 19976044 | solution.py:244
  383.6 2.9 fusion.77
  387.9 5.2 fusion.89
  400.0 4.3 carry.3
  404.3 5.7 all-to-all-start.3
  418.6 4.7 all-to-all-done.3
  425.2 2.8 fusion.53
  428.0 2.4 copy.167
  432.0 3.1 multiply_reduce_fusion.4
  446.4 2.6 collective-permute-start.14
  452.9 3.0 collective-permute-done.14
  458.6 2.6 collective-permute-done.15
  462.6 4.6 collective-permute-done.16
  468.3 5.9 convolution_convert_fusion
  478.1 2.4 convolution_convert_fusion.1
  480.5 6.9 pad_maximum_fusion
  489.5 4.0 fusion.71
  497.1 6.5 multiply_reduce_fusion.11
  503.7 38.7 %psum.7 = f32[11080]{0:T(1024)S(1)} all-reduce(f32[11080]{0:T(1024)S(1)} %concatenate.120), channel_id=1, replica_groups=mesh['seq'=32] {'seq'}, use_global_device_ids=true, to_apply=%region_34.35 | all-reduce | flops 11080 | bytes 88640 | tf_op jit(solution)/shard_map/psum | solution.py:591
  547.0 22.4 %reduce-scatter.3.cloned.1.call-done = bf16[32,4224]{1,0:T(8,128)(2,1)} async-done(((bf16[1024,4224]{1,0:T(8,128)(2,1)}), bf16[32,4224]{1,0:T(8,128)(2,1)}) %reduce-scatter.3.cloned.1.call-update) | async-done | bytes 270352 | tf_op jit(solution)/shard_map/reduce_scatter | solution.py:569
  574.5 106.5 %reduce-scatter.5.cloned.1.call-done = bf16[32,8192]{1,0:T(8,128)(2,1)} async-done(((bf16[1024,8192]{1,0:T(8,128)(2,1)}), bf16[32,8192]{1,0:T(8,128)(2,1)}) %reduce-scatter.5.cloned.1.call-update) | async-done | bytes 524304 | tf_op jit(solution)/shard_map/reduce_scatter | solution.py:500
  (637 shorter events, 271.2 us)
Async XLA Ops:
  7.2 76.2 %copy-start.36 = (f32[128,1024]{1,0:T(8,128)S(1)}, f32[128,1024]{1,0:T(8,128)}, u32[]{:S(2)}) copy-start(f32[128,1024]{1,0:T(8,128)} %param.24) | copy-start | bytes 1572868
  7.2 71.0 %all-gather.3.cloned.1.call-start = ((), (), s32[]{:S(2)}) async-start(), calls=%async_computation.6 | async-start | bytes 8921088 | tf_op jit(solution)/shard_map/all_gather | solution.py:400
  12.0 264.1 %all-gather.5.cloned.1.call-start = ((), (), s32[]{:S(2)}) async-start(), calls=%async_computation.7 | async-start | bytes 17301504 | tf_op jit(solution)/shard_map/all_gather | solution.py:404
  14.9 69.0 %copy-start.37 = (f32[128,1024]{1,0:T(8,128)S(1)}, f32[128,1024]{1,0:T(8,128)}, u32[]{:S(2)}) copy-start(f32[128,1024]{1,0:T(8,128)} %param.25) | copy-start | bytes 1572868
  81.6 26.1 %copy-start.95 = (pred[128]{0:T(512)(128)(4,1)}, pred[128]{0:T(512)(128)(4,1)S(1)}, u32[]{:S(2)}) copy-start(pred[128]{0:T(512)(128)(4,1)S(1)} %get-tuple-element.881) | copy-start | bytes 388
  83.9 192.2 %copy-start.1 = (f32[128,1024]{1,0:T(8,128)}, f32[128,1024]{1,0:T(8,128)S(1)}, u32[]{:S(2)}) copy-start(f32[128,1024]{1,0:T(8,128)S(1)} %concatenate.94) | copy-start | bytes 1572868
  85.8 36.2 %copy-start.64 = (f32[1792]{0:T(1024)}, f32[1792]{0:T(1024)S(1)}, u32[]{:S(2)}) copy-start(f32[1792]{0:T(1024)S(1)} %get-tuple-element.812) | copy-start | bytes 21508
  85.9 11.5 %copy-start.85 = (f32[128]{0:T(128)}, f32[128]{0:T(128)S(1)}, u32[]{:S(2)}) copy-start(f32[128]{0:T(128)S(1)} %add_rsqrt_fusion.1) | copy-start | bytes 1540
  86.0 11.5 %copy-start.106 = (f32[24]{0:T(128)}, f32[24]{0:T(128)S(1)}, u32[]{:S(2)}) copy-start(f32[24]{0:T(128)S(1)} %exponential_negate_fusion) | copy-start | bytes 292
  87.3 12.4 %copy-start.99 = (pred[128]{0:T(512)(128)(4,1)}, pred[128]{0:T(512)(128)(4,1)S(1)}, u32[]{:S(2)}) copy-start(pred[128]{0:T(512)(128)(4,1)S(1)} %broadcast_compare_fusion) | copy-start | bytes 388
  97.4 195.1 %copy-start.3 = (f32[128,4224]{1,0:T(8,128)}, f32[128,4224]{1,0:T(8,128)S(1)}, u32[]{:S(2)}) copy-start(f32[128,4224]{1,0:T(8,128)S(1)} %get-tuple-element.997) | copy-start | bytes 6488068
  97.9 19.3 %copy-start.38 = (f32[1,24,128]{1,2,0:T(8,128)}, f32[1,24,128]{1,2,0:T(8,128)S(1)}, u32[]{:S(2)}) copy-start(f32[1,24,128]{1,2,0:T(8,128)S(1)} %copy.152) | copy-start | bytes 36868
  98.2 4.7 collective-permute-start.1
  99.7 13.2 %copy-start.93 = (f32[24]{0:T(128)}, f32[24]{0:T(128)S(1)}, u32[]{:S(2)}) copy-start(f32[24]{0:T(128)S(1)} %slice_reduce_fusion.2) | copy-start | bytes 292
  102.8 3.8 collective-permute-start.2
  106.6 6.3 collective-permute-start.3
  107.7 11.4 %copy-start.61 = (f32[128,24]{0,1:T(8,128)}, f32[128,24]{0,1:T(8,128)S(1)}, u32[]{:S(2)}) copy-start(f32[128,24]{0,1:T(8,128)S(1)} %fusion.212) | copy-start | bytes 36868
  109.3 22.6 %collective-permute-start.6 = (bf16[1,1,1,1,1,128,256]{6,5,4,3,2,1,0:T(8,128)(2,1)}, bf16[1,1,1,1,1,128,256]{6,5,4,3,2,1,0:T(8,128)(2,1)}, u32[]{:S(2)}, u32[]{:S(2)}) collective-permute-start(bf16[1,1,1,1,1,128,256]{6,5,4,3,2,1,0:T(8,128)(2,1)} %slice_bitcast_fusion.3), channel_id=1, source_target_pairs={{0,16},{1,17},{2,18},{3,19},{4,20},{5,21},{6,22},{7,23},{8,24},{9,... | collective-permute-start | bytes 196616 | tf_op jit(solution)/shard_map/ppermute | solution.py:75
  111.7 10.3 %collective-permute-start = (f32[3,1792]{1,0:T(4,128)}, f32[3,1792]{1,0:T(4,128)S(1)}, u32[]{:S(2)}, u32[]{:S(2)}) collective-permute-start(f32[3,1792]{1,0:T(4,128)} %slice.528), channel_id=1, source_target_pairs={{0,1},{1,2},{2,3},{3,4},{4,5},{5,6},{6,7},{7,8},{8,9},{9,10},{10,1... | collective-permute-start | bytes 64520 | tf_op jit(solution)/shard_map/ppermute | solution.py:32
  113.6 5.5 collective-permute-start.4
  116.5 13.7 %copy-start.59 = (f32[128,24]{0,1:T(8,128)}, f32[128,24]{0,1:T(8,128)S(1)}, u32[]{:S(2)}) copy-start(f32[128,24]{0,1:T(8,128)S(1)} %copy.154) | copy-start | bytes 36868
  120.5 27.2 %collective-permute-start.5 = (f32[2,2,2,2,1,1,24]{6,5,4,3,2,1,0:T(1,128)}, f32[2,2,2,2,1,1,24]{6,5,4,3,2,1,0:T(1,128)}, u32[]{:S(2)}, u32[]{:S(2)}) collective-permute-start(f32[2,2,2,2,1,1,24]{6,5,4,3,2,1,0:T(1,128)} %pad_maximum_fusion.16), channel_id=1, source_target_pairs={{0,1},{1,0},{2,3},{3,2},{4,5},{5,4},{6,7},{7,6},{8,9},{9,8},{10,11... | collective-permute-start | bytes 4616 | tf_op jit(solution)/shard_map/ppermute | solution.py:75
  130.2 65.5 %copy-start.4 = (f32[128,1536]{0,1:T(8,128)}, f32[128,1536]{0,1:T(8,128)S(1)}, u32[]{:S(2)}) copy-start(f32[128,1536]{0,1:T(8,128)S(1)} %copy.148) | copy-start | bytes 2359300
  134.1 9.4 %collective-permute-start.7 = (bf16[2,1,1,1,1,128,256]{6,5,4,3,2,1,0:T(8,128)(2,1)}, bf16[2,1,1,1,1,128,256]{6,5,4,3,2,1,0:T(8,128)(2,1)}, u32[]{:S(2)}, u32[]{:S(2)}) collective-permute-start(bf16[2,1,1,1,1,128,256]{6,5,4,3,2,1,0:T(8,128)(2,1)} %pad_maximum_fusion.14), channel_id=1, source_target_pairs={{0,8},{1,9},{2,10},{3,11},{4,12},{5,13},{6,14},{7,15},{8,0},{9,1},... | collective-permute-start | bytes 393224 | tf_op jit(solution)/shard_map/ppermute | solution.py:75
  136.2 29.3 %all-to-all-start = ((bf16[32,48,128]{2,1,0:T(8,128)(2,1)}), bf16[32,48,128]{2,1,0:T(8,128)(2,1)}, u32[]{:S(2)}, u32[]{:S(2)}) async-start(bf16[32,48,128]{2,1,0:T(8,128)(2,1)} %add_convert_fusion), calls=%async_computation | async-start | bytes 786432 | tf_op jit(solution)/shard_map/all_to_all | solution.py:125
  145.9 8.8 %collective-permute-start.8 = (bf16[2,2,1,1,1,128,256]{6,5,4,3,2,1,0:T(8,128)(2,1)}, bf16[2,2,1,1,1,128,256]{6,5,4,3,2,1,0:T(8,128)(2,1)}, u32[]{:S(2)}, u32[]{:S(2)}) collective-permute-start(bf16[2,2,1,1,1,128,256]{6,5,4,3,2,1,0:T(8,128)(2,1)} %pad_maximum_fusion.13), channel_id=1, source_target_pairs={{0,4},{1,5},{2,6},{3,7},{4,0},{5,1},{6,2},{7,3},{8,12},{9,13},{10,... | collective-permute-start | bytes 786440 | tf_op jit(solution)/shard_map/ppermute | solution.py:75
  157.3 33.6 %collective-permute-start.9 = (bf16[2,2,2,1,1,128,256]{6,5,4,3,2,1,0:T(8,128)(2,1)}, bf16[2,2,2,1,1,128,256]{6,5,4,3,2,1,0:T(8,128)(2,1)}, u32[]{:S(2)}, u32[]{:S(2)}) collective-permute-start(bf16[2,2,2,1,1,128,256]{6,5,4,3,2,1,0:T(8,128)(2,1)} %pad_maximum_fusion.8), channel_id=1, source_target_pairs={{0,2},{1,3},{2,0},{3,1},{4,6},{5,7},{6,4},{7,5},{8,10},{9,11},{10,... | collective-permute-start | bytes 1572872 | tf_op jit(solution)/shard_map/ppermute | solution.py:75
  169.9 24.2 %all-to-all-start.1 = ((bf16[32,48,128]{2,1,0:T(8,128)(2,1)}), bf16[32,48,128]{2,1,0:T(8,128)(2,1)}, u32[]{:S(2)}, u32[]{:S(2)}) async-start(bf16[32,48,128]{2,1,0:T(8,128)(2,1)} %carry.2), calls=%async_computation.1 | async-start | bytes 786432 | tf_op jit(solution)/shard_map/all_to_all | solution.py:131
  194.1 9.6 %collective-permute-start.10 = (bf16[2,2,2,2,1,128,256]{6,5,4,3,2,1,0:T(8,128)(2,1)}, bf16[2,2,2,2,1,128,256]{6,5,4,3,2,1,0:T(8,128)(2,1)}, u32[]{:S(2)}, u32[]{:S(2)}) collective-permute-start(bf16[2,2,2,2,1,128,256]{6,5,4,3,2,1,0:T(8,128)(2,1)} %pad_maximum_fusion.2), channel_id=1, source_target_pairs={{0,1},{1,0},{2,3},{3,2},{4,5},{5,4},{6,7},{7,6},{8,9},{9,8},{10,11... | collective-permute-start | bytes 3145736 | tf_op jit(solution)/shard_map/ppermute | solution.py:75
  276.1 9.8 %copy-start.108 = (bf16[1024,8192]{1,0:T(8,128)(2,1)S(1)}, bf16[1024,8192]{1,0:T(8,128)(2,1)}, u32[]{:S(2)}) copy-start(bf16[1024,8192]{1,0:T(8,128)(2,1)} %all-gather.5.cloned.1.call-done) | copy-start | bytes 50331652
  280.2 11.4 %copy-start.31 = (f32[128,1024]{1,0:T(8,128)}, f32[128,1024]{1,0:T(8,128)S(1)}, u32[]{:S(2)}) copy-start(f32[128,1024]{1,0:T(8,128)S(1)} %get-tuple-element.999) | copy-start | bytes 1572868
  280.2 11.4 %copy-start.101 = (f32[128]{0:T(128)}, f32[128]{0:T(128)S(1)}, u32[]{:S(2)}) copy-start(f32[128]{0:T(128)S(1)} %add_rsqrt_fusion) | copy-start | bytes 1540
  297.7 10.0 %copy-start.16 = (f32[128,1536]{1,0:T(8,128)S(1)}, f32[128,1536]{1,0:T(8,128)}, u32[]{:S(2)}) copy-start(f32[128,1536]{1,0:T(8,128)} %get-tuple-element.875) | copy-start | bytes 2359300
  297.7 10.0 %copy-start.29 = (f32[128,1536]{1,0:T(8,128)S(1)}, f32[128,1536]{1,0:T(8,128)}, u32[]{:S(2)}) copy-start(f32[128,1536]{1,0:T(8,128)} %copy.162) | copy-start | bytes 2359300
  301.8 98.1 %all-to-all-start.2 = ((bf16[32,48,128]{2,1,0:T(8,128)(2,1)}), bf16[32,48,128]{2,1,0:T(8,128)(2,1)}, u32[]{:S(2)}, u32[]{:S(2)}) async-start(bf16[32,48,128]{2,1,0:T(8,128)(2,1)} %bitcast.51), calls=%async_computation.2 | async-start | bytes 786432 | tf_op jit(solution)/shard_map/all_to_all | solution.py:125
  386.5 25.9 %collective-permute-start.12 = (bf16[2,2,2,2,128,256]{5,4,0,1,2,3:T(8,128)(2,1)}, bf16[2,2,2,2,128,256]{5,4,0,1,2,3:T(8,128)(2,1)}, u32[]{:S(2)}, u32[]{:S(2)}) collective-permute-start(bf16[2,2,2,2,128,256]{5,4,0,1,2,3:T(8,128)(2,1)} %fusion.77), channel_id=1, source_target_pairs={{0,1},{1,0},{2,3},{3,2},{4,5},{5,4},{6,7},{7,6},{8,9},{9,8},{10,11... | collective-permute-start | bytes 3145736 | tf_op jit(solution)/shard_map/ppermute | solution.py:75
  387.9 10.3 %copy-start.28 = (f32[128,1536]{0,1:T(8,128)S(1)}, f32[128,1536]{0,1:T(8,128)}, u32[]{:S(2)}) copy-start(f32[128,1536]{0,1:T(8,128)} %copy.163) | copy-start | bytes 2359300
  404.3 19.0 %all-to-all-start.3 = ((bf16[32,48,128]{2,1,0:T(8,128)(2,1)}), bf16[32,48,128]{2,1,0:T(8,128)(2,1)S(1)}, u32[]{:S(2)}, u32[]{:S(2)}) async-start(bf16[32,48,128]{2,1,0:T(8,128)(2,1)} %carry.3), calls=%async_computation.3 | async-start | bytes 786432 | tf_op jit(solution)/shard_map/all_to_all | solution.py:131
  410.0 159.3 %reduce-scatter.3.cloned.1.call-start = ((), (), s32[]{:S(2)}) async-start(), calls=%async_computation.8 | async-start | bytes 8921088 | tf_op jit(solution)/shard_map/reduce_scatter | solution.py:569
  416.0 9.2 %copy-start.90 = (f32[24,128]{1,0:T(8,128)S(1)}, f32[24,128]{1,0:T(8,128)}, u32[]{:S(2)}) copy-start(f32[24,128]{1,0:T(8,128)} %copy.150) | copy-start | bytes 36868
  416.0 9.2 %copy-start.110 = (f32[24]{0:T(128)S(1)}, f32[24]{0:T(128)}, u32[]{:S(2)}) copy-start(f32[24]{0:T(128)} %param.33) | copy-start | bytes 292
  416.8 26.3 %collective-permute-start.13 = (bf16[2,2,2,128,256]{4,3,0,1,2:T(8,128)(2,1)}, bf16[2,2,2,128,256]{4,3,0,1,2:T(8,128)(2,1)}, u32[]{:S(2)}, u32[]{:S(2)}) collective-permute-start(bf16[2,2,2,128,256]{4,3,0,1,2:T(8,128)(2,1)} %fusion.109), channel_id=1, source_target_pairs={{0,2},{1,3},{2,0},{3,1},{4,6},{5,7},{6,4},{7,5},{8,10},{9,11},{10,... | collective-permute-start | bytes 1572872 | tf_op jit(solution)/shard_map/ppermute | solution.py:75
  436.2 25.6 %collective-permute-start.11 = (f32[3,1792]{1,0:T(4,128)}, f32[3,1792]{1,0:T(4,128)}, u32[]{:S(2)}, u32[]{:S(2)}) collective-permute-start(f32[3,1792]{1,0:T(4,128)} %pad_add_fusion.1), channel_id=1, source_target_pairs={{1,0},{2,1},{3,2},{4,3},{5,4},{6,5},{7,6},{8,7},{9,8},{10,9},{11,1... | collective-permute-start | bytes 64520 | tf_op jit(solution)/shard_map/ppermute | solution.py:32
  446.4 9.5 %collective-permute-start.14 = (bf16[2,2,128,256]{3,2,0,1:T(8,128)(2,1)}, bf16[2,2,128,256]{3,2,0,1:T(8,128)(2,1)S(1)}, u32[]{:S(2)}, u32[]{:S(2)}) collective-permute-start(bf16[2,2,128,256]{3,2,0,1:T(8,128)(2,1)} %fusion.114), channel_id=1, source_target_pairs={{0,4},{1,5},{2,6},{3,7},{4,0},{5,1},{6,2},{7,3},{8,12},{9,13},{10,... | collective-permute-start | bytes 786440 | tf_op jit(solution)/shard_map/ppermute | solution.py:75
  452.9 14.4 %copy-start.41 = (bf16[128,1536]{1,0:T(8,128)(2,1)S(1)}, bf16[128,1536]{1,0:T(8,128)(2,1)}, u32[]{:S(2)}) copy-start(bf16[128,1536]{1,0:T(8,128)(2,1)} %get-tuple-element.889) | copy-start | bytes 1179652
  456.0 5.2 collective-permute-start.15
  461.3 5.9 collective-permute-start.16
  474.3 206.8 %reduce-scatter.5.cloned.1.call-start = ((), (), s32[]{:S(2)}) async-start(), calls=%async_computation.9 | async-start | bytes 17301504 | tf_op jit(solution)/shard_map/reduce_scatter | solution.py:500
  (106 other events, 353.1 us)
Sparse Core Ops, SparseCore 0:
  12.1 65.9 all-gather.2
  80.3 116.9 all-gather.4
  474.4 94.9 reduce-scatter.2
  571.5 109.5 reduce-scatter.4

commit v2 on v1

--- a/solution.py
+++ b/solution.py
@@ -103,7 +103,9 @@
         high = ((here & bit) != 0).astype(jnp.int32)
         kept = lax.dynamic_index_in_dim(block, high, axis=place, keepdims=False)
         sent = lax.dynamic_index_in_dim(block, 1 - high, axis=place, keepdims=False)
-        block = kept + swapped(sent.astype(jnp.bfloat16), axis, bit).astype(jnp.float32)
+        block = kept.astype(jnp.float32) + swapped(sent.astype(jnp.bfloat16), axis, bit).astype(
+            jnp.float32
+        )
     return block.reshape((rows,) + total.shape[1:])
 
 
@@ -227,124 +229,154 @@
     return (local_out, final_state, reach, ssm_c.reshape(row_count, NS))
 
 
-def over_keys(update, initial_carry, key_rows_all, row_limit, query_rows, doc_span):
-    count_all = key_rows_all.shape[0]
-    block_size = math.gcd(count_all, 512)
-    blocks = count_all // block_size
-    visits = min(blocks, (doc_span + query_rows - 1) // block_size + 2)
-    lowest = (row_limit - query_rows - doc_span + 1) // block_size
-    begin = jnp.clip(lowest, 0, blocks - visits)
-
-    def visit(number, current_block):
-        offset = (begin + number) * block_size
-        return update(
-            current_block, lax.dynamic_slice_in_dim(key_rows_all, offset, block_size, 0), offset
-        )
-
-    return lax.fori_loop(0, visits, visit, initial_carry)
-
-
-def block_scores(query_quadruple, positions, seg_rows, doc_ids, block_forward_pass, key_start):
-    rows_per_block = block_forward_pass.shape[0]
-    key_columns = KEYVALUE_HEADS * HEAD_SIZE
-    key_row_block = block_forward_pass[:, :key_columns].reshape(
-        rows_per_block, KEYVALUE_HEADS, HEAD_SIZE
-    )
-    value_row_block = block_forward_pass[:, key_columns:].reshape(
-        rows_per_block, KEYVALUE_HEADS, HEAD_SIZE
-    )
-    key_pos = key_start + jnp.arange(rows_per_block, dtype=jnp.int32)
-    key_seg = lax.dynamic_slice_in_dim(doc_ids, key_start, rows_per_block)
-    visible = (key_pos[None, :] <= positions[:, None]) & (key_seg[None, :] == seg_rows[:, None])
-    attention_scores = jnp.einsum(
-        "uoiy,woy->oiuw", query_quadruple, key_row_block, preferred_element_type=jnp.float32
-    ) * HEAD_SIZE ** (-0.5)
-    return (key_row_block, value_row_block, visible[None, None], attention_scores)
-
-
-def stats_step(
-    query_quadruple, positions, seg_rows, doc_ids, denominator, block_forward_pass, key_start
+def stacked_heads(values, kv):
+    group = QUERY_HEADS // KEYVALUE_HEADS
+    heads = range(kv * group, (kv + 1) * group)
+    return jnp.concatenate([values[:, h * HEAD_SIZE : (h + 1) * HEAD_SIZE] for h in heads], axis=0)
+
+
+def visible_pairs(number, block, first_row, seg_rows, seg_all_ref, rows):
+    group = QUERY_HEADS // KEYVALUE_HEADS
+    row_pos = first_row + lax.broadcasted_iota(jnp.int32, (rows, block), 0)
+    key_pos = number * block + lax.broadcasted_iota(jnp.int32, (rows, block), 1)
+    visible = (key_pos <= row_pos) & (seg_all_ref[pl.ds(number, 1), :] == seg_rows)
+    bias = jnp.where(visible, 0.0, NEG)
+    return jnp.concatenate([bias] * group, axis=0)
+
+
+def attention_forward_kernel(
+    bounds_ref, query_ref, keyval_ref, seg_row_ref, seg_all_ref, out_ref, total_ref
 ):
-    key_row_block, value_row_block, visible, attention_scores = block_scores(
-        query_quadruple, positions, seg_rows, doc_ids, block_forward_pass, key_start
-    )
-    return denominator + jnp.sum(jnp.exp(jnp.where(visible, attention_scores, NEG)), axis=3)
-
-
-def values_step(
-    query_quadruple,
-    positions,
-    seg_rows,
-    doc_ids,
-    log_total,
-    current_block,
-    block_forward_pass,
-    key_start,
+    rows, block = (seg_row_ref.shape[0], seg_all_ref.shape[1])
+    height = rows * (QUERY_HEADS // KEYVALUE_HEADS)
+    queries = [stacked_heads(query_ref[...], kv) for kv in range(KEYVALUE_HEADS)]
+    seg_rows = seg_row_ref[...]
+
+    def visit(number, carried):
+        at = pl.multiple_of(number * block, block)
+        bias = visible_pairs(number, block, bounds_ref[2], seg_rows, seg_all_ref, rows)
+        keyval = keyval_ref[pl.ds(at, block), :]
+        new = []
+        for kv in range(KEYVALUE_HEADS):
+            most, total, mixed = carried[kv]
+            key = keyval[:, kv * HEAD_SIZE : (kv + 1) * HEAD_SIZE]
+            value_at = (KEYVALUE_HEADS + kv) * HEAD_SIZE
+            value = keyval[:, value_at : value_at + HEAD_SIZE]
+            scores = matmul_nt(queries[kv], key) * HEAD_SIZE ** (-0.5) + bias
+            new_most = jnp.maximum(most, jnp.max(scores, axis=1, keepdims=True))
+            shrink = jnp.exp(most - new_most)
+            weights = jnp.exp(scores - new_most)
+            total = total * shrink + jnp.sum(weights, axis=1, keepdims=True)
+            mixed = mixed * shrink + matmul(weights.astype(jnp.bfloat16), value)
+            new.append((new_most, total, mixed))
+        return tuple(new)
+
+    start = (
+        jnp.full((height, 1), NEG, jnp.float32),
+        jnp.zeros((height, 1), jnp.float32),
+        jnp.zeros((height, HEAD_SIZE), jnp.float32),
+    )
+    done = lax.fori_loop(bounds_ref[0], bounds_ref[1], visit, (start,) * KEYVALUE_HEADS)
+    for kv in range(KEYVALUE_HEADS):
+        most, total, mixed = done[kv]
+        mixed = mixed / total
+        total_ref[kv] = most + jnp.log(total)
+        for g in range(height // rows):
+            at = (kv * (height // rows) + g) * HEAD_SIZE
+            out_ref[:, at : at + HEAD_SIZE] = mixed[g * rows : (g + 1) * rows]
+
+
+def attention_backward_kernel(
+    bounds_ref,
+    query_ref,
+    keyval_ref,
+    seg_row_ref,
+    seg_all_ref,
+    total_ref,
+    mid_ref,
+    grad_ref,
+    query_grad_ref,
+    keyval_grad_ref,
 ):
-    key_row_block, value_row_block, visible, attention_scores = block_scores(
-        query_quadruple, positions, seg_rows, doc_ids, block_forward_pass, key_start
-    )
-    attention_weights_soft = jnp.exp(
-        jnp.where(visible, attention_scores - log_total[..., None], NEG)
-    ).astype(jnp.bfloat16)
-    return current_block + jnp.einsum(
-        "zilr,rzq->lziq",
-        attention_weights_soft,
-        value_row_block,
-        preferred_element_type=jnp.float32,
-    )
-
-
-def back_step(
-    query_quadruple,
-    positions,
-    seg_rows,
-    doc_ids,
-    log_total,
-    gradient_quadruple,
-    row_delta,
-    current_block,
-    block_forward_pass,
-    key_start,
-):
-    query_accumulator, keyvalue_accumulator = current_block
-    key_row_block, value_row_block, visible, attention_scores = block_scores(
-        query_quadruple, positions, seg_rows, doc_ids, block_forward_pass, key_start
-    )
-    attention_weights_soft = jnp.exp(
-        jnp.where(visible, attention_scores - log_total[..., None], NEG)
-    )
-    probability_gradient = jnp.einsum(
-        "uoiy,woy->oiuw", gradient_quadruple, value_row_block, preferred_element_type=jnp.float32
-    )
-    score_gradient = (
-        attention_weights_soft * (probability_gradient - row_delta[..., None])
-    ).astype(jnp.bfloat16)
-    query_accumulator = query_accumulator + jnp.einsum(
-        "zilr,rzq->lziq", score_gradient, key_row_block, preferred_element_type=jnp.float32
-    )
-    key_portion = jnp.einsum(
-        "luzn,zlup->nlp", score_gradient, query_quadruple, preferred_element_type=jnp.float32
-    ) * HEAD_SIZE ** (-0.5)
-    value_portion = jnp.einsum(
-        "luzn,zlup->nlp",
-        attention_weights_soft.astype(jnp.bfloat16),
-        gradient_quadruple,
-        preferred_element_type=jnp.float32,
-    )
-    rows_per_block = block_forward_pass.shape[0]
-    block_gradient_out = jnp.concatenate(
-        [
-            key_portion.reshape(rows_per_block, KEYVALUE_HEADS * HEAD_SIZE),
-            value_portion.reshape(rows_per_block, KEYVALUE_HEADS * HEAD_SIZE),
-        ],
-        axis=1,
-    )
-    old_rows = lax.dynamic_slice_in_dim(keyvalue_accumulator, key_start, rows_per_block, 0)
-    keyvalue_accumulator = lax.dynamic_update_slice_in_dim(
-        keyvalue_accumulator, old_rows + block_gradient_out, key_start, 0
-    )
-    return (query_accumulator, keyvalue_accumulator)
+    rows, block = (seg_row_ref.shape[0], seg_all_ref.shape[1])
+    height = rows * (QUERY_HEADS // KEYVALUE_HEADS)
+    heads = range(KEYVALUE_HEADS)
+    queries = [stacked_heads(query_ref[...], kv) for kv in heads]
+    grads = [stacked_heads(grad_ref[...], kv) for kv in heads]
+    deltas = [
+        jnp.sum(grads[kv] * stacked_heads(mid_ref[...], kv), axis=1, keepdims=True) for kv in heads
+    ]
+    grads = [part.astype(jnp.bfloat16) for part in grads]
+    totals = [total_ref[kv] for kv in heads]
+    seg_rows = seg_row_ref[...]
+    keyval_grad_ref[...] = jnp.zeros(keyval_grad_ref.shape, keyval_grad_ref.dtype)
+
+    def visit(number, carried):
+        at = pl.multiple_of(number * block, block)
+        bias = visible_pairs(number, block, bounds_ref[2], seg_rows, seg_all_ref, rows)
+        keyval = keyval_ref[pl.ds(at, block), :]
+        new = []
+        for kv in heads:
+            key = keyval[:, kv * HEAD_SIZE : (kv + 1) * HEAD_SIZE]
+            value_at = (KEYVALUE_HEADS + kv) * HEAD_SIZE
+            value = keyval[:, value_at : value_at + HEAD_SIZE]
+            scores = matmul_nt(queries[kv], key) * HEAD_SIZE ** (-0.5) + bias
+            weights = jnp.exp(scores - totals[kv])
+            score_grad = (weights * (matmul_nt(grads[kv], value) - deltas[kv])).astype(jnp.bfloat16)
+            new.append(carried[kv] + matmul(score_grad, key))
+            key_grad = matmul_tn(score_grad, queries[kv]) * HEAD_SIZE ** (-0.5)
+            value_grad = matmul_tn(weights.astype(jnp.bfloat16), grads[kv])
+            low = keyval_grad_ref.dtype
+            keyval_grad_ref[pl.ds(at, block), kv * HEAD_SIZE : (kv + 1) * HEAD_SIZE] = (
+                key_grad.astype(low)
+            )
+            keyval_grad_ref[pl.ds(at, block), value_at : value_at + HEAD_SIZE] = value_grad.astype(
+                low
+            )
+        return tuple(new)
+
+    start = jnp.zeros((height, HEAD_SIZE), jnp.float32)
+    done = lax.fori_loop(bounds_ref[0], bounds_ref[1], visit, (start,) * KEYVALUE_HEADS)
+    for kv in heads:
+        for g in range(height // rows):
+            at = (kv * (height // rows) + g) * HEAD_SIZE
+            query_grad_ref[:, at : at + HEAD_SIZE] = (
+                done[kv][g * rows : (g + 1) * rows] * HEAD_SIZE ** (-0.5)
+            ).astype(query_grad_ref.dtype)
+
+
+def in_smem():
+    return pl.BlockSpec(memory_space=pltpu.SMEM)
+
+
+def in_vmem():
+    return pl.BlockSpec(memory_space=pltpu.VMEM)
+
+
+def attention_forward(bounds, query, keyval_all, seg_rows, seg_all):
+    rows = query.shape[0]
+    height = rows * (QUERY_HEADS // KEYVALUE_HEADS)
+    return pl.pallas_call(
+        attention_forward_kernel,
+        in_specs=[in_smem()] + [in_vmem()] * 4,
+        out_shape=(
+            jax.ShapeDtypeStruct(query.shape, jnp.float32),
+            jax.ShapeDtypeStruct((KEYVALUE_HEADS, height, 1), jnp.float32),
+        ),
+        name="attend",
+    )(bounds, query, keyval_all, seg_rows, seg_all)
+
+
+def attention_backward(bounds, query, keyval_all, seg_rows, seg_all, totals, mid, grad):
+    return pl.pallas_call(
+        attention_backward_kernel,
+        in_specs=[in_smem()] + [in_vmem()] * 7,
+        out_shape=(
+            jax.ShapeDtypeStruct(query.shape, jnp.bfloat16),
+            jax.ShapeDtypeStruct(keyval_all.shape, jnp.bfloat16),
+        ),
+        name="attend_back",
+    )(bounds, query, keyval_all, seg_rows, seg_all, totals, mid, grad)
 
 
 def local(
@@ -371,9 +403,7 @@
     devices = lax.axis_size("seq")
     here = lax.axis_index("seq")
     sequence_total = local_row_count * devices
-    doc_span = sequence_total // 2 + local_row_count
     first_row = here * local_row_count
-    query_group_width = QUERY_HEADS // KEYVALUE_HEADS
     query_cols = QUERY_HEADS * HEAD_SIZE
     keyval_cols = 2 * KEYVALUE_HEADS * HEAD_SIZE
     feature_rows = in_weight.shape[0]
@@ -444,31 +474,17 @@
     cross_base = jnp.einsum("tn,hpn->thp", c_here, state_in, precision=HIGH)
     ssm_out = (local_out + cross_base * reach.T[:, :, None]).reshape(local_row_count, DSSM)
     gated = (ssm_out * jax.nn.silu(gate_mix)).astype(jnp.bfloat16)
-    query_quadruple = query_reduced.reshape(
-        local_row_count, KEYVALUE_HEADS, query_group_width, HEAD_SIZE
-    )
-    positions = first_row + jnp.arange(local_row_count, dtype=jnp.int32)
-    row_limit = first_row + local_row_count
-    statistics_initial = jnp.zeros(
-        (KEYVALUE_HEADS, query_group_width, local_row_count), jnp.float32
-    )
-    middle_initial = jnp.zeros(
-        (local_row_count, KEYVALUE_HEADS, query_group_width, HEAD_SIZE), jnp.float32
-    )
-    stats_update = partial(stats_step, query_quadruple, positions, seg_here, doc_ids)
-    denominator = over_keys(
-        stats_update, statistics_initial, keyval_all, row_limit, local_row_count, doc_span
-    )
-    log_total = jnp.log(denominator)
-    attention_middle = over_keys(
-        partial(values_step, query_quadruple, positions, seg_here, doc_ids, log_total),
-        middle_initial,
-        keyval_all,
-        row_limit,
-        local_row_count,
-        doc_span,
-    )
-    attn_low = attention_middle.reshape(local_row_count, query_cols).astype(jnp.bfloat16)
+    key_block = math.gcd(sequence_total, 256)
+    first_key = jnp.sum((doc_ids < seg_here[0]).astype(jnp.int32))
+    bounds = jnp.stack(
+        [first_key // key_block, (first_row + local_row_count - 1) // key_block + 1, first_row]
+    ).astype(jnp.int32)
+    seg_column = seg_here[:, None]
+    seg_all = doc_ids.reshape(sequence_total // key_block, key_block)
+    attention_middle, log_total = attention_forward(
+        bounds, query_reduced, keyval_all, seg_column, seg_all
+    )
+    attn_low = attention_middle.astype(jnp.bfloat16)
     mixed_low = jnp.concatenate([gated, attn_low], axis=1)
     resid = layer_input + matmul_nt(mixed_low, outward_full)
     scale_two = rms_scale(resid)
@@ -497,42 +513,23 @@
         ],
         axis=1,
     )
+    mixed_grad = matmul(resid_low, outward_full)
+    second_grad, mixed_grad = lax.optimization_barrier((second_grad, mixed_grad))
     second_share = lax.psum_scatter(
         second_grad, "seq", scatter_dimension=0, tiled=True, axis_index_groups=[order]
     ).astype(jnp.float32)
-    mixed_grad = matmul(resid_low, outward_full)
     gated_grad = mixed_grad[:, :DSSM]
-    attention_gradient = mixed_grad[:, DSSM:]
-    gradient_quadruple = attention_gradient.astype(jnp.bfloat16).reshape(
-        local_row_count, KEYVALUE_HEADS, query_group_width, HEAD_SIZE
-    )
-    row_delta = jnp.sum(
-        attention_gradient.reshape(local_row_count, KEYVALUE_HEADS, query_group_width, HEAD_SIZE)
-        * attention_middle,
-        axis=3,
-    ).transpose(1, 2, 0)
-    back_init = (
-        jnp.zeros((local_row_count, KEYVALUE_HEADS, query_group_width, HEAD_SIZE), jnp.float32),
-        jnp.zeros((sequence_total, keyval_cols), jnp.float32),
-    )
-    back_update = partial(
-        back_step,
-        query_quadruple,
-        positions,
-        seg_here,
-        doc_ids,
+    query_grad_low, keyval_partial = attention_backward(
+        bounds,
+        query_reduced,
+        keyval_all,
+        seg_column,
+        seg_all,
         log_total,
-        gradient_quadruple,
-        row_delta,
-    )
-    query_accumulator, keyvalue_accumulator = over_keys(
-        back_update, back_init, keyval_all, row_limit, local_row_count, doc_span
-    )
-    keyval_here = scattered_by_halving(keyvalue_accumulator, "seq")
-    query_grad_low = (
-        query_accumulator.reshape(local_row_count, query_cols) * HEAD_SIZE ** (-0.5)
-    ).astype(jnp.bfloat16)
-    keyval_grad_low = keyval_here.astype(jnp.bfloat16)
+        attention_middle,
+        mixed_grad[:, DSSM:],
+    )
+    keyval_grad_low = scattered_by_halving(keyval_partial, "seq").astype(jnp.bfloat16)
     ssm_grad = gated_grad * jax.nn.silu(gate_mix)
     gate_mix_grad = gated_grad * ssm_out * silu_slope(gate_mix)
     ssm_grad_three = ssm_grad.reshape(local_row_count, HM, HP)

time: 704 us -> 627 us (0.89)
  local copies, waits for them, and re-layouts: 144 us -> 83.3 us
  matrix products: 124 us -> 85.7 us
  starting transfers between devices: 45.3 us -> 60.6 us
  other arithmetic: 82.1 us -> 69.3 us
  waiting for transfers between devices: 232 us -> 243 us
  Pallas kernels: 8.67 us -> 18 us
    dot_general x42 -> x0, matrix products: 48.2 us -> none  [the longest x6 16.1 us: values_step(): jnp.einsum('zilr,rzq->lziq', attention_weights_soft, value_row_block, pre...]
    dynamic_slice x30 -> x2, local copies, waits for them, and re-layouts: 37.2 us -> 5.58 us  [the longest x1 3.2 us: scattered_by_halving(): kept = lax.dynamic_index_in_dim(block, high, axis=place, keepdims=False)]
    slice x22 -> x1, local copies, waits for them, and re-layouts: 21.7 us -> 0.72 us  [local(): mixed_grad[:, DSSM:]]
    and x18 -> x0, other arithmetic: 15.4 us -> none  [block_scores(): (key_pos[None, :] <= positions[:, None]) & (key_seg[None, :] == seg_rows[...]
    reduce_scatter x1, waiting for transfers between devices: 22.4 us -> 36.5 us  [local(): lax.psum_scatter(matmul_tn(normed_one, first_grad_low).astype(jnp.bfloat1...]
    all_to_all x2, starting transfers between devices: 9.73 us -> 19.9 us  [carried_states(): back = lax.all_to_all(folded, axis, 0, 0, tiled=True)]
    pallas_call x0 -> x2, Pallas kernels: none -> 9.35 us  [the longest x1 5.05 us: attention_backward(): pl.pallas_call(attention_backward_kernel, in_specs=[in_smem()] + [in_vmem...]
    all_to_all x2, starting transfers between devices: 9.24 us -> 16.9 us  [carried_states(): fresh = lax.all_to_all(sent, axis, 0, 0, tiled=True)]
  transfers between devices with their start and end apart: 25 -> 25, of which waited for: 12 -> 12; matrix products, arithmetic and copies ran while one was open for 43% -> 27% of each run, Pallas kernels for 1% -> 3%
where the time goes in v2:
time: 627 us; the launch traced here: 618 us
  waiting for transfers between devices  243 us (39%)
  matrix products  85.7 us (14%)
  local copies, waits for them, and re-layouts  83.3 us (13%)
  other arithmetic  69.3 us (11%)
  starting transfers between devices  60.6 us (10%)
  blocking collectives  39.5 us (6%)
  between operations  18.7 us (3%)
  Pallas kernels  18 us (3%)
    reduce_scatter x1, waiting for transfers between devices, local(): lax.psum_scatter(second_grad, 'seq', scatter_dimension=0, tiled=True, axi...  107 us
    all_gather x1, waiting for transfers between devices, local(): lax.all_gather(first_pack, 'seq', axis=0, tiled=True, axis_index_groups=[...  63.3 us
    psum x1, blocking collectives, local(): lax.psum(jnp.concatenate([part.reshape(-1) for part in small]), 'seq')  39.5 us
    reduce_scatter x1, waiting for transfers between devices, local(): lax.psum_scatter(matmul_tn(normed_one, first_grad_low).astype(jnp.bfloat1...  36.5 us
    ppermute x15, waiting for transfers between devices, swapped(): return lax.ppermute(values, axis, [(i, i ^ bit) for i in range(size)])  32.2 us
    dot_general x4, matrix products, matmul_nt(): lax.dot_general(left, right, (((1,), (1,)), ((), ())), preferred_element_...  21.3 us
    all_to_all x2, starting transfers between devices, carried_states(): back = lax.all_to_all(folded, axis, 0, 0, tiled=True)  19.9 us
    ppermute x15, starting transfers between devices, swapped(): return lax.ppermute(values, axis, [(i, i ^ bit) for i in range(size)])  18.9 us
  transfers between devices with their start and end apart: 25, of which 12 were waited for; matrix products, arithmetic and copies ran while one was open for 27% of the time, Pallas kernels for 3%

profile of v2, /device:TPU:0, one launch (start us, length us, event | category | flops | bytes accessed | tf_op | source)
XLA Modules:
  0.0 617.8 jit_solution(4293833725243334448)
XLA Ops:
  14.9 63.3 %all-gather.3.cloned.1.call-done = bf16[1024,4224]{1,0:T(8,128)(2,1)} async-done(((bf16[32,4224]{1,0:T(8,128)(2,1)}), bf16[1024,4224]{1,0:T(8,128)(2,1)}) %all-gather.3.cloned.1.call-update) | async-done | bytes 8650768 | tf_op jit(solution)/shard_map/all_gather | solution.py:430
  92.6 6.0 fusion.149
  99.2 2.8 collective-permute-start
  103.7 3.6 collective-permute-done.1
  123.6 4.2 fusion.58
  137.0 4.3 all-to-all-start
  141.3 3.0 collective-permute-done.7
  151.4 4.7 collective-permute-done.8
  158.8 6.4 %collective-permute-start.9 = (bf16[2,2,2,1,1,128,256]{6,5,4,3,2,1,0:T(8,128)(2,1)}, bf16[2,2,2,1,1,128,256]{6,5,4,3,2,1,0:T(8,128)(2,1)}, u32[]{:S(2)}, u32[]{:S(2)}) collective-permute-start(bf16[2,2,2,1,1,128,256]{6,5,4,3,2,1,0:T(8,128)(2,1)} %pad_maximum_fusion.8), channel_id=1, source_target_pairs={{0,2},{1,3},{2,0},{3,1},{4,6},{5,7},{6,4},{7,5},{8,10},{9,11},{10,... | collective-permute-start | bytes 1572872 | tf_op jit(solution)/shard_map/ppermute | solution.py:75
  168.6 4.3 carry.2
  173.0 4.1 all-to-all-start.1
  178.8 2.5 convolution_bitcast_fusion
  181.3 11.4 %collective-permute-done.9 = bf16[2,2,2,1,1,128,256]{6,5,4,3,2,1,0:T(8,128)(2,1)} collective-permute-done((bf16[2,2,2,1,1,128,256]{6,5,4,3,2,1,0:T(8,128)(2,1)}, bf16[2,2,2,1,1,128,256]{6,5,4,3,2,1,0:T(8,128)(2,1)}, u32[]{:S(2)}, u32[]{:S(2)}) %collective-permute-start.9) | collective-permute-done | bytes 524320 | tf_op jit(solution)/shard_map/ppermute | solution.py:75
  197.4 5.7 fusion.37
  203.1 2.3 copy.122
  210.5 4.3 attend.1
  216.4 4.0 multiply_reduce_fusion.14
  220.4 4.9 fusion.2
  225.3 3.4 multiply_convert_fusion.1
  228.8 2.4 convolution_convert_fusion.1
  231.2 7.0 %multiply_reduce_fusion.10 = (f32[1024]{0:T(1024)}, f32[128]{0:T(128)S(1)}, f32[128,1024]{1,0:T(8,128)S(1)}) fusion(f32[128,1024]{1,0:T(8,128)S(1)} %get-tuple-element.233, f32[128]{0:T(128)S(1)} %add_rsqrt_fusion, f32[1024]{0:T(1024)S(1)} %copy-done.45, bf16[1024,8192]{1,0:T(8,128)(2,1)} %all-gather.5.cloned.1.call-done, ...), kind=kOutput, calls=%fused_computation.126 | convolution fusion | flops 1076624256 | bytes 10494976 | tf_op jit(solution)/shard_map/dot_general | solution.py:148
  241.8 7.1 %pad_maximum_fusion = bf16[1024,8192]{1,0:T(8,128)(2,1)} fusion(bf16[1024,2048]{1,0:T(8,128)(2,1)S(1)} %convolution_convert_fusion.2, bf16[1024,2048]{1,0:T(8,128)(2,1)S(1)} %convolution_convert_fusion.3, bf16[1024,4096]{1,0:T(8,128)(2,1)S(1)} %convolution_convert_fusion.1), kind=kLoop, calls=%fused_computation | loop fusion | flops 50331648 | bytes 33554432 | tf_op jit(solution)/shard_map/concatenate | solution.py:508
  248.9 3.2 fusion.8
  254.8 2.3 copy.127
  261.8 2.3 convolution_convert_fusion.4
  264.1 12.6 %all-to-all-start.2 = ((bf16[32,48,128]{2,1,0:T(8,128)(2,1)}), bf16[32,48,128]{2,1,0:T(8,128)(2,1)}, u32[]{:S(2)}, u32[]{:S(2)}) async-start(bf16[32,48,128]{2,1,0:T(8,128)(2,1)} %bitcast.275), calls=%async_computation.2 | async-start | bytes 786432 | tf_op jit(solution)/shard_map/all_to_all | solution.py:127
  276.7 5.1 attend_back.1
  281.8 3.2 constant_dynamic-slice_fusion.1
  286.0 2.3 copy.126
  293.9 2.4 copy.167
  296.4 4.4 fusion.60
  305.1 2.5 convolution_bitcast_fusion.2
  307.7 2.7 fusion.48
  310.3 4.3 carry.3
  314.6 15.8 %all-to-all-start.3 = ((bf16[32,48,128]{2,1,0:T(8,128)(2,1)}), bf16[32,48,128]{2,1,0:T(8,128)(2,1)}, u32[]{:S(2)}, u32[]{:S(2)}) async-start(bf16[32,48,128]{2,1,0:T(8,128)(2,1)} %carry.3), calls=%async_computation.3 | async-start | bytes 786432 | tf_op jit(solution)/shard_map/all_to_all | solution.py:133
  340.0 3.7 all-to-all-done.3
  345.9 2.4 fusion.47
  348.4 2.8 fusion.25
  364.5 3.7 multiply_reduce_fusion.4
  377.2 2.3 pad_add_fusion
  384.0 3.1 collective-permute-done.15
  388.7 3.7 collective-permute-done.16
  394.6 5.9 convolution_convert_fusion
  402.6 3.7 fusion.43
  407.9 6.7 %multiply_reduce_fusion.11 = (f32[1024]{0:T(1024)S(1)}, f32[128]{0:T(128)S(1)}, f32[128,1024]{1,0:T(8,128)S(1)}) fusion(f32[128,1024]{1,0:T(8,128)S(1)} %concatenate.87, f32[128]{0:T(128)S(1)} %copy-done.66, f32[1024]{0:T(1024)S(1)} %get-tuple-element.103, bf16[128,4224]{1,0:T(8,128)(2,1)S(1)} %concatenate.112, ...), kind=kOutput, calls=%fused_computation.127 | convolution fusion | flops 1108081536 | bytes 10789888 | tf_op jit(solution)/shard_map/dot_general | solution.py:148
  414.6 39.5 %psum.7 = f32[11080]{0:T(1024)S(1)} all-reduce(f32[11080]{0:T(1024)S(1)} %concatenate.114), channel_id=1, replica_groups=mesh['seq'=32] {'seq'}, use_global_device_ids=true, to_apply=%region_27.28 | all-reduce | flops 11080 | bytes 88640 | tf_op jit(solution)/shard_map/psum | solution.py:588
  458.6 36.5 %reduce-scatter.3.cloned.1.call-done = bf16[32,4224]{1,0:T(8,128)(2,1)} async-done(((bf16[1024,4224]{1,0:T(8,128)(2,1)}), bf16[32,4224]{1,0:T(8,128)(2,1)}) %reduce-scatter.3.cloned.1.call-update) | async-done | bytes 270352 | tf_op jit(solution)/shard_map/reduce_scatter | solution.py:566
  500.3 106.5 %reduce-scatter.5.cloned.1.call-done = bf16[32,8192]{1,0:T(8,128)(2,1)} async-done(((bf16[1024,8192]{1,0:T(8,128)(2,1)}), bf16[32,8192]{1,0:T(8,128)(2,1)}) %reduce-scatter.5.cloned.1.call-update) | async-done | bytes 524304 | tf_op jit(solution)/shard_map/reduce_scatter | solution.py:518
  (380 shorter events, 153.7 us)
Async XLA Ops:
  7.2 71.1 %copy-start.44 = (s32[4096]{0:T(1024)S(1)}, s32[4096]{0:T(1024)}, u32[]{:S(2)}) copy-start(s32[4096]{0:T(1024)} %param.20) | copy-start | bytes 49156
  7.2 78.2 %copy-start.31 = (f32[128,1024]{1,0:T(8,128)S(1)}, f32[128,1024]{1,0:T(8,128)}, u32[]{:S(2)}) copy-start(f32[128,1024]{1,0:T(8,128)} %param.18) | copy-start | bytes 1572868
  7.2 71.0 %all-gather.3.cloned.1.call-start = ((), (), s32[]{:S(2)}) async-start(), calls=%async_computation.6 | async-start | bytes 8921088 | tf_op jit(solution)/shard_map/all_gather | solution.py:430
  12.0 204.3 %all-gather.5.cloned.1.call-start = ((), (), s32[]{:S(2)}) async-start(), calls=%async_computation.7 | async-start | bytes 17301504 | tf_op jit(solution)/shard_map/all_gather | solution.py:434
  78.2 7.7 %copy-start.32 = (f32[128,1024]{1,0:T(8,128)S(1)}, f32[128,1024]{1,0:T(8,128)}, u32[]{:S(2)}) copy-start(f32[128,1024]{1,0:T(8,128)} %param.19) | copy-start | bytes 1572868
  79.6 32.0 %copy-start.75 = (pred[128]{0:T(512)(128)(4,1)}, pred[128]{0:T(512)(128)(4,1)S(1)}, u32[]{:S(2)}) copy-start(pred[128]{0:T(512)(128)(4,1)S(1)} %get-tuple-element.117) | copy-start | bytes 388
  88.5 13.4 %copy-start.82 = (f32[24]{0:T(128)}, f32[24]{0:T(128)S(1)}, u32[]{:S(2)}) copy-start(f32[24]{0:T(128)S(1)} %exponential_negate_fusion) | copy-start | bytes 292
  89.2 14.4 %copy-start.79 = (pred[128]{0:T(512)(128)(4,1)}, pred[128]{0:T(512)(128)(4,1)S(1)}, u32[]{:S(2)}) copy-start(pred[128]{0:T(512)(128)(4,1)S(1)} %broadcast_compare_fusion) | copy-start | bytes 388
  89.2 9.3 %copy-start.65 = (f32[128]{0:T(128)}, f32[128]{0:T(128)S(1)}, u32[]{:S(2)}) copy-start(f32[128]{0:T(128)S(1)} %add_rsqrt_fusion.1) | copy-start | bytes 1540
  92.6 9.4 %copy-start.71 = (f32[24]{0:T(128)S(1)}, f32[24]{0:T(128)}, u32[]{:S(2)}) copy-start(f32[24]{0:T(128)} %param.25) | copy-start | bytes 292
  99.2 24.5 %collective-permute-start = (f32[3,1792]{1,0:T(4,128)}, f32[3,1792]{1,0:T(4,128)}, u32[]{:S(2)}, u32[]{:S(2)}) collective-permute-start(f32[3,1792]{1,0:T(4,128)} %slice.492), channel_id=1, source_target_pairs={{0,1},{1,2},{2,3},{3,4},{4,5},{5,6},{6,7},{7,8},{8,9},{9,10},{10,1... | collective-permute-start | bytes 64520 | tf_op jit(solution)/shard_map/ppermute | solution.py:32
  102.7 4.7 collective-permute-start.1
  103.6 11.8 %copy-start.73 = (f32[24]{0:T(128)}, f32[24]{0:T(128)S(1)}, u32[]{:S(2)}) copy-start(f32[24]{0:T(128)S(1)} %slice_reduce_fusion.2) | copy-start | bytes 292
  107.3 3.8 collective-permute-start.2
  111.1 4.3 collective-permute-start.3
  113.9 18.9 %collective-permute-start.6 = (bf16[1,1,1,1,1,128,256]{6,5,4,3,2,1,0:T(8,128)(2,1)}, bf16[1,1,1,1,1,128,256]{6,5,4,3,2,1,0:T(8,128)(2,1)}, u32[]{:S(2)}, u32[]{:S(2)}) collective-permute-start(bf16[1,1,1,1,1,128,256]{6,5,4,3,2,1,0:T(8,128)(2,1)} %slice_bitcast_fusion.3), channel_id=1, source_target_pairs={{0,16},{1,17},{2,18},{3,19},{4,20},{5,21},{6,22},{7,23},{8,24},{9,... | collective-permute-start | bytes 196616 | tf_op jit(solution)/shard_map/ppermute | solution.py:75
  116.1 6.2 %collective-permute-start.4 = (f32[2,2,2,1,1,1,24]{6,5,4,3,2,1,0:T(1,128)}, f32[2,2,2,1,1,1,24]{6,5,4,3,2,1,0:T(1,128)}, u32[]{:S(2)}, u32[]{:S(2)}) collective-permute-start(f32[2,2,2,1,1,1,24]{6,5,4,3,2,1,0:T(1,128)} %pad_maximum_fusion.17), channel_id=1, source_target_pairs={{0,2},{1,3},{2,0},{3,1},{4,6},{5,7},{6,4},{7,5},{8,10},{9,11},{10,... | collective-permute-start | bytes 2312 | tf_op jit(solution)/shard_map/ppermute | solution.py:75
  123.6 24.3 %collective-permute-start.5 = (f32[2,2,2,2,1,1,24]{6,5,4,3,2,1,0:T(1,128)}, f32[2,2,2,2,1,1,24]{6,5,4,3,2,1,0:T(1,128)}, u32[]{:S(2)}, u32[]{:S(2)}) collective-permute-start(f32[2,2,2,2,1,1,24]{6,5,4,3,2,1,0:T(1,128)} %pad_maximum_fusion.16), channel_id=1, source_target_pairs={{0,1},{1,0},{2,3},{3,2},{4,5},{5,4},{6,7},{7,6},{8,9},{9,8},{10,11... | collective-permute-start | bytes 4616 | tf_op jit(solution)/shard_map/ppermute | solution.py:75
  135.0 9.4 %collective-permute-start.7 = (bf16[2,1,1,1,1,128,256]{6,5,4,3,2,1,0:T(8,128)(2,1)}, bf16[2,1,1,1,1,128,256]{6,5,4,3,2,1,0:T(8,128)(2,1)}, u32[]{:S(2)}, u32[]{:S(2)}) collective-permute-start(bf16[2,1,1,1,1,128,256]{6,5,4,3,2,1,0:T(8,128)(2,1)} %pad_maximum_fusion.14), channel_id=1, source_target_pairs={{0,8},{1,9},{2,10},{3,11},{4,12},{5,13},{6,14},{7,15},{8,0},{9,1},... | collective-permute-start | bytes 393224 | tf_op jit(solution)/shard_map/ppermute | solution.py:75
  137.0 31.6 %all-to-all-start = ((bf16[32,48,128]{2,1,0:T(8,128)(2,1)}), bf16[32,48,128]{2,1,0:T(8,128)(2,1)}, u32[]{:S(2)}, u32[]{:S(2)}) async-start(bf16[32,48,128]{2,1,0:T(8,128)(2,1)} %add_convert_fusion), calls=%async_computation | async-start | bytes 786432 | tf_op jit(solution)/shard_map/all_to_all | solution.py:127
  146.7 9.5 %collective-permute-start.8 = (bf16[2,2,1,1,1,128,256]{6,5,4,3,2,1,0:T(8,128)(2,1)}, bf16[2,2,1,1,1,128,256]{6,5,4,3,2,1,0:T(8,128)(2,1)}, u32[]{:S(2)}, u32[]{:S(2)}) collective-permute-start(bf16[2,2,1,1,1,128,256]{6,5,4,3,2,1,0:T(8,128)(2,1)} %pad_maximum_fusion.13), channel_id=1, source_target_pairs={{0,4},{1,5},{2,6},{3,7},{4,0},{5,1},{6,2},{7,3},{8,12},{9,13},{10,... | collective-permute-start | bytes 786440 | tf_op jit(solution)/shard_map/ppermute | solution.py:75
  158.8 33.9 %collective-permute-start.9 = (bf16[2,2,2,1,1,128,256]{6,5,4,3,2,1,0:T(8,128)(2,1)}, bf16[2,2,2,1,1,128,256]{6,5,4,3,2,1,0:T(8,128)(2,1)}, u32[]{:S(2)}, u32[]{:S(2)}) collective-permute-start(bf16[2,2,2,1,1,128,256]{6,5,4,3,2,1,0:T(8,128)(2,1)} %pad_maximum_fusion.8), channel_id=1, source_target_pairs={{0,2},{1,3},{2,0},{3,1},{4,6},{5,7},{6,4},{7,5},{8,10},{9,11},{10,... | collective-permute-start | bytes 1572872 | tf_op jit(solution)/shard_map/ppermute | solution.py:75
  173.0 22.9 %all-to-all-start.1 = ((bf16[32,48,128]{2,1,0:T(8,128)(2,1)}), bf16[32,48,128]{2,1,0:T(8,128)(2,1)}, u32[]{:S(2)}, u32[]{:S(2)}) async-start(bf16[32,48,128]{2,1,0:T(8,128)(2,1)} %carry.2), calls=%async_computation.1 | async-start | bytes 786432 | tf_op jit(solution)/shard_map/all_to_all | solution.py:133
  195.8 11.7 %collective-permute-start.10 = (bf16[2,2,2,2,1,128,256]{6,5,4,3,2,1,0:T(8,128)(2,1)}, bf16[2,2,2,2,1,128,256]{6,5,4,3,2,1,0:T(8,128)(2,1)}, u32[]{:S(2)}, u32[]{:S(2)}) collective-permute-start(bf16[2,2,2,2,1,128,256]{6,5,4,3,2,1,0:T(8,128)(2,1)} %pad_maximum_fusion.2), channel_id=1, source_target_pairs={{0,1},{1,0},{2,3},{3,2},{4,5},{5,4},{6,7},{7,6},{8,9},{9,8},{10,11... | collective-permute-start | bytes 3145736 | tf_op jit(solution)/shard_map/ppermute | solution.py:75
  197.4 5.7 copy-start.23
  220.4 19.1 %copy-start.26 = (f32[128,1024]{1,0:T(8,128)}, f32[128,1024]{1,0:T(8,128)S(1)}, u32[]{:S(2)}) copy-start(f32[128,1024]{1,0:T(8,128)S(1)} %get-tuple-element.233) | copy-start | bytes 1572868
  228.8 9.4 %copy-start.40 = (bf16[128,2048]{1,0:T(8,128)(2,1)}, bf16[128,2048]{1,0:T(8,128)(2,1)S(1)}, u32[]{:S(2)}) copy-start(bf16[128,2048]{1,0:T(8,128)(2,1)S(1)} %get-tuple-element.129) | copy-start | bytes 1572868
  264.1 46.2 %all-to-all-start.2 = ((bf16[32,48,128]{2,1,0:T(8,128)(2,1)}), bf16[32,48,128]{2,1,0:T(8,128)(2,1)}, u32[]{:S(2)}, u32[]{:S(2)}) async-start(bf16[32,48,128]{2,1,0:T(8,128)(2,1)} %bitcast.275), calls=%async_computation.2 | async-start | bytes 786432 | tf_op jit(solution)/shard_map/all_to_all | solution.py:127
  296.2 38.0 %collective-permute-start.12 = (bf16[2,2,2,2,128,256]{5,4,0,1,2,3:T(8,128)(2,1)}, bf16[2,2,2,2,128,256]{5,4,0,1,2,3:T(8,128)(2,1)}, u32[]{:S(2)}, u32[]{:S(2)}) collective-permute-start(bf16[2,2,2,2,128,256]{5,4,0,1,2,3:T(8,128)(2,1)} %bitcast.254), channel_id=1, source_target_pairs={{0,1},{1,0},{2,3},{3,2},{4,5},{5,4},{6,7},{7,6},{8,9},{9,8},{10,11... | collective-permute-start | bytes 3145736 | tf_op jit(solution)/shard_map/ppermute | solution.py:75
  314.6 29.1 %all-to-all-start.3 = ((bf16[32,48,128]{2,1,0:T(8,128)(2,1)}), bf16[32,48,128]{2,1,0:T(8,128)(2,1)}, u32[]{:S(2)}, u32[]{:S(2)}) async-start(bf16[32,48,128]{2,1,0:T(8,128)(2,1)} %carry.3), calls=%async_computation.3 | async-start | bytes 786432 | tf_op jit(solution)/shard_map/all_to_all | solution.py:133
  330.5 164.6 %reduce-scatter.3.cloned.1.call-start = ((), (), s32[]{:S(2)}) async-start(), calls=%async_computation.8 | async-start | bytes 8921088 | tf_op jit(solution)/shard_map/reduce_scatter | solution.py:566
  338.3 30.4 %collective-permute-start.13 = (bf16[2,2,2,128,256]{4,3,0,1,2:T(8,128)(2,1)}, bf16[2,2,2,128,256]{4,3,0,1,2:T(8,128)(2,1)}, u32[]{:S(2)}, u32[]{:S(2)}) collective-permute-start(bf16[2,2,2,128,256]{4,3,0,1,2:T(8,128)(2,1)} %fusion.80), channel_id=1, source_target_pairs={{0,2},{1,3},{2,0},{3,1},{4,6},{5,7},{6,4},{7,5},{8,10},{9,11},{10,... | collective-permute-start | bytes 1572872 | tf_op jit(solution)/shard_map/ppermute | solution.py:75
  351.2 9.1 %copy-start.54 = (f32[128,24]{0,1:T(8,128)S(1)}, f32[128,24]{0,1:T(8,128)}, u32[]{:S(2)}) copy-start(f32[128,24]{0,1:T(8,128)} %get-tuple-element.235) | copy-start | bytes 36868
  368.6 5.0 copy-start.2
  372.6 7.8 %collective-permute-start.14 = (bf16[2,2,128,256]{3,2,0,1:T(8,128)(2,1)S(1)}, bf16[2,2,128,256]{3,2,0,1:T(8,128)(2,1)}, u32[]{:S(2)}, u32[]{:S(2)}) collective-permute-start(bf16[2,2,128,256]{3,2,0,1:T(8,128)(2,1)S(1)} %fusion.85), channel_id=1, source_target_pairs={{0,4},{1,5},{2,6},{3,7},{4,0},{5,1},{6,2},{7,3},{8,12},{9,13},{10,... | collective-permute-start | bytes 786440 | tf_op jit(solution)/shard_map/ppermute | solution.py:75
  375.7 7.7 %copy-start.38 = (f32[128,24]{1,0:T(8,128)S(1)}, f32[128,24]{1,0:T(8,128)}, u32[]{:S(2)}) copy-start(f32[128,24]{1,0:T(8,128)} %copy.143) | copy-start | bytes 36868
  375.7 7.7 %copy-start.43 = (f32[24,128]{0,1:T(8,128)S(1)}, f32[24,128]{0,1:T(8,128)}, u32[]{:S(2)}) copy-start(f32[24,128]{0,1:T(8,128)} %copy.134) | copy-start | bytes 36868
  375.7 7.7 %copy-start.72 = (f32[24]{0:T(128)S(1)}, f32[24]{0:T(128)}, u32[]{:S(2)}) copy-start(f32[24]{0:T(128)} %param.25) | copy-start | bytes 292
  375.7 7.7 %copy-start.74 = (f32[24]{0:T(128)S(1)}, f32[24]{0:T(128)}, u32[]{:S(2)}) copy-start(f32[24]{0:T(128)} %copy-done.73) | copy-start | bytes 292
  375.7 7.6 %copy-start.80 = (pred[128]{0:T(512)(128)(4,1)S(1)}, pred[128]{0:T(512)(128)(4,1)}, u32[]{:S(2)}) copy-start(pred[128]{0:T(512)(128)(4,1)} %copy-done.79) | copy-start | bytes 388
  375.7 7.6 %copy-start.83 = (f32[24]{0:T(128)S(1)}, f32[24]{0:T(128)}, u32[]{:S(2)}) copy-start(f32[24]{0:T(128)} %copy-done.82) | copy-start | bytes 292
  375.7 12.9 %collective-permute-start.11 = (f32[3,1792]{1,0:T(4,128)}, f32[3,1792]{1,0:T(4,128)S(1)}, u32[]{:S(2)}, u32[]{:S(2)}) collective-permute-start(f32[3,1792]{1,0:T(4,128)} %pad_add_fusion.1), channel_id=1, source_target_pairs={{1,0},{2,1},{3,2},{4,3},{5,4},{6,5},{7,6},{8,7},{9,8},{10,9},{11,1... | collective-permute-start | bytes 64520 | tf_op jit(solution)/shard_map/ppermute | solution.py:32
  381.4 5.7 collective-permute-start.15
  387.2 7.4 %copy-start.66 = (f32[128]{0:T(128)S(1)}, f32[128]{0:T(128)}, u32[]{:S(2)}) copy-start(f32[128]{0:T(128)} %copy-done.65) | copy-start | bytes 1540
  387.2 5.2 collective-permute-start.16
  400.6 206.2 %reduce-scatter.5.cloned.1.call-start = ((), (), s32[]{:S(2)}) async-start(), calls=%async_computation.9 | async-start | bytes 17301504 | tf_op jit(solution)/shard_map/reduce_scatter | solution.py:518
  407.8 6.7 %copy-start.81 = (f32[1024]{0:T(1024)S(1)}, f32[1024]{0:T(1024)}, u32[]{:S(2)}) copy-start(f32[1024]{0:T(1024)} %get-tuple-element.96) | copy-start | bytes 12292
  407.8 48.7 %copy-start.8 = (f32[128,1024]{1,0:T(8,128)S(1)}, f32[128,1024]{1,0:T(8,128)}, u32[]{:S(2)}) copy-start(f32[128,1024]{1,0:T(8,128)} %copy-done.7) | copy-start | bytes 1572868
  (66 other events, 181.5 us)
Sparse Core Ops, SparseCore 0:
  12.2 65.9 all-gather.2
  80.3 117.0 all-gather.4
  400.7 94.4 reduce-scatter.2
  497.3 109.4 reduce-scatter.4

commit v3 on v2

--- a/solution.py
+++ b/solution.py
@@ -16,7 +16,6 @@
 QUERY_HEADS = 8
 KEYVALUE_HEADS = 2
 HEAD_SIZE = 64
-SPAN = 128
 DSSM = 1536
 CONV_CH = 1792
 
@@ -123,7 +122,7 @@
 def carried_states(decay_rows, states, axis, reverse):
     size = lax.axis_size(axis)
     share = states.shape[0] // size
-    sent = states.astype(jnp.bfloat16).reshape(size, share, states.shape[1])
+    sent = states.reshape(size, share, states.shape[1])
     fresh = lax.all_to_all(sent, axis, 0, 0, tiled=True)
     folded = pl.pallas_call(
         partial(carry_kernel, reverse=reverse),
@@ -131,7 +130,7 @@
         name="carry",
     )(decay_rows, fresh)
     back = lax.all_to_all(folded, axis, 0, 0, tiled=True)
-    return back.reshape(states.shape).astype(jnp.float32)
+    return back.reshape(states.shape)
 
 
 def matmul(left, right):
@@ -164,69 +163,6 @@
 def silu_slope(values):
     logistic = jax.nn.sigmoid(values)
     return logistic * (1.0 + values * (1.0 - logistic))
-
-
-def conv_apply(seg_window, conv_ext, conv_weight, conv_bias):
-    out_rows = conv_ext.shape[0] - (KC - 1)
-    summed = jnp.broadcast_to(conv_bias[None, :], (out_rows, conv_ext.shape[1]))
-    for offset in range(KC):
-        same_doc = seg_window[offset : offset + out_rows] == seg_window[KC - 1 :]
-        summed = summed + conv_weight[offset][None, :] * jnp.where(
-            same_doc[:, None], conv_ext[offset : offset + out_rows], 0.0
-        )
-    return jax.nn.silu(summed)
-
-
-def ssm_core(seg_here, seg_before, conv_act, dt_raw, dt_bias, decay_log, skip_gain):
-    row_count = conv_act.shape[0]
-    blocks_count = row_count // SPAN
-    ssm_x = conv_act[:, : HM * HP].reshape(blocks_count, SPAN, HM, HP)
-    ssm_b = conv_act[:, HM * HP : HM * HP + NS].reshape(blocks_count, SPAN, NS)
-    ssm_c = conv_act[:, HM * HP + NS :].reshape(blocks_count, SPAN, NS)
-    step_size = jax.nn.softplus(dt_raw + dt_bias[None, :])
-    log_decay = -jnp.exp(decay_log)[None, :] * step_size
-    step_heads = step_size.reshape(blocks_count, SPAN, HM).transpose(0, 2, 1)
-    cumulative = jnp.cumsum(log_decay.reshape(blocks_count, SPAN, HM).transpose(0, 2, 1), axis=2)
-    seg_blocks = seg_here.reshape(blocks_count, SPAN)
-    seg_prior = jnp.concatenate([jnp.reshape(seg_before, (1,)), seg_blocks[:-1, -1]])
-    seg_last = seg_blocks[:, -1]
-    lower = jnp.arange(SPAN)[:, None] >= jnp.arange(SPAN)[None, :]
-    visible = (lower[None] & (seg_blocks[:, :, None] == seg_blocks[:, None, :]))[:, None]
-    gaps = cumulative[:, :, :, None] - cumulative[:, :, None, :]
-    mixing = jnp.where(visible, jnp.exp(jnp.where(visible, gaps, 0.0)), 0.0)
-    inner = jnp.einsum("ktn,ksn->kts", ssm_c, ssm_b, precision=HIGH)
-    weighted = mixing * inner[:, None] * step_heads[:, :, None, :]
-    intra = jnp.einsum("khts,kshp->kthp", weighted, ssm_x, precision=HIGH)
-    to_end = (
-        jnp.where(
-            (seg_blocks == seg_last[:, None])[:, None, :],
-            jnp.exp(cumulative[:, :, -1:] - cumulative),
-            0.0,
-        )
-        * step_heads
-    )
-    block_states = jnp.einsum("khs,kshp,ksn->khpn", to_end, ssm_x, ssm_b, precision=HIGH)
-    from_start = jnp.where((seg_blocks == seg_prior[:, None])[:, None, :], jnp.exp(cumulative), 0.0)
-    block_decay = from_start[:, :, -1]
-
-    def advance(carried, inputs):
-        state_now, product = carried
-        decay_now, fresh = inputs
-        return (
-            (decay_now[:, None, None] * state_now + fresh, product * decay_now),
-            (state_now, product),
-        )
-
-    initial_carry = (jnp.zeros((HM, HP, NS), jnp.float32), jnp.ones((HM,), jnp.float32))
-    (final_state, unused), (entering, products) = lax.scan(
-        advance, initial_carry, (block_decay, block_states)
-    )
-    carried_in = jnp.einsum("kht,ktn,khpn->kthp", from_start, ssm_c, entering, precision=HIGH)
-    local_out = (intra + carried_in + skip_gain[None, None, :, None] * ssm_x).reshape(
-        row_count, HM, HP
-    )
-    reach = (from_start * products[:, :, None]).transpose(1, 0, 2).reshape(HM, row_count)
-    return (local_out, final_state, reach, ssm_c.reshape(row_count, NS))
 
 
 def stacked_heads(values, kv):
@@ -377,6 +313,338 @@
         ),
         name="attend_back",
     )(bounds, query, keyval_all, seg_rows, seg_all, totals, mid, grad)
+
+
+EDGE = 8
+
+
+def dot_exact(left, right, contract):
+    return lax.dot_general(
+        left, right, (contract, ((), ())), precision=HIGH, preferred_element_type=jnp.float32
+    )
+
+
+def low(values):
+    return values.astype(jnp.bfloat16)
+
+
+def head_columns(width):
+    head = lax.broadcasted_iota(jnp.int32, (HM, width), 0)
+    channel = lax.broadcasted_iota(jnp.int32, (HM, width), 1)
+    return ((channel >= head * HP) & (channel < (head + 1) * HP)).astype(jnp.float32)
+
+
+def to_channels(per_head):
+    return dot_exact(per_head, head_columns(DSSM), ((1,), (0,)))
+
+
+def to_heads(per_channel):
+    return dot_exact(per_channel, head_columns(DSSM), ((1,), (1,)))
+
+
+def silu_of(values):
+    return values * jax.nn.sigmoid(values)
+
+
+def softplus_of(values):
+    return jnp.maximum(values, 0.0) + jnp.log1p(jnp.exp(-jnp.abs(values)))
+
+
+class Decays:
+    def __init__(self, dt_raw, dt_bias, decay_log, seg_column, seg_row, seg_before):
+        rows = dt_raw.shape[0]
+        at = lax.broadcasted_iota(jnp.int32, (rows, rows), 0)
+        to = lax.broadcasted_iota(jnp.int32, (rows, rows), 1)
+        self.lower = (at >= to).astype(jnp.float32)
+        self.same = (at == to).astype(jnp.float32)
+        self.shifted = dt_raw + dt_bias
+        self.step = softplus_of(self.shifted)
+        self.rate = -jnp.exp(decay_log)
+        self.log_decay = self.rate * self.step
+        self.total = dot_exact(self.lower, self.log_decay, ((1,), (0,)))
+        self.total_lanes = dot_exact(self.total, self.same, ((0,), (0,)))
+        self.step_lanes = dot_exact(self.step, self.same, ((0,), (0,)))
+        self.bias = jnp.where((at >= to) & (seg_column == seg_row), 0.0, NEG)
+        last = lax.broadcasted_iota(jnp.int32, (rows, HM), 0) == rows - 1
+        self.last = last.astype(jnp.float32)
+        end = jnp.sum(self.last * self.total, axis=0, keepdims=True)
+        to_last = seg_column == seg_column[rows - 1 :, :]
+        self.end_only = jnp.where(to_last, jnp.exp(jnp.where(to_last, end - self.total, 0.0)), 0.0)
+        self.to_end = self.end_only * self.step
+        self.reach = jnp.where(seg_column == seg_before, jnp.exp(self.total), 0.0)
+
+    def mixing(self, h):
+        gap = self.total[:, h : h + 1] - self.total_lanes[h : h + 1, :]
+        return jnp.exp(gap + self.bias)
+
+
+def conv_pieces(pre_ref):
+    act = silu_of(pre_ref[...])
+    return (act[:, :DSSM], act[:, DSSM : DSSM + NS], act[:, DSSM + NS :])
+
+
+def in_half(values, second):
+    lane = lax.broadcasted_iota(jnp.int32, values.shape, 1)
+    return jnp.where((lane >= HP) == second, values, jnp.zeros_like(values))
+
+
+def ssm_forward_kernel(
+    seg_before_ref,
+    projected_ref,
+    edge_ref,
+    same_ref,
+    seg_column_ref,
+    seg_row_ref,
+    conv_weight_ref,
+    conv_bias_ref,
+    dt_bias_ref,
+    decay_log_ref,
+    skip_ref,
+    pre_ref,
+    local_ref,
+    state_ref,
+    reach_ref,
+    ext_ref,
+    *,
+    dt_at,
+):
+    rows = projected_ref.shape[0]
+    ext_ref[:EDGE] = edge_ref[...]
+    ext_ref[EDGE:] = projected_ref[:, DSSM : DSSM + CONV_CH]
+    pre = jnp.broadcast_to(conv_bias_ref[...], (rows, CONV_CH))
+    for k in range(KC):
+        at = EDGE - (KC - 1) + k
+        pre = pre + conv_weight_ref[k : k + 1, :] * (
+            same_ref[:, k : k + 1] * ext_ref[at : at + rows, :]
+        )
+    pre_ref[...] = pre
+    ssm_x, ssm_b, ssm_c = conv_pieces(pre_ref)
+    decays = Decays(
+        projected_ref[:, dt_at : dt_at + HM],
+        dt_bias_ref[...],
+        decay_log_ref[...],
+        seg_column_ref[...],
+        seg_row_ref[...],
+        seg_before_ref[0],
+    )
+    inner = dot_exact(ssm_c, ssm_b, ((1,), (1,)))
+    x_low = low(ssm_x)
+    skip = to_channels(jnp.broadcast_to(skip_ref[...], (EDGE, HM)))[:1]
+    for pair in range(HM // 2):
+        at = pair * 2 * HP
+        x_pair = x_low[:, at : at + 2 * HP]
+        parts = []
+        for h in (2 * pair, 2 * pair + 1):
+            weighted = decays.mixing(h) * inner * decays.step_lanes[h : h + 1, :]
+            parts.append(in_half(matmul(low(weighted), x_pair), h % 2 == 1))
+        local_ref[:, at : at + 2 * HP] = (
+            parts[0] + parts[1] + skip[:, at : at + 2 * HP] * ssm_x[:, at : at + 2 * HP]
+        )
+    state_ref[...] = low(matmul_tn(low(ssm_x * to_channels(decays.to_end)), low(ssm_b)))
+    reach_ref[...] = decays.reach
+
+
+def ssm_join_kernel(projected_ref, local_ref, pre_ref, state_ref, reach_ref, out_ref, gated_ref):
+    ssm_c = silu_of(pre_ref[:, DSSM + NS :])
+    crossed = matmul_nt(low(ssm_c), state_ref[...])
+    out = local_ref[...] + crossed * to_channels(reach_ref[...])
+    out_ref[...] = out
+    gated_ref[...] = low(out * silu_of(projected_ref[:, :DSSM]))
+
+
+def ssm_gate_back_kernel(
+    projected_ref, mixed_grad_ref, out_ref, pre_ref, reach_ref, gate_grad_ref, grad_ref, state_ref
+):
+    gate = projected_ref[:, :DSSM]
+    gated_grad = mixed_grad_ref[:, :DSSM]
+    grad = gated_grad * silu_of(gate)
+    grad_ref[...] = grad
+    gate_grad_ref[...] = low(gated_grad * out_ref[...] * silu_slope(gate))
+    ssm_c = silu_of(pre_ref[:, DSSM + NS :])
+    state_ref[...] = low(matmul_tn(low(grad * to_channels(reach_ref[...])), low(ssm_c)))
+
+
+def ssm_backward_kernel(
+    seg_before_ref,
+    projected_ref,
+    edge_ref,
+    same_ref,
+    seg_column_ref,
+    seg_row_ref,
+    conv_weight_ref,
+    dt_bias_ref,
+    decay_log_ref,
+    skip_ref,
+    pre_ref,
+    grad_ref,
+    state_in_ref,
+    state_grad_ref,
+    conv_in_grad_ref,
+    edge_grad_ref,
+    dt_grad_ref,
+    conv_weight_grad_ref,
+    conv_bias_grad_ref,
+    head_grad_ref,
+    ext_ref,
+    act_grad_ref,
+    *,
+    dt_at,
+):
+    rows = projected_ref.shape[0]
+    ssm_x, ssm_b, ssm_c = conv_pieces(pre_ref)
+    decays = Decays(
+        projected_ref[:, dt_at : dt_at + HM],
+        dt_bias_ref[...],
+        decay_log_ref[...],
+        seg_column_ref[...],
+        seg_row_ref[...],
+        seg_before_ref[0],
+    )
+    inner = dot_exact(ssm_c, ssm_b, ((1,), (1,)))
+    grad = grad_ref[...]
+    x_low, grad_low, b_low, c_low = (low(ssm_x), low(grad), low(ssm_b), low(ssm_c))
+    skip = to_channels(jnp.broadcast_to(skip_ref[...], (EDGE, HM)))[:1]
+    to_end_wide = to_channels(decays.to_end)
+    state_in, state_grad = (state_in_ref[...], state_grad_ref[...])
+    from_state = matmul_nt(b_low, state_grad)
+    head_lane = lax.broadcasted_iota(jnp.int32, (rows, HM), 1)
+    head_row = lax.broadcasted_iota(jnp.int32, (HM, rows), 0)
+    row_sums = jnp.zeros((rows, HM), jnp.float32)
+    step_grad_lanes = jnp.zeros((HM, rows), jnp.float32)
+    inner_grad = jnp.zeros((rows, rows), jnp.float32)
+    for pair in range(HM // 2):
+        at = pair * 2 * HP
+        x_pair = x_low[:, at : at + 2 * HP]
+        x_grad = skip[:, at : at + 2 * HP] * grad[:, at : at + 2 * HP]
+        x_grad = x_grad + to_end_wide[:, at : at + 2 * HP] * from_state[:, at : at + 2 * HP]
+        for h in (2 * pair, 2 * pair + 1):
+            out_grad = in_half(grad_low[:, at : at + 2 * HP], h % 2 == 1)
+            mixing = decays.mixing(h)
+            steps = decays.step_lanes[h : h + 1, :]
+            weighted = mixing * inner * steps
+            weight_grad = matmul_nt(out_grad, x_pair) * mixing
+            inner_grad = inner_grad + weight_grad * steps
+            step_part = weight_grad * inner
+            step_grad_lanes = jnp.where(
+                head_row == h, jnp.sum(step_part, axis=0, keepdims=True), step_grad_lanes
+            )
+            row_sums = jnp.where(
+                head_lane == h, jnp.sum(step_part * steps, axis=1, keepdims=True), row_sums
+            )
+            x_grad = x_grad + matmul_tn(low(weighted), out_grad)
+        act_grad_ref[:, at : at + 2 * HP] = x_grad
+    inner_low = low(inner_grad)
+    act_grad_ref[:, DSSM : DSSM + NS] = matmul(low(ssm_x * to_end_wide), state_grad) + matmul_tn(
+        inner_low, c_low
+    )
+    act_grad_ref[:, DSSM + NS :] = matmul(
+        low(grad * to_channels(decays.reach)), state_in
+    ) + matmul(inner_low, b_low)
+    crossed = matmul_nt(c_low, state_in)
+    products = state_in.astype(jnp.float32) * state_grad.astype(jnp.float32)
+    carried = dot_exact(jnp.ones((EDGE, NS), jnp.float32), products, ((1,), (1,)))
+    decay_grad = to_heads(carried)[:1]
+    reach_grad = to_heads(grad * crossed) + decays.last * decay_grad
+    end_grad = to_heads(ssm_x * from_state)
+    end_part = end_grad * decays.to_end
+    step_columns = dot_exact(decays.same, step_grad_lanes, ((1,), (1,)))
+    total_grad = (
+        row_sums
+        - step_columns * decays.step
+        + reach_grad * decays.reach
+        - end_part
+        + decays.last * jnp.sum(end_part, axis=0, keepdims=True)
+    )
+    log_grad = dot_exact(decays.lower, total_grad, ((0,), (0,)))
+    step_grad = step_columns + end_grad * decays.end_only + log_grad * decays.rate
+    dt_grad = step_grad * jax.nn.sigmoid(decays.shifted)
+    dt_grad_ref[...] = dt_grad
+    head_grad_ref[0:1, :] = jnp.sum(dt_grad, axis=0, keepdims=True)
+    head_grad_ref[1:2, :] = jnp.sum(log_grad * decays.log_decay, axis=0, keepdims=True)
+    head_grad_ref[2:3, :] = jnp.sum(to_heads(grad * ssm_x), axis=0, keepdims=True)
+    pre_grad = act_grad_ref[...] * silu_slope(pre_ref[...])
+    conv_bias_grad_ref[...] = jnp.sum(pre_grad, axis=0, keepdims=True)
+    ext_ref[:EDGE] = edge_ref[...]
+    ext_ref[EDGE:] = projected_ref[:, DSSM : DSSM + CONV_CH]
+    parts = []
+    for k in range(KC):
+        at = EDGE - (KC - 1) + k
+        masked = pre_grad * same_ref[:, k : k + 1]
+        conv_weight_grad_ref[k : k + 1, :] = jnp.sum(
+            masked * ext_ref[at : at + rows, :], axis=0, keepdims=True
+        )
+        parts.append(masked * conv_weight_ref[k : k + 1, :])
+    ext_ref[...] = jnp.zeros(ext_ref.shape, jnp.float32)
+    for k in range(KC):
+        at = EDGE - (KC - 1) + k
+        ext_ref[at : at + rows, :] = ext_ref[at : at + rows, :] + parts[k]
+    edge_grad_ref[...] = ext_ref[:EDGE]
+    conv_in_grad_ref[...] = ext_ref[EDGE:]
+
+
+def of(shape, kind=jnp.float32):
+    return jax.ShapeDtypeStruct(shape, kind)
+
+
+def ssm_forward(dt_at, *operands):
+    rows = operands[1].shape[0]
+    return pl.pallas_call(
+        partial(ssm_forward_kernel, dt_at=dt_at),
+        in_specs=[in_smem()] + [in_vmem()] * 10,
+        out_shape=(
+            of((rows, CONV_CH)),
+            of((rows, DSSM)),
+            of((DSSM, NS), jnp.bfloat16),
+            of((rows, HM)),
+        ),
+        scratch_shapes=[pltpu.VMEM((rows + EDGE, CONV_CH), jnp.float32)],
+        name="ssm_forward",
+    )(*operands)
+
+
+def ssm_join(projected, *operands):
+    rows = projected.shape[0]
+    return pl.pallas_call(
+        ssm_join_kernel,
+        in_specs=[in_vmem()] * 5,
+        out_shape=(of((rows, DSSM)), of((rows, DSSM), jnp.bfloat16)),
+        name="ssm_join",
+    )(projected, *operands)
+
+
+def ssm_gate_back(projected, *operands):
+    rows = projected.shape[0]
+    return pl.pallas_call(
+        ssm_gate_back_kernel,
+        in_specs=[in_vmem()] * 5,
+        out_shape=(
+            of((rows, DSSM), jnp.bfloat16),
+            of((rows, DSSM)),
+            of((DSSM, NS), jnp.bfloat16),
+        ),
+        name="ssm_gate_back",
+    )(projected, *operands)
+
+
+def ssm_backward(dt_at, *operands):
+    rows = operands[1].shape[0]
+    return pl.pallas_call(
+        partial(ssm_backward_kernel, dt_at=dt_at),
+        in_specs=[in_smem()] + [in_vmem()] * 13,
+        out_shape=(
+            of((rows, CONV_CH)),
+            of((EDGE, CONV_CH)),
+            of((rows, HM)),
+            of((KC, CONV_CH)),
+            of((1, CONV_CH)),
+            of((3, HM)),
+        ),
+        scratch_shapes=[
+            pltpu.VMEM((rows + EDGE, CONV_CH), jnp.float32),
+            pltpu.VMEM((rows, CONV_CH), jnp.float32),
+        ],
+        name="ssm_backward",
+    )(*operands)
 
 
 def local(
@@ -449,37 +717,47 @@
     scale_one = rms_scale(layer_input)
     normed_one = (layer_input * scale_one * gain_first).astype(jnp.bfloat16)
     projected = matmul(normed_one, first_full)
-    gate_mix = projected[:, :DSSM]
-    conv_in = projected[:, DSSM:q_at]
     query_reduced = projected[:, q_at:kv_at].astype(jnp.bfloat16)
     keyval_low = projected[:, kv_at:dt_at].astype(jnp.bfloat16)
-    dt_raw = projected[:, dt_at:gain_at]
-    edge_rows = passed_along(conv_in[local_row_count - (KC - 1) :], "seq", 1)
+    edge_rows = passed_along(projected[local_row_count - EDGE :, DSSM:q_at], "seq", 1)
     keyval_all = gathered_by_doubling(keyval_low, "seq")
-    conv_ext = jnp.concatenate([edge_rows, conv_in], axis=0)
-    conv_act, conv_pull = jax.vjp(partial(conv_apply, seg_window), conv_ext, conv_weight, conv_bias)
-    ssm_parts, ssm_pull = jax.vjp(
-        partial(ssm_core, seg_here, seg_before), conv_act, dt_raw, dt_bias, decay_log, skip_gain
-    )
-    local_out, dev_state, reach, c_here = ssm_parts
-    dev_decay = reach[:, -1]
-    share = HM * HP // devices
+    seg_column = seg_here[:, None]
+    same_doc = jnp.stack(
+        [
+            (seg_window[k : k + local_row_count] == seg_here).astype(jnp.float32)
+            for k in range(KC)
+        ],
+        axis=1,
+    )
+    step_sum = jnp.sum(jax.nn.softplus(projected[:, dt_at:gain_at] + dt_bias[None, :]), axis=0)
+    dev_decay = jnp.where(
+        seg_here[local_row_count - 1] == seg_before, jnp.exp(-jnp.exp(decay_log) * step_sum), 0.0
+    )
+    share = DSSM // devices
     decay_all = gathered_by_doubling(dev_decay[None], "seq")
     decay_rows = lax.dynamic_slice_in_dim(
         jnp.repeat(decay_all, HP, axis=1), here * share, share, 1
     )[:, :, None]
-    state_in = carried_states(decay_rows, dev_state.reshape(HM * HP, NS), "seq", False).reshape(
-        HM, HP, NS
-    )
-    cross_base = jnp.einsum("tn,hpn->thp", c_here, state_in, precision=HIGH)
-    ssm_out = (local_out + cross_base * reach.T[:, :, None]).reshape(local_row_count, DSSM)
-    gated = (ssm_out * jax.nn.silu(gate_mix)).astype(jnp.bfloat16)
+    placing = (
+        seg_before[None],
+        projected,
+        edge_rows,
+        same_doc,
+        seg_column,
+        seg_here[None, :],
+        conv_weight,
+    )
+    head_rows = (dt_bias[None, :], decay_log[None, :], skip_gain[None, :])
+    conv_pre, local_out, dev_state, reach = ssm_forward(
+        dt_at, *placing, conv_bias[None, :], *head_rows
+    )
+    state_in = carried_states(decay_rows, dev_state, "seq", False)
+    ssm_out, gated = ssm_join(projected, local_out, conv_pre, state_in, reach)
     key_block = math.gcd(sequence_total, 256)
     first_key = jnp.sum((doc_ids < seg_here[0]).astype(jnp.int32))
     bounds = jnp.stack(
         [first_key // key_block, (first_row + local_row_count - 1) // key_block + 1, first_row]
     ).astype(jnp.int32)
-    seg_column = seg_here[:, None]
     seg_all = doc_ids.reshape(sequence_total // key_block, key_block)
     attention_middle, log_total = attention_forward(
         bounds, query_reduced, keyval_all, seg_column, seg_all
@@ -517,8 +795,11 @@
     second_grad, mixed_grad = lax.optimization_barrier((second_grad, mixed_grad))
     second_share = lax.psum_scatter(
         second_grad, "seq", scatter_dimension=0, tiled=True, axis_index_groups=[order]
-    ).astype(jnp.float32)
-    gated_grad = mixed_grad[:, :DSSM]
+    )
+    gate_mix_grad, ssm_grad, state_in_grad = ssm_gate_back(
+        projected, mixed_grad, ssm_out, conv_pre, reach
+    )
+    state_out_grad = carried_states(decay_rows, state_in_grad, "seq", True)
     query_grad_low, keyval_partial = attention_backward(
         bounds,
         query_reduced,
@@ -530,31 +811,20 @@
         mixed_grad[:, DSSM:],
     )
     keyval_grad_low = scattered_by_halving(keyval_partial, "seq").astype(jnp.bfloat16)
-    ssm_grad = gated_grad * jax.nn.silu(gate_mix)
-    gate_mix_grad = gated_grad * ssm_out * silu_slope(gate_mix)
-    ssm_grad_three = ssm_grad.reshape(local_row_count, HM, HP)
-    weighted_grad = ssm_grad_three * reach.T[:, :, None]
-    state_in_grad = jnp.einsum("thp,tn->hpn", weighted_grad, c_here, precision=HIGH)
-    c_grad = jnp.einsum("thp,hpn->tn", weighted_grad, state_in, precision=HIGH)
-    reach_grad = jnp.einsum("thp,thp->ht", ssm_grad_three, cross_base, precision=HIGH)
-    state_out_grad = carried_states(
-        decay_rows, state_in_grad.reshape(HM * HP, NS), "seq", True
-    ).reshape(HM, HP, NS)
-    decay_grad = jnp.sum(state_out_grad * state_in, axis=(1, 2))
-    reach_grad = jnp.concatenate(
-        [reach_grad[:, :-1], reach_grad[:, -1:] + decay_grad[:, None]], axis=1
-    )
-    act_grad_ssm, dt_raw_grad, dt_bias_grad, decay_log_grad, skip_grad = ssm_pull(
-        (ssm_grad_three, state_out_grad, reach_grad, c_grad)
-    )
-    ext_grad, conv_weight_grad, conv_bias_grad = conv_pull(act_grad_ssm)
-    edge_back = passed_along(ext_grad[: KC - 1], "seq", -1)
-    conv_in_grad = ext_grad[KC - 1 :] + jnp.concatenate(
-        [jnp.zeros((local_row_count - (KC - 1), CONV_CH), jnp.float32), edge_back], axis=0
+    conv_own_grad, edge_grad, dt_raw_grad, conv_weight_grad, conv_bias_grad, head_grad = (
+        ssm_backward(dt_at, *placing, *head_rows, conv_pre, ssm_grad, state_in, state_out_grad)
+    )
+    edge_back = passed_along(edge_grad, "seq", -1)
+    conv_in_grad = jnp.concatenate(
+        [
+            conv_own_grad[: local_row_count - EDGE],
+            conv_own_grad[local_row_count - EDGE :] + edge_back,
+        ],
+        axis=0,
     )
     first_grad_low = jnp.concatenate(
         [
-            gate_mix_grad.astype(jnp.bfloat16),
+            gate_mix_grad,
             conv_in_grad.astype(jnp.bfloat16),
             query_grad_low,
             keyval_grad_low,
@@ -563,13 +833,12 @@
         ],
         axis=1,
     )
+    first_grad = matmul_tn(normed_one, first_grad_low).astype(jnp.bfloat16)
+    first_grad, second_share = lax.optimization_barrier((first_grad, second_share))
     first_share = lax.psum_scatter(
-        matmul_tn(normed_one, first_grad_low).astype(jnp.bfloat16),
-        "seq",
-        scatter_dimension=0,
-        tiled=True,
-        axis_index_groups=[order],
+        first_grad, "seq", scatter_dimension=0, tiled=True, axis_index_groups=[order]
     ).astype(jnp.float32)
+    second_share = second_share.astype(jnp.float32)
     normed_one_grad = matmul_nt(first_grad_low, first_full)
     gain1_grad = jnp.sum(normed_one_grad * layer_input * scale_one, axis=0)
     input_grad = reordered(
@@ -578,10 +847,10 @@
     )
     small = (
         conv_weight_grad,
-        conv_bias_grad,
-        dt_bias_grad,
-        decay_log_grad,
-        skip_grad,
+        conv_bias_grad[0],
+        head_grad[0],
+        head_grad[1],
+        head_grad[2],
         gain1_grad,
         gain2_grad,
     )

time: 627 us -> 497 us (0.79)
  local copies, waits for them, and re-layouts: 83.3 us -> 40.8 us
  other arithmetic: 69.3 us -> 29.1 us
  matrix products: 85.7 us -> 48.2 us
  waiting for transfers between devices: 243 us -> 212 us
  Pallas kernels: 18 us -> 44.6 us
  starting transfers between devices: 60.6 us -> 52.5 us
    reduce_scatter x1, waiting for transfers between devices: 107 us -> 23.4 us  [local(): lax.psum_scatter(second_grad, 'seq', scatter_dimension=0, tiled=True, axi...]
    dot_general x14 -> x0, matrix products: 36 us -> none  [the longest x3 12.9 us: ssm_core(): intra = jnp.einsum('khts,kshp->kthp', weighted, ssm_x, precision=HIGH)]
    pallas_call x0 -> x4, Pallas kernels: none -> 26.6 us  [the longest x1 12.3 us: ssm_backward(): pl.pallas_call(partial(ssm_backward_kernel, dt_at=dt_at), in_specs=[in_sm...]
    all_to_all x2, waiting for transfers between devices: 0.01 us -> 21.4 us  [carried_states(): fresh = lax.all_to_all(sent, axis, 0, 0, tiled=True)]
    ppermute x15, waiting for transfers between devices: 32.2 us -> 50 us  [swapped(): return lax.ppermute(values, axis, [(i, i ^ bit) for i in range(size)])]
    all_to_all x2, waiting for transfers between devices: 3.74 us -> 17.7 us  [carried_states(): back = lax.all_to_all(folded, axis, 0, 0, tiled=True)]
    all_to_all x2, starting transfers between devices: 19.9 us -> 6.08 us  [carried_states(): back = lax.all_to_all(folded, axis, 0, 0, tiled=True)]
    reduce_sum x8 -> x1, other arithmetic: 12.4 us -> 0.07 us  [local(): jnp.sum(jax.nn.softplus(projected[:, dt_at:gain_at] + dt_bias[None, :]),...]
  transfers between devices with their start and end apart: 25 -> 25, of which waited for: 12 -> 14; matrix products, arithmetic and copies ran while one was open for 27% -> 14% of each run, Pallas kernels for 3% -> 9%
where the time goes in v3:
time: 497 us; the launch traced here: 487 us
  waiting for transfers between devices  212 us (43%)
  starting transfers between devices  52.5 us (11%)
  matrix products  48.2 us (10%)
  Pallas kernels  44.6 us (9%)
  local copies, waits for them, and re-layouts  40.8 us (8%)
  blocking collectives  39.8 us (8%)
  other arithmetic  29.1 us (6%)
  between operations  19.6 us (4%)
    all_gather x1, waiting for transfers between devices, local(): lax.all_gather(first_pack, 'seq', axis=0, tiled=True, axis_index_groups=[...  63.3 us
    ppermute x15, waiting for transfers between devices, swapped(): return lax.ppermute(values, axis, [(i, i ^ bit) for i in range(size)])  50 us
    psum x1, blocking collectives, local(): lax.psum(jnp.concatenate([part.reshape(-1) for part in small]), 'seq')  39.8 us
    reduce_scatter x1, waiting for transfers between devices, local(): lax.psum_scatter(first_grad, 'seq', scatter_dimension=0, tiled=True, axis...  36.5 us
    reduce_scatter x1, waiting for transfers between devices, local(): lax.psum_scatter(second_grad, 'seq', scatter_dimension=0, tiled=True, axi...  23.4 us
    all_to_all x2, starting transfers between devices, carried_states(): fresh = lax.all_to_all(sent, axis, 0, 0, tiled=True)  22.6 us
    all_to_all x2, waiting for transfers between devices, carried_states(): fresh = lax.all_to_all(sent, axis, 0, 0, tiled=True)  21.4 us
    dot_general x4, matrix products, matmul_nt(): lax.dot_general(left, right, (((1,), (1,)), ((), ())), preferred_element_...  21 us
  transfers between devices with their start and end apart: 25, of which 14 were waited for; matrix products, arithmetic and copies ran while one was open for 14% of the time, Pallas kernels for 9%

profile of v3, /device:TPU:0, one launch (start us, length us, event | category | flops | bytes accessed | tf_op | source)
XLA Modules:
  0.0 487.0 jit_solution(3669152495718178882)
XLA Ops:
  13.1 1.8 pad_maximum_fusion.6
  14.9 63.3 %all-gather.3.cloned.1.call-done = bf16[1024,4224]{1,0:T(8,128)(2,1)} async-done(((bf16[32,4224]{1,0:T(8,128)(2,1)}), bf16[1024,4224]{1,0:T(8,128)(2,1)}) %all-gather.3.cloned.1.call-update) | async-done | bytes 8650768 | tf_op jit(solution)/shard_map/all_gather | solution.py:698
  84.6 5.2 %fusion.42 = (bf16[128,4224]{1,0:T(8,128)(2,1)S(1)}, f32[128,4224]{1,0:T(8,128)S(1)}) fusion(bf16[1024,4224]{1,0:T(8,128)(2,1)} %all-gather.3.cloned.1.call-done, f32[128,1024]{1,0:T(8,128)S(1)} %concatenate.77, f32[1024]{0:T(1024)S(1)} %get-tuple-element.71, f32[128]{0:T(128)S(1)} %add_rsqrt_fusion.1), kind=kOutput, calls=%fused_computation.134 | convolution fusion | flops 1108230144 | bytes 12423680 | tf_op jit(solution)/shard_map/dot_general | solution.py:137
  91.3 1.7 collective-permute-start.1
  92.9 5.4 %collective-permute-done.6 = bf16[1,1,1,1,1,128,256]{6,5,4,3,2,1,0:T(8,128)(2,1)S(1)} collective-permute-done((bf16[1,1,1,1,1,128,256]{6,5,4,3,2,1,0:T(8,128)(2,1)S(1)}, bf16[1,1,1,1,1,128,256]{6,5,4,3,2,1,0:T(8,128)(2,1)S(1)}, u32[]{:S(2)}, u32[]{:S(2)}) %collective-permute-start.6) | collective-permute-done | bytes 65568 | tf_op jit(solution)/shard_map/ppermute | solution.py:74
  98.5 2.1 collective-permute-start.2
  100.6 6.5 %collective-permute-done.7 = bf16[2,1,1,1,1,128,256]{6,5,4,3,2,1,0:T(8,128)(2,1)S(1)} collective-permute-done((bf16[2,1,1,1,1,128,256]{6,5,4,3,2,1,0:T(8,128)(2,1)S(1)}, bf16[2,1,1,1,1,128,256]{6,5,4,3,2,1,0:T(8,128)(2,1)S(1)}, u32[]{:S(2)}, u32[]{:S(2)}) %collective-permute-start.7) | collective-permute-done | bytes 131104 | tf_op jit(solution)/shard_map/ppermute | solution.py:74
  107.3 2.1 collective-permute-start.3
  109.3 4.7 collective-permute-done.8
  115.0 5.0 %collective-permute-start.9 = (bf16[2,2,2,1,1,128,256]{6,5,4,3,2,1,0:T(8,128)(2,1)}, bf16[2,2,2,1,1,128,256]{6,5,4,3,2,1,0:T(8,128)(2,1)}, u32[]{:S(2)}, u32[]{:S(2)}) collective-permute-start(bf16[2,2,2,1,1,128,256]{6,5,4,3,2,1,0:T(8,128)(2,1)} %pad_maximum_fusion.7), channel_id=1, source_target_pairs={{0,2},{1,3},{2,0},{3,1},{4,6},{5,7},{6,4},{7,5},{8,10},{9,11},{10,... | collective-permute-start | bytes 1572872 | tf_op jit(solution)/shard_map/ppermute | solution.py:74
  123.6 20.2 %collective-permute-done.4 = f32[2,2,2,1,1,1,24]{6,5,4,3,2,1,0:T(1,128)S(1)} collective-permute-done((f32[2,2,2,1,1,1,24]{6,5,4,3,2,1,0:T(1,128)S(1)}, f32[2,2,2,1,1,1,24]{6,5,4,3,2,1,0:T(1,128)S(1)}, u32[]{:S(2)}, u32[]{:S(2)}) %collective-permute-start.4) | collective-permute-done | bytes 800 | tf_op jit(solution)/shard_map/ppermute | solution.py:74
  145.0 5.7 %ssm_forward.1 = (f32[128,1792]{1,0:T(8,128)}, f32[128,1536]{1,0:T(8,128)}, bf16[1536,128]{1,0:T(8,128)(2,1)}, f32[128,24]{1,0:T(8,128)}) custom-call(s32[1]{0:T(128)} %slice.341.seg_before_ref, f32[128,4224]{1,0:T(8,128)} %copy-done, f32[8,1792]{1,0:T(8,128)} %copy-done.20, f32[128,4]{1,0:T(8,128)} %stack.38.same_ref, ...), custom_call_target="tpu_custom_call" | custom-call | tf_op jit(solution)/shard_map/ssm_forward/pallas_call | solution.py:591
  150.7 4.1 all-to-all-start
  159.9 12.4 %all-to-all-done.fresh_ref = bf16[32,48,128]{2,1,0:T(8,128)(2,1)S(1)} async-done(((bf16[32,48,128]{2,1,0:T(8,128)(2,1)}), bf16[32,48,128]{2,1,0:T(8,128)(2,1)S(1)}, u32[]{:S(2)}, u32[]{:S(2)}) %all-to-all-start) | async-done | bytes 393248 | tf_op jit(solution)/shard_map/all_to_all | solution.py:126
  173.1 4.3 carry.2
  177.4 2.6 all-to-all-start.1
  185.7 1.6 slice.430.query_ref
  187.2 10.5 %all-to-all-done.1 = bf16[32,48,128]{2,1,0:T(8,128)(2,1)S(1)} async-done(((bf16[32,48,128]{2,1,0:T(8,128)(2,1)}), bf16[32,48,128]{2,1,0:T(8,128)(2,1)S(1)}, u32[]{:S(2)}, u32[]{:S(2)}) %all-to-all-start.1) | async-done | bytes 393248 | tf_op jit(solution)/shard_map/all_to_all | solution.py:132
  198.5 4.1 ssm_join.1
  205.5 4.1 attend.1
  210.6 3.8 multiply_reduce_fusion.4
  214.4 4.9 %fusion.2 = f32[128,4096]{1,0:T(8,128)S(1)} fusion(bf16[1024,8192]{1,0:T(8,128)(2,1)} %all-gather.5.cloned.1.call-done, f32[128,1024]{1,0:T(8,128)S(1)} %get-tuple-element.179, f32[1024]{0:T(1024)S(1)} %get-tuple-element.70, f32[128]{0:T(128)S(1)} %add_rsqrt_fusion), kind=kOutput, calls=%fused_computation.5 | convolution fusion | flops 1074135040 | bytes 11014656 | tf_op jit(solution)/shard_map/dot_general | solution.py:137
  219.3 3.4 multiply_convert_fusion.1
  222.7 2.4 convolution_convert_fusion.1
  225.1 7.0 %multiply_reduce_fusion = (f32[1024]{0:T(1024)}, f32[128]{0:T(128)S(1)}, f32[128,1024]{1,0:T(8,128)S(1)}) fusion(f32[128,1024]{1,0:T(8,128)S(1)} %get-tuple-element.179, f32[128]{0:T(128)S(1)} %add_rsqrt_fusion, f32[1024]{0:T(1024)S(1)} %get-tuple-element.70, bf16[1024,8192]{1,0:T(8,128)(2,1)} %all-gather.5.cloned.1.call-done, ...), kind=kOutput, calls=%fused_computation.42 | convolution fusion | flops 1076624256 | bytes 10494976 | tf_op jit(solution)/shard_map/dot_general | solution.py:147
  234.8 6.9 %pad_maximum_fusion = bf16[1024,8192]{1,0:T(8,128)(2,1)} fusion(bf16[1024,2048]{1,0:T(8,128)(2,1)S(1)} %convolution_convert_fusion.2, bf16[1024,2048]{1,0:T(8,128)(2,1)S(1)} %convolution_convert_fusion.3, bf16[1024,4096]{1,0:T(8,128)(2,1)S(1)} %convolution_convert_fusion.1), kind=kLoop, calls=%fused_computation | loop fusion | flops 50331648 | bytes 33554432 | tf_op jit(solution)/shard_map/concatenate | solution.py:786
  241.7 2.9 fusion.8.mixed_grad_ref
  246.4 5.2 %attend_back.1 = (bf16[128,512]{1,0:T(8,128)(2,1)}, bf16[4096,256]{1,0:T(8,128)(2,1)}) custom-call(s32[3]{0:T(128)} %pad_add_fusion.1.bounds_ref, bf16[128,512]{1,0:T(8,128)(2,1)} %slice.430.query_ref, bf16[4096,256]{1,0:T(8,128)(2,1)} %bitcast.85, s32[128,1]{1,0:T(8,128)} %copy.63.seg_column_ref.seg_row_ref, s32[16,256]{1,0:T(8,128)} %reshape.110.seg_all_ref, ...), custom_call_target="tpu_custom_call" | custom-call | tf_op jit(solution)/shard_map/attend_back/pallas_call | solution.py:307
  251.6 2.7 constant_dynamic-slice_fusion.1
  254.4 4.4 ssm_gate_back.1
  258.9 18.5 %all-to-all-start.2 = ((bf16[32,48,128]{2,1,0:T(8,128)(2,1)}), bf16[32,48,128]{2,1,0:T(8,128)(2,1)S(1)}, u32[]{:S(2)}, u32[]{:S(2)}) async-start(bf16[32,48,128]{2,1,0:T(8,128)(2,1)} %bitcast.92), calls=%async_computation.2 | async-start | bytes 786432 | tf_op jit(solution)/shard_map/all_to_all | solution.py:126
  278.4 1.9 convert_add_fusion
  281.1 1.8 collective-permute-start.13
  282.9 9.0 %all-to-all-done.2.fresh_ref = bf16[32,48,128]{2,1,0:T(8,128)(2,1)S(1)} async-done(((bf16[32,48,128]{2,1,0:T(8,128)(2,1)}), bf16[32,48,128]{2,1,0:T(8,128)(2,1)S(1)}, u32[]{:S(2)}, u32[]{:S(2)}) %all-to-all-start.2) | async-done | bytes 393248 | tf_op jit(solution)/shard_map/all_to_all | solution.py:126
  292.6 4.3 carry.3
  296.9 3.5 all-to-all-start.3
  300.5 2.8 collective-permute-done.13
  307.6 7.3 %all-to-all-done.3 = bf16[32,48,128]{2,1,0:T(8,128)(2,1)S(1)} async-done(((bf16[32,48,128]{2,1,0:T(8,128)(2,1)}), bf16[32,48,128]{2,1,0:T(8,128)(2,1)S(1)}, u32[]{:S(2)}, u32[]{:S(2)}) %all-to-all-start.3) | async-done | bytes 393248 | tf_op jit(solution)/shard_map/all_to_all | solution.py:132
  315.6 12.3 %ssm_backward.1 = (f32[128,1792]{1,0:T(8,128)}, f32[8,1792]{1,0:T(8,128)}, f32[128,24]{1,0:T(8,128)}, f32[4,1792]{1,0:T(4,128)}, f32[1,1792]{1,0:T(1,128)}, /*index=5*/f32[3,24]{1,0:T(4,128)}) custom-call(s32[1]{0:T(128)} %slice.341.seg_before_ref, f32[128,4224]{1,0:T(8,128)} %copy-done, f32[8,1792]{1,0:T(8,128)} %copy-done.20, f32[128,4]{1,0:T(8,128)} %stack.38.same_ref, ...), custom_call_target="tpu_custom_call" | custom-call | tf_op jit(solution)/shard_map/ssm_backward/pallas_call | solution.py:631
  331.7 3.4 collective-permute-start.15
  336.0 4.8 collective-permute-done.15
  342.2 5.5 %collective-permute-done.16 = bf16[128,256]{1,0:T(8,128)(2,1)S(1)} collective-permute-done((bf16[128,256]{1,0:T(8,128)(2,1)S(1)}, bf16[128,256]{1,0:T(8,128)(2,1)S(1)}, u32[]{:S(2)}, u32[]{:S(2)}) %collective-permute-start.16) | collective-permute-done | bytes 65568 | tf_op jit(solution)/shard_map/ppermute | solution.py:74
  348.8 5.9 %convolution_convert_fusion = bf16[1024,4224]{1,0:T(8,128)(2,1)} fusion(bf16[128,4224]{1,0:T(8,128)(2,1)S(1)} %concatenate.98, f32[128,1024]{1,0:T(8,128)S(1)} %concatenate.77, f32[1024]{0:T(1024)S(1)} %get-tuple-element.71, f32[128]{0:T(128)S(1)} %add_rsqrt_fusion.1), kind=kOutput, calls=%fused_computation.1 | convolution fusion | flops 1112014848 | bytes 10260992 | tf_op jit(solution)/shard_map/dot_general | solution.py:141
  354.7 23.4 %reduce-scatter.3.cloned.1.call-done = bf16[32,8192]{1,0:T(8,128)(2,1)} async-done(((bf16[1024,8192]{1,0:T(8,128)(2,1)}), bf16[32,8192]{1,0:T(8,128)(2,1)}) %reduce-scatter.3.cloned.1.call-update) | async-done | bytes 524304 | tf_op jit(solution)/shard_map/reduce_scatter | solution.py:796
  379.5 3.7 fusion.15
  384.5 6.5 %multiply_reduce_fusion.1 = (f32[1024]{0:T(1024)S(1)}, f32[128]{0:T(128)S(1)}, f32[128,1024]{1,0:T(8,128)S(1)}) fusion(f32[128,1024]{1,0:T(8,128)S(1)} %concatenate.77, f32[128]{0:T(128)S(1)} %add_rsqrt_fusion.1, f32[1024]{0:T(1024)S(1)} %get-tuple-element.71, bf16[128,4224]{1,0:T(8,128)(2,1)S(1)} %concatenate.98, ...), kind=kOutput, calls=%fused_computation.43 | convolution fusion | flops 1108081536 | bytes 10789888 | tf_op jit(solution)/shard_map/dot_general | solution.py:147
  391.1 39.8 %psum.7 = f32[11080]{0:T(1024)S(1)} all-reduce(f32[11080]{0:T(1024)S(1)} %concatenate.100), channel_id=1, replica_groups=mesh['seq'=32] {'seq'}, use_global_device_ids=true, to_apply=%region_8.9 | all-reduce | flops 11080 | bytes 88640 | tf_op jit(solution)/shard_map/psum | solution.py:857
  438.4 36.5 %reduce-scatter.5.cloned.1.call-done = bf16[32,4224]{1,0:T(8,128)(2,1)} async-done(((bf16[1024,4224]{1,0:T(8,128)(2,1)}), bf16[32,4224]{1,0:T(8,128)(2,1)}) %reduce-scatter.5.cloned.1.call-update) | async-done | bytes 270352 | tf_op jit(solution)/shard_map/reduce_scatter | solution.py:838
  (200 shorter events, 65.5 us)
Async XLA Ops:
  7.2 75.0 %copy-start.8 = (f32[128,1024]{1,0:T(8,128)S(1)}, f32[128,1024]{1,0:T(8,128)}, u32[]{:S(2)}) copy-start(f32[128,1024]{1,0:T(8,128)} %param.18) | copy-start | bytes 1572868
  7.2 71.0 %all-gather.3.cloned.1.call-start = ((), (), s32[]{:S(2)}) async-start(), calls=%async_computation.6 | async-start | bytes 8921088 | tf_op jit(solution)/shard_map/all_gather | solution.py:698
  12.0 198.5 %all-gather.5.cloned.1.call-start = ((), (), s32[]{:S(2)}) async-start(), calls=%async_computation.7 | async-start | bytes 17301504 | tf_op jit(solution)/shard_map/all_gather | solution.py:702
  80.3 41.2 %copy-start.24 = (s32[128]{0:T(128)}, s32[128]{0:T(128)S(1)}, u32[]{:S(2)}) copy-start(s32[128]{0:T(128)S(1)} %get-tuple-element.73) | copy-start | bytes 1540
  84.5 6.7 %copy-start.27 = (f32[24]{0:T(128)S(1)}, f32[24]{0:T(128)}, u32[]{:S(2)}) copy-start(f32[24]{0:T(128)} %param.25) | copy-start | bytes 292
  84.6 6.7 %copy-start.28 = (f32[24]{0:T(128)S(1)}, f32[24]{0:T(128)}, u32[]{:S(2)}) copy-start(f32[24]{0:T(128)} %param.26) | copy-start | bytes 292
  84.6 35.6 %copy-start.25 = (f32[1792]{0:T(1024)S(1)}, f32[1792]{0:T(1024)}, u32[]{:S(2)}) copy-start(f32[1792]{0:T(1024)} %param.24) | copy-start | bytes 21508
  89.8 19.6 %copy-start.10 = (bf16[128,4224]{1,0:T(8,128)(2,1)}, bf16[128,4224]{1,0:T(8,128)(2,1)S(1)}, u32[]{:S(2)}) copy-start(bf16[128,4224]{1,0:T(8,128)(2,1)S(1)} %get-tuple-element.176) | copy-start | bytes 3244036
  89.8 54.6 %copy-start = (f32[128,4224]{1,0:T(8,128)}, f32[128,4224]{1,0:T(8,128)S(1)}, u32[]{:S(2)}) copy-start(f32[128,4224]{1,0:T(8,128)S(1)} %get-tuple-element.177.projected_ref) | copy-start | bytes 6488068
  89.8 8.6 %collective-permute-start.6 = (bf16[1,1,1,1,1,128,256]{6,5,4,3,2,1,0:T(8,128)(2,1)S(1)}, bf16[1,1,1,1,1,128,256]{6,5,4,3,2,1,0:T(8,128)(2,1)S(1)}, u32[]{:S(2)}, u32[]{:S(2)}) collective-permute-start(bf16[1,1,1,1,1,128,256]{6,5,4,3,2,1,0:T(8,128)(2,1)S(1)} %slice_bitcast_fusion.3), channel_id=1, source_target_pairs={{0,16},{1,17},{2,18},{3,19},{4,20},{5,21},{6,22},{7,23},{8,24},{9,... | collective-permute-start | bytes 196616 | tf_op jit(solution)/shard_map/ppermute | solution.py:74
  91.3 7.2 %collective-permute-start.1 = (f32[1,1,1,1,1,1,24]{6,5,4,3,2,1,0:T(1,128)S(1)}, f32[1,1,1,1,1,1,24]{6,5,4,3,2,1,0:T(1,128)S(1)}, u32[]{:S(2)}, u32[]{:S(2)}) collective-permute-start(f32[1,1,1,1,1,1,24]{6,5,4,3,2,1,0:T(1,128)S(1)} %fusion.29), channel_id=1, source_target_pairs={{0,16},{1,17},{2,18},{3,19},{4,20},{5,21},{6,22},{7,23},{8,24},{9,... | collective-permute-start | bytes 296 | tf_op jit(solution)/shard_map/ppermute | solution.py:74
  98.4 8.7 %collective-permute-start.7 = (bf16[2,1,1,1,1,128,256]{6,5,4,3,2,1,0:T(8,128)(2,1)S(1)}, bf16[2,1,1,1,1,128,256]{6,5,4,3,2,1,0:T(8,128)(2,1)S(1)}, u32[]{:S(2)}, u32[]{:S(2)}) collective-permute-start(bf16[2,1,1,1,1,128,256]{6,5,4,3,2,1,0:T(8,128)(2,1)S(1)} %pad_maximum_fusion.14), channel_id=1, source_target_pairs={{0,8},{1,9},{2,10},{3,11},{4,12},{5,13},{6,14},{7,15},{8,0},{9,1},... | collective-permute-start | bytes 393224 | tf_op jit(solution)/shard_map/ppermute | solution.py:74
  98.5 8.7 %collective-permute-start.2 = (f32[2,1,1,1,1,1,24]{6,5,4,3,2,1,0:T(1,128)S(1)}, f32[2,1,1,1,1,1,24]{6,5,4,3,2,1,0:T(1,128)S(1)}, u32[]{:S(2)}, u32[]{:S(2)}) collective-permute-start(f32[2,1,1,1,1,1,24]{6,5,4,3,2,1,0:T(1,128)S(1)} %pad_maximum_fusion.19), channel_id=1, source_target_pairs={{0,8},{1,9},{2,10},{3,11},{4,12},{5,13},{6,14},{7,15},{8,0},{9,1},... | collective-permute-start | bytes 584 | tf_op jit(solution)/shard_map/ppermute | solution.py:74
  107.1 6.9 %collective-permute-start.8 = (bf16[2,2,1,1,1,128,256]{6,5,4,3,2,1,0:T(8,128)(2,1)S(1)}, bf16[2,2,1,1,1,128,256]{6,5,4,3,2,1,0:T(8,128)(2,1)S(1)}, u32[]{:S(2)}, u32[]{:S(2)}) collective-permute-start(bf16[2,2,1,1,1,128,256]{6,5,4,3,2,1,0:T(8,128)(2,1)S(1)} %pad_maximum_fusion.13), channel_id=1, source_target_pairs={{0,4},{1,5},{2,6},{3,7},{4,0},{5,1},{6,2},{7,3},{8,12},{9,13},{10,... | collective-permute-start | bytes 786440 | tf_op jit(solution)/shard_map/ppermute | solution.py:74
  107.3 12.8 %collective-permute-start.3 = (f32[2,2,1,1,1,1,24]{6,5,4,3,2,1,0:T(1,128)S(1)}, f32[2,2,1,1,1,1,24]{6,5,4,3,2,1,0:T(1,128)S(1)}, u32[]{:S(2)}, u32[]{:S(2)}) collective-permute-start(f32[2,2,1,1,1,1,24]{6,5,4,3,2,1,0:T(1,128)S(1)} %pad_maximum_fusion.18), channel_id=1, source_target_pairs={{0,4},{1,5},{2,6},{3,7},{4,0},{5,1},{6,2},{7,3},{8,12},{9,13},{10,... | collective-permute-start | bytes 1160 | tf_op jit(solution)/shard_map/ppermute | solution.py:74
  114.1 40.8 %copy-start.6 = (bf16[2,2,1,1,1,128,256]{6,5,4,3,2,1,0:T(8,128)(2,1)}, bf16[2,2,1,1,1,128,256]{6,5,4,3,2,1,0:T(8,128)(2,1)S(1)}, u32[]{:S(2)}) copy-start(bf16[2,2,1,1,1,128,256]{6,5,4,3,2,1,0:T(8,128)(2,1)S(1)} %get-tuple-element.134) | copy-start | bytes 786436
  115.0 39.9 %collective-permute-start.9 = (bf16[2,2,2,1,1,128,256]{6,5,4,3,2,1,0:T(8,128)(2,1)}, bf16[2,2,2,1,1,128,256]{6,5,4,3,2,1,0:T(8,128)(2,1)}, u32[]{:S(2)}, u32[]{:S(2)}) collective-permute-start(bf16[2,2,2,1,1,128,256]{6,5,4,3,2,1,0:T(8,128)(2,1)} %pad_maximum_fusion.7), channel_id=1, source_target_pairs={{0,2},{1,3},{2,0},{3,1},{4,6},{5,7},{6,4},{7,5},{8,10},{9,11},{10,... | collective-permute-start | bytes 1572872 | tf_op jit(solution)/shard_map/ppermute | solution.py:74
  120.1 23.7 %collective-permute-start.4 = (f32[2,2,2,1,1,1,24]{6,5,4,3,2,1,0:T(1,128)S(1)}, f32[2,2,2,1,1,1,24]{6,5,4,3,2,1,0:T(1,128)S(1)}, u32[]{:S(2)}, u32[]{:S(2)}) collective-permute-start(f32[2,2,2,1,1,1,24]{6,5,4,3,2,1,0:T(1,128)S(1)} %pad_maximum_fusion.17), channel_id=1, source_target_pairs={{0,2},{1,3},{2,0},{3,1},{4,6},{5,7},{6,4},{7,5},{8,10},{9,11},{10,... | collective-permute-start | bytes 2312 | tf_op jit(solution)/shard_map/ppermute | solution.py:74
  122.3 22.1 %collective-permute-start = (f32[8,1792]{1,0:T(8,128)S(1)}, f32[8,1792]{1,0:T(8,128)S(1)}, u32[]{:S(2)}, u32[]{:S(2)}) collective-permute-start(f32[8,1792]{1,0:T(8,128)S(1)} %slice.428), channel_id=1, source_target_pairs={{0,1},{1,2},{2,3},{3,4},{4,5},{5,6},{6,7},{7,8},{8,9},{9,10},{10,1... | collective-permute-start | bytes 172040 | tf_op jit(solution)/shard_map/ppermute | solution.py:31
  144.4 13.1 %collective-permute-start.5 = (f32[2,2,2,2,1,1,24]{6,5,4,3,2,1,0:T(1,128)}, f32[2,2,2,2,1,1,24]{6,5,4,3,2,1,0:T(1,128)}, u32[]{:S(2)}, u32[]{:S(2)}) collective-permute-start(f32[2,2,2,2,1,1,24]{6,5,4,3,2,1,0:T(1,128)} %pad_maximum_fusion.16), channel_id=1, source_target_pairs={{0,1},{1,0},{2,3},{3,2},{4,5},{5,4},{6,7},{7,6},{8,9},{9,8},{10,11... | collective-permute-start | bytes 4616 | tf_op jit(solution)/shard_map/ppermute | solution.py:74
  150.7 21.6 %all-to-all-start = ((bf16[32,48,128]{2,1,0:T(8,128)(2,1)}), bf16[32,48,128]{2,1,0:T(8,128)(2,1)S(1)}, u32[]{:S(2)}, u32[]{:S(2)}) async-start(bf16[32,48,128]{2,1,0:T(8,128)(2,1)} %bitcast.91), calls=%async_computation | async-start | bytes 786432 | tf_op jit(solution)/shard_map/all_to_all | solution.py:126
  154.9 25.2 %copy-start.21 = (s32[4096]{0:T(1024)S(1)}, s32[4096]{0:T(1024)}, u32[]{:S(2)}) copy-start(s32[4096]{0:T(1024)} %param.20) | copy-start | bytes 49156
  154.9 29.7 %copy-start.9 = (f32[128,1024]{1,0:T(8,128)S(1)}, f32[128,1024]{1,0:T(8,128)}, u32[]{:S(2)}) copy-start(f32[128,1024]{1,0:T(8,128)} %param.19) | copy-start | bytes 1572868
  157.3 45.3 %collective-permute-start.10 = (bf16[2,2,2,2,1,128,256]{6,5,4,3,2,1,0:T(8,128)(2,1)}, bf16[2,2,2,2,1,128,256]{6,5,4,3,2,1,0:T(8,128)(2,1)}, u32[]{:S(2)}, u32[]{:S(2)}) collective-permute-start(bf16[2,2,2,2,1,128,256]{6,5,4,3,2,1,0:T(8,128)(2,1)} %pad_maximum_fusion.2), channel_id=1, source_target_pairs={{0,1},{1,0},{2,3},{3,2},{4,5},{5,4},{6,7},{7,6},{8,9},{9,8},{10,11... | collective-permute-start | bytes 3145736 | tf_op jit(solution)/shard_map/ppermute | solution.py:74
  177.4 20.3 %all-to-all-start.1 = ((bf16[32,48,128]{2,1,0:T(8,128)(2,1)}), bf16[32,48,128]{2,1,0:T(8,128)(2,1)S(1)}, u32[]{:S(2)}, u32[]{:S(2)}) async-start(bf16[32,48,128]{2,1,0:T(8,128)(2,1)} %carry.2), calls=%async_computation.1 | async-start | bytes 786432 | tf_op jit(solution)/shard_map/all_to_all | solution.py:132
  180.0 198.1 %reduce-scatter.3.cloned.1.call-start = ((), (), s32[]{:S(2)}) async-start(), calls=%async_computation.8 | async-start | bytes 17301504 | tf_op jit(solution)/shard_map/reduce_scatter | solution.py:796
  203.9 6.6 %copy-start.18 = (bf16[128,1536]{1,0:T(8,128)(2,1)S(1)}, bf16[128,1536]{1,0:T(8,128)(2,1)}, u32[]{:S(2)}) copy-start(bf16[128,1536]{1,0:T(8,128)(2,1)} %get-tuple-element.46) | copy-start | bytes 1179652
  214.4 19.0 %copy-start.4 = (f32[128,1024]{1,0:T(8,128)}, f32[128,1024]{1,0:T(8,128)S(1)}, u32[]{:S(2)}) copy-start(f32[128,1024]{1,0:T(8,128)S(1)} %get-tuple-element.179) | copy-start | bytes 1572868
  222.7 9.4 %copy-start.16 = (bf16[128,2048]{1,0:T(8,128)(2,1)}, bf16[128,2048]{1,0:T(8,128)(2,1)S(1)}, u32[]{:S(2)}) copy-start(bf16[128,2048]{1,0:T(8,128)(2,1)S(1)} %get-tuple-element.78) | copy-start | bytes 1572868
  254.4 23.0 %collective-permute-start.12 = (bf16[2,2,2,2,128,256]{5,4,0,1,2,3:T(8,128)(2,1)S(1)}, bf16[2,2,2,2,128,256]{5,4,0,1,2,3:T(8,128)(2,1)S(1)}, u32[]{:S(2)}, u32[]{:S(2)}) collective-permute-start(bf16[2,2,2,2,128,256]{5,4,0,1,2,3:T(8,128)(2,1)S(1)} %bitcast.90), channel_id=1, source_target_pairs={{0,1},{1,0},{2,3},{3,2},{4,5},{5,4},{6,7},{7,6},{8,9},{9,8},{10,11... | collective-permute-start | bytes 3145736 | tf_op jit(solution)/shard_map/ppermute | solution.py:74
  258.9 33.0 %all-to-all-start.2 = ((bf16[32,48,128]{2,1,0:T(8,128)(2,1)}), bf16[32,48,128]{2,1,0:T(8,128)(2,1)S(1)}, u32[]{:S(2)}, u32[]{:S(2)}) async-start(bf16[32,48,128]{2,1,0:T(8,128)(2,1)} %bitcast.92), calls=%async_computation.2 | async-start | bytes 786432 | tf_op jit(solution)/shard_map/all_to_all | solution.py:126
  281.1 22.2 %collective-permute-start.13 = (bf16[2,2,2,128,256]{4,3,0,1,2:T(8,128)(2,1)}, bf16[2,2,2,128,256]{4,3,0,1,2:T(8,128)(2,1)}, u32[]{:S(2)}, u32[]{:S(2)}) collective-permute-start(bf16[2,2,2,128,256]{4,3,0,1,2:T(8,128)(2,1)} %fusion.19), channel_id=1, source_target_pairs={{0,2},{1,3},{2,0},{3,1},{4,6},{5,7},{6,4},{7,5},{8,10},{9,11},{10,... | collective-permute-start | bytes 1572872 | tf_op jit(solution)/shard_map/ppermute | solution.py:74
  296.9 17.9 %all-to-all-start.3 = ((bf16[32,48,128]{2,1,0:T(8,128)(2,1)}), bf16[32,48,128]{2,1,0:T(8,128)(2,1)S(1)}, u32[]{:S(2)}, u32[]{:S(2)}) async-start(bf16[32,48,128]{2,1,0:T(8,128)(2,1)} %carry.3), calls=%async_computation.3 | async-start | bytes 786432 | tf_op jit(solution)/shard_map/all_to_all | solution.py:132
  300.4 174.4 %reduce-scatter.5.cloned.1.call-start = ((), (), s32[]{:S(2)}) async-start(), calls=%async_computation.9 | async-start | bytes 8921088 | tf_op jit(solution)/shard_map/reduce_scatter | solution.py:838
  306.2 25.4 %copy-start.3 = (f32[2,2,2,128,256]{4,3,0,1,2:T(8,128)S(1)}, f32[2,2,2,128,256]{4,3,0,1,2:T(8,128)}, u32[]{:S(2)}) copy-start(f32[2,2,2,128,256]{4,3,0,1,2:T(8,128)} %copy-done.2) | copy-start | bytes 3145732
  306.2 25.4 %collective-permute-start.14 = (bf16[2,2,128,256]{3,2,0,1:T(8,128)(2,1)}, bf16[2,2,128,256]{3,2,0,1:T(8,128)(2,1)S(1)}, u32[]{:S(2)}, u32[]{:S(2)}) collective-permute-start(bf16[2,2,128,256]{3,2,0,1:T(8,128)(2,1)} %fusion.20), channel_id=1, source_target_pairs={{0,4},{1,5},{2,6},{3,7},{4,0},{5,1},{6,2},{7,3},{8,12},{9,13},{10,... | collective-permute-start | bytes 786440 | tf_op jit(solution)/shard_map/ppermute | solution.py:74
  315.6 32.1 %copy-start.19 = (bf16[128,1536]{1,0:T(8,128)(2,1)S(1)}, bf16[128,1536]{1,0:T(8,128)(2,1)}, u32[]{:S(2)}) copy-start(bf16[128,1536]{1,0:T(8,128)(2,1)} %get-tuple-element.51) | copy-start | bytes 1179652
  327.9 19.8 %copy-start.22 = (bf16[128,512]{1,0:T(8,128)(2,1)S(1)}, bf16[128,512]{1,0:T(8,128)(2,1)}, u32[]{:S(2)}) copy-start(bf16[128,512]{1,0:T(8,128)(2,1)} %get-tuple-element.57) | copy-start | bytes 393220
  328.8 6.3 %collective-permute-start.11 = (f32[8,1792]{1,0:T(8,128)}, f32[8,1792]{1,0:T(8,128)S(1)}, u32[]{:S(2)}, u32[]{:S(2)}) collective-permute-start(f32[8,1792]{1,0:T(8,128)} %get-tuple-element.55), channel_id=1, source_target_pairs={{1,0},{2,1},{3,2},{4,3},{5,4},{6,5},{7,6},{8,7},{9,8},{10,9},{11,1... | collective-permute-start | bytes 172040 | tf_op jit(solution)/shard_map/ppermute | solution.py:31
  331.7 9.0 %collective-permute-start.15 = (bf16[2,128,256]{2,1,0:T(8,128)(2,1)S(1)}, bf16[2,128,256]{2,1,0:T(8,128)(2,1)S(1)}, u32[]{:S(2)}, u32[]{:S(2)}) collective-permute-start(bf16[2,128,256]{2,1,0:T(8,128)(2,1)S(1)} %fusion.21), channel_id=1, source_target_pairs={{0,8},{1,9},{2,10},{3,11},{4,12},{5,13},{6,14},{7,15},{8,0},{9,1},... | collective-permute-start | bytes 393224 | tf_op jit(solution)/shard_map/ppermute | solution.py:74
  340.8 6.9 %collective-permute-start.16 = (bf16[128,256]{1,0:T(8,128)(2,1)S(1)}, bf16[128,256]{1,0:T(8,128)(2,1)S(1)}, u32[]{:S(2)}, u32[]{:S(2)}) collective-permute-start(bf16[128,256]{1,0:T(8,128)(2,1)S(1)} %fusion.27), channel_id=1, source_target_pairs={{0,16},{1,17},{2,18},{3,19},{4,20},{5,21},{6,22},{7,23},{8,24},{9,... | collective-permute-start | bytes 196616 | tf_op jit(solution)/shard_map/ppermute | solution.py:74
  354.7 23.5 %copy-start.31 = (s32[32]{0:T(128)S(1)}, s32[32]{0:T(128)}, u32[]{:S(2)}) copy-start(s32[32]{0:T(128)} %constant.114.clone) | copy-start | bytes 388
  354.7 24.7 %copy-start.5 = (f32[128,1024]{1,0:T(8,128)S(1)}, f32[128,1024]{1,0:T(8,128)}, u32[]{:S(2)}) copy-start(f32[128,1024]{1,0:T(8,128)} %copy-done.4) | copy-start | bytes 1572868
  354.7 24.7 %copy-start.17 = (bf16[128,2048]{1,0:T(8,128)(2,1)S(1)}, bf16[128,2048]{1,0:T(8,128)(2,1)}, u32[]{:S(2)}) copy-start(bf16[128,2048]{1,0:T(8,128)(2,1)} %copy-done.16) | copy-start | bytes 1572868
  379.4 5.0 %copy-start.26 = (f32[1,1792]{1,0:T(1,128)S(1)}, f32[1,1792]{1,0:T(1,128)}, u32[]{:S(2)}) copy-start(f32[1,1792]{1,0:T(1,128)} %get-tuple-element.61) | copy-start | bytes 21508
  379.5 5.0 %copy-start.30 = (f32[3,24]{1,0:T(4,128)S(1)}, f32[3,24]{1,0:T(4,128)}, u32[]{:S(2)}) copy-start(f32[3,24]{1,0:T(4,128)} %get-tuple-element.62) | copy-start | bytes 868
  384.5 6.5 %copy-start.29 = (f32[1024]{0:T(1024)S(1)}, f32[1024]{0:T(1024)}, u32[]{:S(2)}) copy-start(f32[1024]{0:T(1024)} %get-tuple-element.66) | copy-start | bytes 12292
  391.0 44.4 %copy-start.7 = (bf16[32,8192]{1,0:T(8,128)(2,1)S(1)}, bf16[32,8192]{1,0:T(8,128)(2,1)}, u32[]{:S(2)}) copy-start(bf16[32,8192]{1,0:T(8,128)(2,1)} %reduce-scatter.3.cloned.1.call-done) | copy-start | bytes 1572868
  (9 other events, 11.5 us)
Sparse Core Ops, SparseCore 0:
  12.1 65.9 all-gather.2
  80.3 120.8 all-gather.4
  244.8 133.2 reduce-scatter.2
  380.3 94.5 reduce-scatter.4
